TPU v7x, 256 devices: a whole 4x4x8 slice. The times are simulated.
256 devices in a mesh: seq: 32 (over z, y), tp: 8 (over x, core).
Axes of the slice: x: 4, y: 4, z: 8, core: 2. Of those that a mesh axis runs over, the one named last changes fastest.
Arguments:
- query_raw: bfloat16 [16384, 4096], P('seq', 'tp'), may hold values from -6 to 6
- key_raw: bfloat16 [16384, 4096], P('seq', 'tp'), may hold values from -6 to 6
- value_raw: bfloat16 [16384, 4096], P('seq', 'tp'), may hold values from -6 to 6
- conv_taps: float32 [3, 4, 4096], P(None, None, 'tp'), may hold values from -3 to 3
- layout_boxes: int32 [4, 16384], P(None, 'seq'), may hold values from 0 to 1023
- box_tables: bfloat16 [2, 1024, 4096], P(None, None, 'tp'), may hold values from -4 to 4
- log_decay: float32 [32, 16384], P('tp', 'seq'), may hold values from -1 to 0, as said below
- norm_gain: float32 [4096], P('tp'), may hold values from 0.25 to 1.75
- out_weight: bfloat16 [4096, 4096], P('tp', 'seq'), may hold values from -0.09375 to 0.09375
- grad_output: bfloat16 [16384, 4096], P('seq', 'tp'), may hold values from -6 to 6
Outputs:
- layer_out: bfloat16 [16384, 4096], P('seq', 'tp')
- grad_query: bfloat16 [16384, 4096], P('seq', 'tp')
- grad_key: bfloat16 [16384, 4096], P('seq', 'tp')
- grad_value: bfloat16 [16384, 4096], P('seq', 'tp')
- grad_taps: float32 [3, 4, 4096], P(None, None, 'tp')
- grad_tables: float32 [2, 1024, 4096], P(None, None, 'tp')
- grad_gain: float32 [4096], P('tp')
- grad_weight: float32 [4096, 4096], P('tp', 'seq')
Inputs may be any that keep to these rules, and one draw needn't show every extreme that they name: `log_decay`: each entry is the logarithm (at most 0) of one head's state decay at one token.
All inputs are finite; a program needn't handle non-finite values.
Results may differ from a plain program's by a relative error of at most 0.02.
Values may be sent and summed in bfloat16 or wider, within the bound.
A program may use at most 128 MiB of HBM per device.

v0:
```python
import jax
import jax.numpy as jnp
from jax import lax
from jax.sharding import PartitionSpec as P

HIGHEST = lax.Precision.HIGHEST


def shifted(x, axis, by):
    length = lax.axis_size(axis)
    pairs = [(i, i + by) for i in range(length) if 0 <= i + by < length]
    return lax.ppermute(x, axis, pairs)


def entering(x, axis, combine, identity, reverse):
    length, here = (lax.axis_size(axis), lax.axis_index(axis))
    everything = jax.tree.map(
        lambda part, kind: lax.all_gather(part.astype(kind), axis), x, (jnp.bfloat16, jnp.bfloat16)
    )
    start = jax.tree.map(
        lambda part, zero: jnp.broadcast_to(jnp.asarray(zero, part.dtype), part.shape), x, identity
    )

    def turn(k, before):
        at = length - 1 - k if reverse else k
        reached = at > here if reverse else at < here
        new = combine(
            before, jax.tree.map(lambda part, own: part[at].astype(own.dtype), everything, x)
        )
        return jax.tree.map(lambda a, b: jnp.where(reached, a, b), new, before)

    return lax.fori_loop(0, length, turn, start)


def combine(earlier, later):
    return (earlier[0] * later[0], later[0][:, None, None] * earlier[1] + later[1])


def on_device(
    query_raw,
    key_raw,
    value_raw,
    conv_taps,
    layout_boxes,
    box_tables,
    log_decay,
    norm_gain,
    out_weight,
    grad_output,
):
    row_count, feat_width = query_raw.shape
    head_count = log_decay.shape[0]
    head_size = feat_width // head_count
    kernel = conv_taps.shape[1]
    buckets = box_tables.shape[1]
    feature_scale = head_size ** (-0.5)
    stacked = jnp.stack([query_raw, key_raw, value_raw])
    rim_rows = shifted(stacked[:, row_count - (kernel - 1) :, :], "seq", 1)
    padded = jnp.concatenate([rim_rows, stacked], axis=1).astype(jnp.float32)
    conved = jnp.zeros((3, row_count, feat_width), jnp.float32)
    for tap_step in range(kernel):
        conved = (
            conved
            + conv_taps[:, tap_step, None, :]
            * padded[:, kernel - 1 - tap_step : kernel - 1 - tap_step + row_count, :]
        )
    bucket_ids = jnp.arange(buckets, dtype=jnp.int32)

    def count_table(first, second):
        return (first[:, None] == bucket_ids[None, :]).astype(jnp.bfloat16) + (
            second[:, None] == bucket_ids[None, :]
        ).astype(jnp.bfloat16)

    hot_x = count_table(layout_boxes[0], layout_boxes[2])
    hot_y = count_table(layout_boxes[1], layout_boxes[3])
    layout = jnp.dot(hot_x, box_tables[0], preferred_element_type=jnp.float32) + jnp.dot(
        hot_y, box_tables[1], preferred_element_type=jnp.float32
    )
    query_feat = (feature_scale * (conved[0] + layout)).astype(jnp.bfloat16)
    key_feat = (conved[1] + layout).astype(jnp.bfloat16)
    value_feat = conved[2].astype(jnp.bfloat16)

    def split_heads(matrix):
        return matrix.reshape(row_count, head_count, head_size).transpose(1, 0, 2)

    def join_heads(blocks):
        return blocks.transpose(1, 0, 2).reshape(row_count, feat_width)

    query_heads = split_heads(query_feat)
    key_heads = split_heads(key_feat)
    value_heads = split_heads(value_feat)
    decay_sum = jnp.cumsum(log_decay, axis=1)
    decay_total = decay_sum[:, -1]
    head_decay = jnp.exp(decay_sum)[:, :, None]
    tail_decay = jnp.exp(decay_total[:, None] - decay_sum)[:, :, None]
    block_decay = jnp.exp(decay_total)
    positions = jnp.arange(row_count, dtype=jnp.int32)
    causal_mask = positions[:, None] >= positions[None, :]
    decay_mask = jnp.where(
        causal_mask[None],
        jnp.exp(jnp.minimum(decay_sum[:, :, None] - decay_sum[:, None, :], 0.0)),
        0.0,
    )
    identity = (
        jnp.ones((head_count,), jnp.float32),
        jnp.zeros((head_count, head_size, head_size), jnp.float32),
    )
    local_state = jnp.einsum("hsi,hsj->hij", key_heads * tail_decay, value_heads, precision=HIGHEST)
    incoming = entering((block_decay, local_state), "seq", combine, identity, False)[1]
    scores = decay_mask * jnp.einsum(
        "hti,hsi->hts", query_heads, key_heads, preferred_element_type=jnp.float32
    )
    attended = jnp.einsum("hts,hsj->htj", scores, value_heads, precision=HIGHEST)
    attended = attended + head_decay * jnp.einsum(
        "hti,hij->htj", query_heads, incoming, precision=HIGHEST
    )
    inverse = lax.rsqrt(jnp.mean(attended * attended, axis=-1, keepdims=True) + 1e-06)
    unit_norm = attended * inverse
    gain_heads = norm_gain.reshape(head_count, 1, head_size)
    normed = join_heads(unit_norm * gain_heads).astype(jnp.bfloat16)
    partial_sum = jnp.dot(
        normed,
        lax.all_gather(out_weight, "seq", axis=1, tiled=True),
        preferred_element_type=jnp.float32,
    )
    layer_out = lax.psum_scatter(
        partial_sum.astype(jnp.bfloat16), "tp", scatter_dimension=1, tiled=True
    )
    cotangent = lax.all_gather(grad_output, "tp", axis=1, tiled=True)
    contract_last = (((1,), (1,)), ((), ()))
    grad_normed_sum = lax.dot_general(
        cotangent,
        lax.all_gather(out_weight, "seq", axis=1, tiled=True),
        contract_last,
        preferred_element_type=jnp.float32,
    )
    grad_normed = grad_normed_sum.astype(jnp.bfloat16)
    contract_first = (((0,), (0,)), ((), ()))
    weight_terms = lax.dot_general(
        normed, cotangent, contract_first, preferred_element_type=jnp.float32
    )
    grad_weight = lax.psum_scatter(
        weight_terms.astype(jnp.bfloat16), "seq", scatter_dimension=1, tiled=True
    ).astype(jnp.float32)
    grad_heads = split_heads(grad_normed).astype(jnp.float32)
    gain_terms = jnp.sum(grad_heads * unit_norm, axis=1).reshape(feat_width)
    grad_unit = grad_heads * gain_heads
    grad_attended = inverse * (
        grad_unit - unit_norm * jnp.mean(grad_unit * unit_norm, axis=-1, keepdims=True)
    )
    back_state = jnp.einsum(
        "hti,htj->hij", query_heads * head_decay, grad_attended, precision=HIGHEST
    )
    later_state = entering((block_decay, back_state), "seq", combine, identity, True)[1]
    grad_scores = decay_mask * jnp.einsum(
        "htj,hsj->hts", grad_attended, value_heads, precision=HIGHEST
    )
    grad_qh = jnp.einsum(
        "hts,hsi->hti", grad_scores, key_heads, precision=HIGHEST
    ) + head_decay * jnp.einsum("htj,hij->hti", grad_attended, incoming, precision=HIGHEST)
    grad_kh = jnp.einsum(
        "hts,hti->hsi", grad_scores, query_heads, precision=HIGHEST
    ) + tail_decay * jnp.einsum("hsj,hij->hsi", value_heads, later_state, precision=HIGHEST)
    grad_vh = jnp.einsum(
        "hts,htj->hsj", scores, grad_attended, precision=HIGHEST
    ) + tail_decay * jnp.einsum("hsi,hij->hsj", key_heads, later_state, precision=HIGHEST)
    grad_pre = jnp.stack(
        [feature_scale * join_heads(grad_qh), join_heads(grad_kh), join_heads(grad_vh)]
    )
    next_rows = shifted(grad_pre[:, : kernel - 1, :], "seq", -1)
    extended = jnp.concatenate([grad_pre, next_rows], axis=1)
    grad_inputs = jnp.zeros((3, row_count, feat_width), jnp.float32)
    for tap_step in range(kernel):
        grad_inputs = (
            grad_inputs
            + conv_taps[:, tap_step, None, :] * extended[:, tap_step : tap_step + row_count, :]
        )
    tap_terms = jnp.stack(
        [
            jnp.sum(
                grad_pre * padded[:, kernel - 1 - tap_step : kernel - 1 - tap_step + row_count, :],
                axis=1,
            )
            for tap_step in range(kernel)
        ],
        axis=1,
    )
    grad_layout = (grad_pre[0] + grad_pre[1]).astype(jnp.bfloat16)
    table_terms = jnp.stack(
        [
            lax.dot_general(hot_x, grad_layout, contract_first, preferred_element_type=jnp.float32),
            lax.dot_general(hot_y, grad_layout, contract_first, preferred_element_type=jnp.float32),
        ]
    )
    grad_taps, grad_tables, grad_gain = (
        lax.psum(tap_terms.astype(jnp.bfloat16), "seq").astype(jnp.float32),
        lax.psum(table_terms.astype(jnp.bfloat16), "seq").astype(jnp.float32),
        lax.psum(gain_terms.astype(jnp.bfloat16), "seq").astype(jnp.float32),
    )
    grad_query = grad_inputs[0].astype(jnp.bfloat16)
    grad_key = grad_inputs[1].astype(jnp.bfloat16)
    grad_value = grad_inputs[2].astype(jnp.bfloat16)
    return (
        layer_out,
        grad_query,
        grad_key,
        grad_value,
        grad_taps,
        grad_tables,
        grad_gain,
        grad_weight,
    )


def solution(mesh):
    return jax.shard_map(
        on_device,
        mesh=mesh,
        in_specs=(
            P("seq", "tp"),
            P("seq", "tp"),
            P("seq", "tp"),
            P(None, None, "tp"),
            P(None, "seq"),
            P(None, None, "tp"),
            P("tp", "seq"),
            P("tp"),
            P("tp", "seq"),
            P("seq", "tp"),
        ),
        out_specs=(
            P("seq", "tp"),
            P("seq", "tp"),
            P("seq", "tp"),
            P("seq", "tp"),
            P(None, None, "tp"),
            P(None, None, "tp"),
            P("tp"),
            P("tp", "seq"),
        ),
        check_vma=False,
    )
```

profile of v0, /device:TPU:2, one launch (start us, length us, event | category | flops | bytes accessed | tf_op | source)
XLA Modules:
  0.0 766.2 jit_solution(2590251355340707665)
XLA Ops:
  8.7 1.3 copy.61
  10.0 1.3 copy.60
  11.2 1.3 copy.59
  12.7 3.5 collective-permute-start
  16.2 1.2 reduce-window.6
  18.2 2.3 fusion.59
  20.5 4.1 collective-permute-done
  25.4 3.7 multiply_add_fusion
  29.3 1.1 fusion.62
  30.7 2.0 convolution_convert_fusion.6
  34.3 79.6 %all-reduce = bf16[128]{0:T(256)(128)(2,1)S(1)} all-reduce(bf16[128]{0:T(256)(128)(2,1)S(1)} %dynamic-update-slice), channel_id=2, replica_groups=mesh['seq'=32,'tp'=8] {'seq'}, use_global_device_ids=true, to_apply=%add | all-reduce | flops 128 | bytes 512
  114.0 2.8 fusion.95
  116.8 15.7 %all-gather.8.cloned.1.call-done = bf16[512,4096]{1,0:T(8,128)(2,1)} async-done(((bf16[512,128]{1,0:T(8,128)(2,1)}), bf16[512,4096]{1,0:T(8,128)(2,1)}) %all-gather.8.cloned.1.call-update) | async-done | bytes 4194320 | tf_op jit(solution)/shard_map/all_gather | solution.py:123
  132.5 5.8 convolution_convert_fusion.4
  138.4 79.8 %all-gather.12.cloned.1.call-done = bf16[128,128,128]{2,1,0:T(8,128)(2,1)} async-done(((bf16[4,128,128]{2,1,0:T(8,128)(2,1)}), bf16[128,128,128]{2,1,0:T(8,128)(2,1)}) %all-gather.12.cloned.1.call-update) | async-done | bytes 4194320 | tf_op jit(solution)/shard_map/all_gather | solution.py:18
  218.2 33.9 %while.30 = (s32[]{:T(128)}, f32[4,128,128]{2,1,0:T(8,128)S(1)}, s32[]{:T(128)}, bf16[32,4]{1,0:T(8,128)(2,1)S(1)}, bf16[32,4,128,128]{3,2,1,0:T(8,128)(2,1)}, /*index=5*/s32[]{:T(128)}, s32[]{:T(128)}) while((s32[]{:T(128)}, f32[4,128,128]{2,1,0:T(8,128)S(1)}, s32[]{:T(128)}, bf16[32,4]{1,0:T(8,128)(2,1)S(1)}, ...), condition=%wide.region_3.4_spmd.clone, body=%wide.region_2.3_spmd.clone.sunk | while | flops 327688 | bytes 655513 | solution.py:32
  220.3 1.0 fusion.135
  221.4 1.0 fusion.135
  224.6 1.0 fusion.135
  227.7 1.0 fusion.135
  230.9 1.0 fusion.135
  232.0 1.0 fusion.135
  234.1 1.0 fusion.135
  252.7 1.0 copy-done.8
  253.8 6.7 multiply_reduce_fusion.4
  261.0 2.1 convolution_convert_fusion.5
  263.3 1.7 fusion.76
  265.8 6.5 convolution_convert_fusion
  272.3 6.5 copy.96
  278.8 2.0 fusion.108
  280.8 3.9 fusion.39
  284.7 4.5 fusion.36
  289.2 52.6 %all-gather.14.cloned.1.call-done = bf16[128,128,128]{2,1,0:T(8,128)(2,1)} async-done(((bf16[4,128,128]{2,1,0:T(8,128)(2,1)}), bf16[128,128,128]{2,1,0:T(8,128)(2,1)}) %all-gather.14.cloned.1.call-update) | async-done | bytes 4194320 | tf_op jit(solution)/shard_map/all_gather | solution.py:18
  341.8 34.1 %while.31 = (s32[]{:T(128)}, f32[4,128,128]{2,1,0:T(8,128)S(1)}, s32[]{:T(128)}, bf16[32,4]{1,0:T(8,128)(2,1)S(1)}, bf16[32,4,128,128]{3,2,1,0:T(8,128)(2,1)}, /*index=5*/s32[]{:T(128)}, s32[]{:T(128)}, s32[]{:T(128)}, s32[]{:T(128)}) while((s32[]{:T(128)}, f32[4,128,128]{2,1,0:T(8,128)S(1)}, s32[]{:T(128)}, ...), condition=%wide.region_8.9_spmd.clone, body=%wide.region_7.8_spmd.clone.sunk | while | flops 327692 | bytes 655575 | solution.py:32
  353.5 1.0 fusion.136
  354.6 1.0 fusion.136
  358.9 1.0 fusion.136
  360.0 1.0 fusion.136
  361.0 1.0 fusion.136
  364.2 1.0 fusion.136
  365.3 1.0 fusion.136
  367.4 1.0 fusion.136
  368.5 1.0 fusion.136
  371.7 1.0 fusion.136
  372.8 1.0 fusion.136
  374.9 1.0 fusion.136
  376.0 2.0 fusion.48
  377.9 1.5 add_convert_fusion
  381.4 1.5 pad_maximum_fusion.2
  383.2 6.6 convolution_convert_fusion.1
  389.8 1.2 copy-done.4
  391.0 6.3 fusion.42
  399.3 1.4 copy.76
  400.6 1.3 collective-permute-start.1
  401.9 4.4 collective-permute-done.1
  406.4 1.2 copy.77
  407.6 1.7 pad_maximum_fusion
  410.0 7.6 multiply_reduce_fusion.3
  420.8 139.0 %all-reduce.1 = (bf16[3,4,512]{2,0,1:T(4,128)(2,1)S(1)}, bf16[512]{0:T(512)(128)(2,1)S(1)}) all-reduce(bf16[3,4,512]{2,0,1:T(4,128)(2,1)S(1)} %pad_maximum_fusion.5, bf16[512]{0:T(512)(128)(2,1)S(1)} %bitcast.272), channel_id=1, replica_groups=mesh['seq'=32,'tp'=8] {'seq'}, use_global_device_ids=true, to_apply=%region_13.14 | all-reduce | flops 6656 | bytes 26624 | tf_op jit(solution)/shard_map/psum | solution.py:196
  561.0 4.7 reduce-scatter.7.cloned.1.call-done
  565.7 1.0 copy.97
  567.4 154.3 %all-reduce.4.cloned.1.call-done = bf16[2,1024,512]{2,1,0:T(8,128)(2,1)} async-done(((bf16[2,1024,512]{2,1,0:T(8,128)(2,1)}), bf16[2,1024,512]{2,1,0:T(8,128)(2,1)}) %all-reduce.4.cloned.1.call-update) | async-done | bytes 2097168 | tf_op jit(solution)/shard_map/psum | solution.py:197
  721.7 4.2 convert_element_type.195
  725.9 33.3 %reduce-scatter.5.cloned.1.call-done = bf16[512,512]{1,0:T(8,128)(2,1)} async-done(((bf16[512,4096]{1,0:T(8,128)(2,1)}), bf16[512,512]{1,0:T(8,128)(2,1)}) %reduce-scatter.5.cloned.1.call-update) | async-done | bytes 524304 | tf_op jit(solution)/shard_map/reduce_scatter | solution.py:126
  (205 shorter events, 63.2 us)
Async XLA Ops:
  7.2 9.0 %copy-start.17 = (f32[4,512]{1,0:T(4,128)S(1)}, f32[4,512]{1,0:T(4,128)}, u32[]{:S(2)}) copy-start(f32[4,512]{1,0:T(4,128)} %param.20) | copy-start | bytes 24580
  7.2 10.9 %copy-start.18 = (s32[4,512]{1,0:T(4,128)S(1)}, s32[4,512]{1,0:T(4,128)}, u32[]{:S(2)}) copy-start(s32[4,512]{1,0:T(4,128)} %param.18) | copy-start | bytes 24580
  7.2 10.9 %copy-start.16 = (f32[3,4,512]{2,1,0:T(4,128)S(1)}, f32[3,4,512]{2,1,0:T(4,128)}, u32[]{:S(2)}) copy-start(f32[3,4,512]{2,1,0:T(4,128)} %param.17) | copy-start | bytes 73732
  7.2 109.6 %all-gather.10.cloned.1.call-start = ((), (), s32[]{:S(2)}) async-start(), calls=%async_computation.4 | async-start | bytes 4718592 | tf_op jit(solution)/shard_map/all_gather | solution.py:129
  7.9 124.6 %all-gather.8.cloned.1.call-start = ((), (), s32[]{:S(2)}) async-start(), calls=%async_computation.2 | async-start | bytes 4325376 | tf_op jit(solution)/shard_map/all_gather | solution.py:123
  8.7 209.5 %all-gather.12.cloned.1.call-start = ((), (), s32[]{:S(2)}) async-start(), calls=%async_computation.6 | async-start | bytes 4325376 | tf_op jit(solution)/shard_map/all_gather | solution.py:18
  12.7 11.8 %collective-permute-start = (bf16[3,3,512]{1,2,0:T(8,128)(2,1)S(1)}, bf16[3,3,512]{1,2,0:T(8,128)(2,1)S(1)}, u32[]{:S(2)}, u32[]{:S(2)}) collective-permute-start(bf16[3,3,512]{1,2,0:T(8,128)(2,1)S(1)} %pad_maximum_fusion.3), channel_id=1, source_target_pairs={{0,8},{8,16},{16,24},{24,32},{32,40},{40,48},{48,56},{56,64},{64,7... | collective-permute-start | bytes 27656 | tf_op jit(solution)/shard_map/ppermute | solution.py:12
  25.4 3.8 copy-start
  25.4 3.9 copy-start.19
  29.2 3.5 copy-start.20
  30.4 86.4 %copy-start.12 = (bf16[512,512]{0,1:T(8,128)(2,1)}, bf16[512,512]{0,1:T(8,128)(2,1)S(1)}, u32[]{:S(2)}) copy-start(bf16[512,512]{0,1:T(8,128)(2,1)S(1)} %get-tuple-element.326) | copy-start | bytes 1572868
  30.6 86.2 %copy-start.6 = (bf16[512,4,128]{2,0,1:T(8,128)(2,1)}, bf16[512,4,128]{2,0,1:T(8,128)(2,1)S(1)}, u32[]{:S(2)}) copy-start(bf16[512,4,128]{2,0,1:T(8,128)(2,1)S(1)} %copy.62) | copy-start | bytes 1572868
  32.7 309.1 %all-gather.14.cloned.1.call-start = ((), (), s32[]{:S(2)}) async-start(), calls=%async_computation.7 | async-start | bytes 4325376 | tf_op jit(solution)/shard_map/all_gather | solution.py:18
  114.0 170.6 %copy-start.14 = (pred[512,512]{1,0:T(8,128)(4,1)}, pred[512,512]{1,0:T(8,128)(4,1)S(1)}, u32[]{:S(2)}) copy-start(pred[512,512]{1,0:T(8,128)(4,1)S(1)} %iota_compare_fusion.4) | copy-start | bytes 786436
  138.4 239.6 %copy-start.5 = (bf16[512,512]{0,1:T(8,128)(2,1)}, bf16[512,512]{0,1:T(8,128)(2,1)S(1)}, u32[]{:S(2)}) copy-start(bf16[512,512]{0,1:T(8,128)(2,1)S(1)} %convolution_convert_fusion.4) | copy-start | bytes 1572868
  252.7 1.1 copy-start.8
  253.8 6.7 copy-start.15
  260.4 18.4 %copy-start.2 = (f32[4,512,128]{1,2,0:T(8,128)}, f32[4,512,128]{1,2,0:T(8,128)S(1)}, u32[]{:S(2)}) copy-start(f32[4,512,128]{1,2,0:T(8,128)S(1)} %get-tuple-element.325) | copy-start | bytes 3145732
  263.1 302.6 %reduce-scatter.7.cloned.1.call-start = ((), (), s32[]{:S(2)}) async-start(), calls=%async_computation.8 | async-start | bytes 4325376
  265.0 0.8 copy-start.9
  280.8 3.9 copy-start.13
  289.2 432.5 %all-reduce.4.cloned.1.call-start = ((), (), s32[]{:S(2)}) async-start(), calls=%async_computation.5 | async-start | bytes 4194304 | tf_op jit(solution)/shard_map/psum | solution.py:197
  375.9 2.0 copy-start.3
  375.9 2.0 copy-start.11
  381.4 1.8 copy-start.10
  382.9 376.3 %reduce-scatter.5.cloned.1.call-start = ((), (), s32[]{:S(2)}) async-start(), calls=%async_computation.3 | async-start | bytes 4718592 | tf_op jit(solution)/shard_map/reduce_scatter | solution.py:126
  389.7 1.2 copy-start.4
  391.0 6.3 copy-start.7
  400.6 5.7 collective-permute-start.1
  407.6 2.4 copy-start.1
Sparse Core Ops, SparseCore 0:
  9.8 36.5 all-gather.9
  48.9 83.6 all-gather.7
  135.7 82.4 all-gather.11
  263.2 78.5 all-gather.13
  345.6 220.0 reduce-scatter.6
  569.0 152.6 all-reduce.3
  724.8 34.2 reduce-scatter.4
where the time goes:
time: 777 us; the launch traced here: 766 us
  waiting for transfers between devices  350 us (45%)
  blocking collectives  219 us (28%)
  other arithmetic  90.9 us (12%)
  matrix products  59 us (8%)
  local copies, waits for them, and re-layouts  24.1 us (3%)
  between operations  15.5 us (2%)
    psum x1, waiting for transfers between devices, on_device(): lax.psum(table_terms.astype(jnp.bfloat16), 'seq').astype(jnp.float32)  154 us
    psum x1, blocking collectives, on_device(): lax.psum(tap_terms.astype(jnp.bfloat16), 'seq').astype(jnp.float32)  139 us
    all_gather x2, waiting for transfers between devices, entering(): lax.all_gather(part.astype(kind), axis)  132 us
    unnamed x1, blocking collectives  79.6 us
    select_n x64, other arithmetic, turn(): return jax.tree.map(lambda a, b: jnp.where(reached, a, b), new, before)  64.9 us
    reduce_scatter x1, waiting for transfers between devices, on_device(): lax.psum_scatter(partial_sum.astype(jnp.bfloat16), 'tp', scatter_dimensio...  33.3 us
    unnamed x58, local copies, waits for them, and re-layouts  19.7 us
    all_gather x1, waiting for transfers between devices, on_device(): lax.all_gather(out_weight, 'seq', axis=1, tiled=True)  15.7 us
  transfers between devices with their start and end apart: 9, of which 8 were waited for; matrix products, arithmetic and copies ran while one was open for 17% of the time, Pallas kernels for 0%

commit v1 on v0

--- a/solution.py
+++ b/solution.py
@@ -12,28 +12,17 @@
     return lax.ppermute(x, axis, pairs)
 
 
-def entering(x, axis, combine, identity, reverse):
-    length, here = (lax.axis_size(axis), lax.axis_index(axis))
-    everything = jax.tree.map(
-        lambda part, kind: lax.all_gather(part.astype(kind), axis), x, (jnp.bfloat16, jnp.bfloat16)
-    )
-    start = jax.tree.map(
-        lambda part, zero: jnp.broadcast_to(jnp.asarray(zero, part.dtype), part.shape), x, identity
-    )
-
-    def turn(k, before):
-        at = length - 1 - k if reverse else k
-        reached = at > here if reverse else at < here
-        new = combine(
-            before, jax.tree.map(lambda part, own: part[at].astype(own.dtype), everything, x)
-        )
-        return jax.tree.map(lambda a, b: jnp.where(reached, a, b), new, before)
-
-    return lax.fori_loop(0, length, turn, start)
-
-
-def combine(earlier, later):
-    return (earlier[0] * later[0], later[0][:, None, None] * earlier[1] + later[1])
+def entering(log_total, state, axis, reverse):
+    length = lax.axis_size(axis)
+    step = -1 if reverse else 1
+    log_total, state = shifted((log_total, state), axis, step)
+    distance = 1
+    while distance < length:
+        far_total, far_state = shifted((log_total, state), axis, step * distance)
+        state = jnp.exp(log_total)[:, None, None] * far_state + state
+        log_total = far_total + log_total
+        distance *= 2
+    return state
 
 
 def on_device(
@@ -93,7 +82,6 @@
     decay_total = decay_sum[:, -1]
     head_decay = jnp.exp(decay_sum)[:, :, None]
     tail_decay = jnp.exp(decay_total[:, None] - decay_sum)[:, :, None]
-    block_decay = jnp.exp(decay_total)
     positions = jnp.arange(row_count, dtype=jnp.int32)
     causal_mask = positions[:, None] >= positions[None, :]
     decay_mask = jnp.where(
@@ -101,12 +89,8 @@
         jnp.exp(jnp.minimum(decay_sum[:, :, None] - decay_sum[:, None, :], 0.0)),
         0.0,
     )
-    identity = (
-        jnp.ones((head_count,), jnp.float32),
-        jnp.zeros((head_count, head_size, head_size), jnp.float32),
-    )
     local_state = jnp.einsum("hsi,hsj->hij", key_heads * tail_decay, value_heads, precision=HIGHEST)
-    incoming = entering((block_decay, local_state), "seq", combine, identity, False)[1]
+    incoming = entering(decay_total, local_state, "seq", False)
     scores = decay_mask * jnp.einsum(
         "hti,hsi->hts", query_heads, key_heads, preferred_element_type=jnp.float32
     )
@@ -151,7 +135,7 @@
     back_state = jnp.einsum(
         "hti,htj->hij", query_heads * head_decay, grad_attended, precision=HIGHEST
     )
-    later_state = entering((block_decay, back_state), "seq", combine, identity, True)[1]
+    later_state = entering(decay_total, back_state, "seq", True)
     grad_scores = decay_mask * jnp.einsum(
         "htj,hsj->hts", grad_attended, value_heads, precision=HIGHEST
     )
@@ -192,11 +176,19 @@
             lax.dot_general(hot_y, grad_layout, contract_first, preferred_element_type=jnp.float32),
         ]
     )
-    grad_taps, grad_tables, grad_gain = (
-        lax.psum(tap_terms.astype(jnp.bfloat16), "seq").astype(jnp.float32),
-        lax.psum(table_terms.astype(jnp.bfloat16), "seq").astype(jnp.float32),
-        lax.psum(gain_terms.astype(jnp.bfloat16), "seq").astype(jnp.float32),
-    )
+    table_rows = 2 * buckets
+    tap_rows = 3 * kernel
+    packed = jnp.concatenate(
+        [
+            table_terms.reshape(table_rows, feat_width),
+            tap_terms.reshape(tap_rows, feat_width),
+            gain_terms.reshape(1, feat_width),
+        ]
+    )
+    summed = lax.psum(packed.astype(jnp.bfloat16), "seq").astype(jnp.float32)
+    grad_tables = summed[:table_rows].reshape(2, buckets, feat_width)
+    grad_taps = summed[table_rows : table_rows + tap_rows].reshape(3, kernel, feat_width)
+    grad_gain = summed[table_rows + tap_rows]
     grad_query = grad_inputs[0].astype(jnp.bfloat16)
     grad_key = grad_inputs[1].astype(jnp.bfloat16)
     grad_value = grad_inputs[2].astype(jnp.bfloat16)

time: 777 us -> 717 us (0.923)
  blocking collectives: 219 us -> 0 us
  waiting for transfers between devices: 350 us -> 465 us
  starting transfers between devices: 5.46 us -> 114 us
  other arithmetic: 90.9 us -> 22 us
  local copies, waits for them, and re-layouts: 24.1 us -> 39.3 us
  matrix products: 59 us -> 50.5 us
    unnamed x8 -> x6, waiting for transfers between devices: 6.13 us -> 219 us
    psum x1 -> x0, blocking collectives: 139 us -> none  [on_device(): lax.psum(tap_terms.astype(jnp.bfloat16), 'seq').astype(jnp.float32)]
    all_gather x2 -> x0, waiting for transfers between devices: 132 us -> none  [entering(): lax.all_gather(part.astype(kind), axis)]
    ppermute x2 -> x24, starting transfers between devices: 4.8 us -> 114 us  [shifted(): return lax.ppermute(x, axis, pairs)]
    unnamed x1 -> x0, blocking collectives: 79.6 us -> none
    select_n x64 -> x0, other arithmetic: 64.9 us -> none  [turn(): return jax.tree.map(lambda a, b: jnp.where(reached, a, b), new, before)]
    ppermute x2 -> x24, waiting for transfers between devices: 8.48 us -> 66.9 us  [shifted(): return lax.ppermute(x, axis, pairs)]
    psum x1, waiting for transfers between devices: 154 us -> 137 us  [on_device(): summed = lax.psum(packed.astype(jnp.bfloat16), 'seq').astype(jnp.float32)]
  transfers between devices with their start and end apart: 9 -> 29, of which waited for: 8 -> 19; matrix products, arithmetic and copies ran while one was open for 17% -> 11% of each run, Pallas kernels for 0% -> 0%
where the time goes in v1:
time: 717 us; the launch traced here: 706 us
  waiting for transfers between devices  465 us (65%)
  starting transfers between devices  114 us (16%)
  matrix products  50.5 us (7%)
  local copies, waits for them, and re-layouts  39.3 us (5%)
  other arithmetic  22 us (3%)
  between operations  14.8 us (2%)
    unnamed x6, waiting for transfers between devices  219 us
    psum x1, waiting for transfers between devices, on_device(): summed = lax.psum(packed.astype(jnp.bfloat16), 'seq').astype(jnp.float32)  137 us
    ppermute x24, starting transfers between devices, shifted(): return lax.ppermute(x, axis, pairs)  114 us
    ppermute x24, waiting for transfers between devices, shifted(): return lax.ppermute(x, axis, pairs)  66.9 us
    reduce_scatter x1, waiting for transfers between devices, on_device(): lax.psum_scatter(partial_sum.astype(jnp.bfloat16), 'tp', scatter_dimensio...  36.4 us
    unnamed x55, local copies, waits for them, and re-layouts  16.6 us
  transfers between devices with their start and end apart: 29, of which 19 were waited for; matrix products, arithmetic and copies ran while one was open for 11% of the time, Pallas kernels for 0%

profile of v1, /device:TPU:2, one launch (start us, length us, event | category | flops | bytes accessed | tf_op | source)
XLA Modules:
  0.0 706.0 jit_solution(11816550346031838033)
XLA Ops:
  12.7 3.5 collective-permute-start
  18.2 2.3 fusion.57
  20.5 4.1 collective-permute-done
  25.4 3.7 multiply_add_fusion
  30.6 1.3 fusion.80
  32.0 4.4 collective-permute-start.6
  36.4 4.7 collective-permute-done.6
  41.1 4.4 collective-permute-start.7
  45.5 3.5 collective-permute-start.1
  50.2 4.4 collective-permute-start.2
  54.6 1.3 collective-permute-done.2
  56.0 8.8 %collective-permute-start.8 = (f32[4,128,128]{2,1,0:T(8,128)S(1)}, f32[4,128,128]{2,1,0:T(8,128)S(1)}, u32[]{:S(2)}, u32[]{:S(2)}) collective-permute-start(f32[4,128,128]{2,1,0:T(8,128)S(1)} %multiply_add_fusion.11), channel_id=1, source_target_pairs={{0,16},{8,24},{16,32},{24,40},{32,48},{40,56},{48,64},{56,72},{64,... | collective-permute-start | bytes 786440 | tf_op jit(solution)/shard_map/ppermute | solution.py:12
  64.8 1.3 collective-permute-start.12
  66.1 3.3 collective-permute-done.8
  69.5 11.2 %collective-permute-start.9 = (f32[4,128,128]{2,1,0:T(8,128)S(1)}, f32[4,128,128]{2,1,0:T(8,128)S(1)}, u32[]{:S(2)}, u32[]{:S(2)}) collective-permute-start(f32[4,128,128]{2,1,0:T(8,128)S(1)} %multiply_add_fusion.10), channel_id=1, source_target_pairs={{0,32},{8,40},{16,48},{24,56},{32,64},{40,72},{48,80},{56,88},{64,... | collective-permute-start | bytes 786440 | tf_op jit(solution)/shard_map/ppermute | solution.py:12
  80.8 1.3 collective-permute-start.13
  82.1 2.9 collective-permute-start.3
  86.3 8.5 %collective-permute-start.4 = (f32[4]{0:T(128)S(1)}, f32[4]{0:T(128)S(1)}, u32[]{:S(2)}, u32[]{:S(2)}) collective-permute-start(f32[4]{0:T(128)S(1)} %get-tuple-element.57), channel_id=1, source_target_pairs={{0,32},{8,40},{16,48},{24,56},{32,64},{40,72},{48,80},{56,88},{64,... | collective-permute-start | bytes 56 | tf_op jit(solution)/shard_map/ppermute | solution.py:12
  94.9 12.6 %collective-permute-start.10 = (f32[4,128,128]{2,1,0:T(8,128)S(1)}, f32[4,128,128]{2,1,0:T(8,128)S(1)}, u32[]{:S(2)}, u32[]{:S(2)}) collective-permute-start(f32[4,128,128]{2,1,0:T(8,128)S(1)} %multiply_add_fusion.9), channel_id=1, source_target_pairs={{0,64},{8,72},{16,80},{24,88},{32,96},{40,104},{48,112},{56,120},{... | collective-permute-start | bytes 786440 | tf_op jit(solution)/shard_map/ppermute | solution.py:12
  107.5 3.1 collective-permute-start.5
  110.6 2.0 collective-permute-done.5
  112.8 20.0 %collective-permute-start.11 = (f32[4,128,128]{2,1,0:T(8,128)S(1)}, f32[4,128,128]{2,1,0:T(8,128)S(1)}, u32[]{:S(2)}, u32[]{:S(2)}) collective-permute-start(f32[4,128,128]{2,1,0:T(8,128)S(1)} %multiply_add_fusion.8), channel_id=1, source_target_pairs={{0,128},{8,136},{16,144},{24,152},{32,160},{40,168},{48,176},{56,1... | collective-permute-start | bytes 786440 | tf_op jit(solution)/shard_map/ppermute | solution.py:12
  133.6 2.7 collective-permute-done.11
  137.1 4.7 multiply_reduce_fusion.4
  141.8 5.4 all-gather.3.cloned.1.call-done
  147.3 5.8 convolution_convert_fusion.4
  153.6 1.4 fusion.77
  155.1 1.3 collective-permute-start.17
  156.4 1.3 collective-permute-start.14
  157.7 6.5 collective-permute-done.14
  164.2 1.3 collective-permute-start.15
  165.5 1.3 collective-permute-start.18
  166.8 3.6 collective-permute-done.15
  170.3 1.3 collective-permute-start.16
  171.6 9.4 %collective-permute-done.16 = f32[4]{0:T(128)S(1)} collective-permute-done((f32[4]{0:T(128)S(1)}, f32[4]{0:T(128)S(1)}, u32[]{:S(2)}, u32[]{:S(2)}) %collective-permute-start.16) | collective-permute-done | bytes 48 | tf_op jit(solution)/shard_map/ppermute | solution.py:12
  181.2 1.3 collective-permute-start.19
  182.5 3.9 fusion.40
  186.4 4.5 collective-permute-done.19
  191.1 12.5 %collective-permute-start.20 = (f32[4,128,128]{2,1,0:T(8,128)S(1)}, f32[4,128,128]{2,1,0:T(8,128)S(1)}, u32[]{:S(2)}, u32[]{:S(2)}) collective-permute-start(f32[4,128,128]{2,1,0:T(8,128)S(1)} %multiply_add_fusion.5), channel_id=1, source_target_pairs={{32,0},{40,8},{48,16},{56,24},{64,32},{72,40},{80,48},{88,56},{96,... | collective-permute-start | bytes 786440 | tf_op jit(solution)/shard_map/ppermute | solution.py:12
  203.6 2.1 fusion.109
  205.8 1.3 collective-permute-start.21
  207.1 3.5 fusion.34
  210.6 8.5 %collective-permute-done.21 = f32[4,128,128]{2,1,0:T(8,128)S(1)} collective-permute-done((f32[4,128,128]{2,1,0:T(8,128)S(1)}, f32[4,128,128]{2,1,0:T(8,128)S(1)}, u32[]{:S(2)}, u32[]{:S(2)}) %collective-permute-start.21) | collective-permute-done | bytes 262176 | tf_op jit(solution)/shard_map/ppermute | solution.py:12
  219.2 1.3 collective-permute-start.22
  220.5 2.8 fusion.37
  223.4 12.4 %collective-permute-done.22 = f32[4,128,128]{2,1,0:T(8,128)S(1)} collective-permute-done((f32[4,128,128]{2,1,0:T(8,128)S(1)}, f32[4,128,128]{2,1,0:T(8,128)S(1)}, u32[]{:S(2)}, u32[]{:S(2)}) %collective-permute-start.22) | collective-permute-done | bytes 262176 | tf_op jit(solution)/shard_map/ppermute | solution.py:12
  236.4 1.5 add_convert_fusion
  237.9 2.0 fusion.51
  239.9 2.0 fusion.50
  243.9 1.4 copy.96
  245.3 1.3 collective-permute-start.23
  246.6 3.1 pad_maximum_fusion.2
  249.7 1.4 collective-permute-done.23
  252.3 1.6 pad_maximum_fusion
  254.6 8.4 %multiply_reduce_fusion.3 = (bf16[3,512]{1,0:T(4,128)(2,1)S(1)}, bf16[3,512]{1,0:T(4,128)(2,1)S(1)}, bf16[3,512]{1,0:T(4,128)(2,1)S(1)}, bf16[3,512]{1,0:T(4,128)(2,1)S(1)}, bf16[3,512,512]{1,2,0:T(8,128)(2,1)}) fusion(f32[3,515,512]{1,2,0:T(8,128)S(1)} %copy-done.1, f32[1,512,512]{1,2,0:T(8,128)S(1)} %bitcast.203, f32[1,512,512]{1,2,0:T(8,128)S(1)} %bitcast.200, ...), kind=kLoop, calls=%fused_computation.17 | loop fusion | flops 14149632 | bytes 26775552 | tf_op jit(solution)/shard_map/reduce_sum | solution.py:164
  263.1 11.5 %concatenate.12 = bf16[2061,512]{1,0:T(8,128)(2,1)} concatenate(bf16[2048,512]{1,0:T(8,128)(2,1)} %bitcast.208, bf16[12,512]{1,0:T(8,128)(2,1)S(1)} %reshape.174, bf16[1,512]{1,0:T(2,128)(2,1)S(1)} %bitcast.249), dimensions={0} | concatenate | bytes 4220928 | tf_op jit(solution)/shard_map/concatenate | solution.py:181
  275.1 6.6 convolution_convert_fusion
  281.6 6.5 copy.116
  288.2 6.6 convolution_convert_fusion.1
  294.8 1.4 copy-done.4
  299.3 137.0 %all-reduce.2.cloned.1.call-done = bf16[2061,512]{1,0:T(8,128)(2,1)} async-done(((bf16[2061,512]{1,0:T(8,128)(2,1)}), bf16[2061,512]{1,0:T(8,128)(2,1)}) %all-reduce.2.cloned.1.call-update) | async-done | bytes 2110480 | tf_op jit(solution)/shard_map/psum | solution.py:188
  437.7 4.2 slice.153
  443.2 217.9 %reduce-scatter.7.cloned.1.call-done = bf16[128,512]{1,0:T(8,128)(2,1)} async-done(((bf16[4096,512]{1,0:T(8,128)(2,1)}), bf16[128,512]{1,0:T(8,128)(2,1)}) %reduce-scatter.7.cloned.1.call-update) | async-done | bytes 131088
  662.8 36.4 %reduce-scatter.5.cloned.1.call-done = bf16[512,512]{1,0:T(8,128)(2,1)} async-done(((bf16[512,4096]{1,0:T(8,128)(2,1)}), bf16[512,512]{1,0:T(8,128)(2,1)}) %reduce-scatter.5.cloned.1.call-update) | async-done | bytes 524304 | tf_op jit(solution)/shard_map/reduce_scatter | solution.py:110
  (125 shorter events, 27.9 us)
Async XLA Ops:
  7.2 9.0 %copy-start.18 = (f32[4,512]{1,0:T(4,128)S(1)}, f32[4,512]{1,0:T(4,128)}, u32[]{:S(2)}) copy-start(f32[4,512]{1,0:T(4,128)} %param.16) | copy-start | bytes 24580
  7.2 10.9 %copy-start.19 = (s32[4,512]{1,0:T(4,128)S(1)}, s32[4,512]{1,0:T(4,128)}, u32[]{:S(2)}) copy-start(s32[4,512]{1,0:T(4,128)} %param.14) | copy-start | bytes 24580
  7.2 10.9 %copy-start.17 = (f32[3,4,512]{2,1,0:T(4,128)S(1)}, f32[3,4,512]{2,1,0:T(4,128)}, u32[]{:S(2)}) copy-start(f32[3,4,512]{2,1,0:T(4,128)} %param.13) | copy-start | bytes 73732
  7.2 134.6 %all-gather.5.cloned.1.call-start = ((), (), s32[]{:S(2)}) async-start(), calls=%async_computation.4 | async-start | bytes 4718592 | tf_op jit(solution)/shard_map/all_gather | solution.py:113
  7.9 139.3 %all-gather.3.cloned.1.call-start = ((), (), s32[]{:S(2)}) async-start(), calls=%async_computation.2 | async-start | bytes 4325376 | tf_op jit(solution)/shard_map/all_gather | solution.py:107
  8.7 427.7 %all-reduce.2.cloned.1.call-start = ((), (), s32[]{:S(2)}) async-start(), calls=%async_computation.5 | async-start | bytes 4227072 | tf_op jit(solution)/shard_map/psum | solution.py:188
  12.7 11.8 %collective-permute-start = (bf16[3,3,512]{1,2,0:T(8,128)(2,1)S(1)}, bf16[3,3,512]{1,2,0:T(8,128)(2,1)S(1)}, u32[]{:S(2)}, u32[]{:S(2)}) collective-permute-start(bf16[3,3,512]{1,2,0:T(8,128)(2,1)S(1)} %pad_maximum_fusion.3), channel_id=1, source_target_pairs={{0,8},{8,16},{16,24},{24,32},{32,40},{40,48},{48,56},{56,64},{64,7... | collective-permute-start | bytes 27656 | tf_op jit(solution)/shard_map/ppermute | solution.py:12
  25.4 3.8 copy-start
  25.4 3.9 copy-start.20
  30.3 25.6 %copy-start.12 = (bf16[512,512]{0,1:T(8,128)(2,1)}, bf16[512,512]{0,1:T(8,128)(2,1)S(1)}, u32[]{:S(2)}) copy-start(bf16[512,512]{0,1:T(8,128)(2,1)S(1)} %get-tuple-element.60) | copy-start | bytes 1572868
  30.6 102.9 %copy-start.2 = (bf16[512,4,128]{2,0,1:T(8,128)(2,1)}, bf16[512,4,128]{2,0,1:T(8,128)(2,1)S(1)}, u32[]{:S(2)}) copy-start(bf16[512,4,128]{2,0,1:T(8,128)(2,1)S(1)} %copy.82) | copy-start | bytes 1572868
  32.0 9.1 %collective-permute-start.6 = (f32[4,128,128]{2,1,0:T(8,128)S(1)}, f32[4,128,128]{2,1,0:T(8,128)S(1)}, u32[]{:S(2)}, u32[]{:S(2)}) collective-permute-start(f32[4,128,128]{2,1,0:T(8,128)S(1)} %fusion.80), channel_id=1, source_target_pairs={{0,8},{8,16},{16,24},{24,32},{32,40},{40,48},{48,56},{56,64},{64,7... | collective-permute-start | bytes 786440 | tf_op jit(solution)/shard_map/ppermute | solution.py:12
  41.1 14.8 %collective-permute-start.7 = (f32[4,128,128]{2,1,0:T(8,128)S(1)}, f32[4,128,128]{2,1,0:T(8,128)S(1)}, u32[]{:S(2)}, u32[]{:S(2)}) collective-permute-start(f32[4,128,128]{2,1,0:T(8,128)S(1)} %collective-permute-done.6), channel_id=1, source_target_pairs={{0,8},{8,16},{16,24},{24,32},{32,40},{40,48},{48,56},{56,64},{64,7... | collective-permute-start | bytes 786440 | tf_op jit(solution)/shard_map/ppermute | solution.py:12
  45.5 4.8 collective-permute-start.1
  50.2 5.7 collective-permute-start.2
  56.0 13.4 %collective-permute-start.8 = (f32[4,128,128]{2,1,0:T(8,128)S(1)}, f32[4,128,128]{2,1,0:T(8,128)S(1)}, u32[]{:S(2)}, u32[]{:S(2)}) collective-permute-start(f32[4,128,128]{2,1,0:T(8,128)S(1)} %multiply_add_fusion.11), channel_id=1, source_target_pairs={{0,16},{8,24},{16,32},{24,40},{32,48},{40,56},{48,64},{56,72},{64,... | collective-permute-start | bytes 786440 | tf_op jit(solution)/shard_map/ppermute | solution.py:12
  64.8 16.0 %collective-permute-start.12 = (f32[4]{0:T(128)S(1)}, f32[4]{0:T(128)S(1)}, u32[]{:S(2)}, u32[]{:S(2)}) collective-permute-start(f32[4]{0:T(128)S(1)} %bitcast.254), channel_id=1, source_target_pairs={{8,0},{16,8},{24,16},{32,24},{40,32},{48,40},{56,48},{64,56},{72,6... | collective-permute-start | bytes 56 | tf_op jit(solution)/shard_map/ppermute | solution.py:12
  69.5 25.3 %collective-permute-start.9 = (f32[4,128,128]{2,1,0:T(8,128)S(1)}, f32[4,128,128]{2,1,0:T(8,128)S(1)}, u32[]{:S(2)}, u32[]{:S(2)}) collective-permute-start(f32[4,128,128]{2,1,0:T(8,128)S(1)} %multiply_add_fusion.10), channel_id=1, source_target_pairs={{0,32},{8,40},{16,48},{24,56},{32,64},{40,72},{48,80},{56,88},{64,... | collective-permute-start | bytes 786440 | tf_op jit(solution)/shard_map/ppermute | solution.py:12
  80.8 56.3 %copy-start.14 = (pred[512,512]{1,0:T(8,128)(4,1)}, pred[512,512]{1,0:T(8,128)(4,1)S(1)}, u32[]{:S(2)}) copy-start(pred[512,512]{1,0:T(8,128)(4,1)S(1)} %iota_compare_fusion.4) | copy-start | bytes 786436
  80.8 75.6 %collective-permute-start.13 = (f32[4]{0:T(128)S(1)}, f32[4]{0:T(128)S(1)}, u32[]{:S(2)}, u32[]{:S(2)}) collective-permute-start(f32[4]{0:T(128)S(1)} %collective-permute-done.12), channel_id=1, source_target_pairs={{8,0},{16,8},{24,16},{32,24},{40,32},{48,40},{56,48},{64,56},{72,6... | collective-permute-start | bytes 56 | tf_op jit(solution)/shard_map/ppermute | solution.py:12
  82.1 4.2 collective-permute-start.3
  86.3 21.2 %collective-permute-start.4 = (f32[4]{0:T(128)S(1)}, f32[4]{0:T(128)S(1)}, u32[]{:S(2)}, u32[]{:S(2)}) collective-permute-start(f32[4]{0:T(128)S(1)} %get-tuple-element.57), channel_id=1, source_target_pairs={{0,32},{8,40},{16,48},{24,56},{32,64},{40,72},{48,80},{56,88},{64,... | collective-permute-start | bytes 56 | tf_op jit(solution)/shard_map/ppermute | solution.py:12
  94.9 17.8 %collective-permute-start.10 = (f32[4,128,128]{2,1,0:T(8,128)S(1)}, f32[4,128,128]{2,1,0:T(8,128)S(1)}, u32[]{:S(2)}, u32[]{:S(2)}) collective-permute-start(f32[4,128,128]{2,1,0:T(8,128)S(1)} %multiply_add_fusion.9), channel_id=1, source_target_pairs={{0,64},{8,72},{16,80},{24,88},{32,96},{40,104},{48,112},{56,120},{... | collective-permute-start | bytes 786440 | tf_op jit(solution)/shard_map/ppermute | solution.py:12
  107.5 5.1 collective-permute-start.5
  112.8 23.5 %collective-permute-start.11 = (f32[4,128,128]{2,1,0:T(8,128)S(1)}, f32[4,128,128]{2,1,0:T(8,128)S(1)}, u32[]{:S(2)}, u32[]{:S(2)}) collective-permute-start(f32[4,128,128]{2,1,0:T(8,128)S(1)} %multiply_add_fusion.8), channel_id=1, source_target_pairs={{0,128},{8,136},{16,144},{24,152},{32,160},{40,168},{48,176},{56,1... | collective-permute-start | bytes 786440 | tf_op jit(solution)/shard_map/ppermute | solution.py:12
  133.6 8.2 %copy-start.5 = (f32[4,512,512]{2,1,0:T(8,128)}, f32[4,512,512]{2,1,0:T(8,128)S(1)}, u32[]{:S(2)}) copy-start(f32[4,512,512]{2,1,0:T(8,128)S(1)} %fusion.95) | copy-start | bytes 12582916
  136.3 0.7 copy-start.9
  137.1 4.7 copy-start.7
  141.8 11.3 %copy-start.16 = (f32[512]{0:T(512)S(1)}, f32[512]{0:T(512)}, u32[]{:S(2)}) copy-start(f32[512]{0:T(512)} %param.17) | copy-start | bytes 6148
  153.1 29.4 %copy-start.6 = (f32[4,512,512]{2,1,0:T(8,128)S(1)}, f32[4,512,512]{2,1,0:T(8,128)}, u32[]{:S(2)}) copy-start(f32[4,512,512]{2,1,0:T(8,128)} %copy-done.5) | copy-start | bytes 12582916
  153.1 29.4 %copy-start.15 = (pred[512,512]{1,0:T(8,128)(4,1)S(1)}, pred[512,512]{1,0:T(8,128)(4,1)}, u32[]{:S(2)}) copy-start(pred[512,512]{1,0:T(8,128)(4,1)} %copy-done.14) | copy-start | bytes 786436
  155.1 10.4 %collective-permute-start.17 = (f32[4,128,128]{2,1,0:T(8,128)S(1)}, f32[4,128,128]{2,1,0:T(8,128)S(1)}, u32[]{:S(2)}, u32[]{:S(2)}) collective-permute-start(f32[4,128,128]{2,1,0:T(8,128)S(1)} %fusion.77), channel_id=1, source_target_pairs={{8,0},{16,8},{24,16},{32,24},{40,32},{48,40},{56,48},{64,56},{72,6... | collective-permute-start | bytes 786440 | tf_op jit(solution)/shard_map/ppermute | solution.py:12
  156.4 7.8 %collective-permute-start.14 = (f32[4]{0:T(128)S(1)}, f32[4]{0:T(128)S(1)}, u32[]{:S(2)}, u32[]{:S(2)}) collective-permute-start(f32[4]{0:T(128)S(1)} %get-tuple-element.51), channel_id=1, source_target_pairs={{16,0},{24,8},{32,16},{40,24},{48,32},{56,40},{64,48},{72,56},{80,... | collective-permute-start | bytes 56 | tf_op jit(solution)/shard_map/ppermute | solution.py:12
  164.2 6.2 collective-permute-start.15
  165.5 15.6 %collective-permute-start.18 = (f32[4,128,128]{2,1,0:T(8,128)S(1)}, f32[4,128,128]{2,1,0:T(8,128)S(1)}, u32[]{:S(2)}, u32[]{:S(2)}) collective-permute-start(f32[4,128,128]{2,1,0:T(8,128)S(1)} %collective-permute-done.17), channel_id=1, source_target_pairs={{8,0},{16,8},{24,16},{32,24},{40,32},{48,40},{56,48},{64,56},{72,6... | collective-permute-start | bytes 786440 | tf_op jit(solution)/shard_map/ppermute | solution.py:12
  170.3 10.7 %collective-permute-start.16 = (f32[4]{0:T(128)S(1)}, f32[4]{0:T(128)S(1)}, u32[]{:S(2)}, u32[]{:S(2)}) collective-permute-start(f32[4]{0:T(128)S(1)} %get-tuple-element.47), channel_id=1, source_target_pairs={{64,0},{72,8},{80,16},{88,24},{96,32},{104,40},{112,48},{120,56},{... | collective-permute-start | bytes 56 | tf_op jit(solution)/shard_map/ppermute | solution.py:12
  181.2 9.8 %collective-permute-start.19 = (f32[4,128,128]{2,1,0:T(8,128)S(1)}, f32[4,128,128]{2,1,0:T(8,128)S(1)}, u32[]{:S(2)}, u32[]{:S(2)}) collective-permute-start(f32[4,128,128]{2,1,0:T(8,128)S(1)} %multiply_add_fusion.6), channel_id=1, source_target_pairs={{16,0},{24,8},{32,16},{40,24},{48,32},{56,40},{64,48},{72,56},{80,... | collective-permute-start | bytes 786440 | tf_op jit(solution)/shard_map/ppermute | solution.py:12
  191.0 16.0 %copy-start.13 = (bf16[512,512]{0,1:T(8,128)(2,1)S(1)}, bf16[512,512]{0,1:T(8,128)(2,1)}, u32[]{:S(2)}) copy-start(bf16[512,512]{0,1:T(8,128)(2,1)} %copy-done.12) | copy-start | bytes 1572868
  191.1 14.6 %collective-permute-start.20 = (f32[4,128,128]{2,1,0:T(8,128)S(1)}, f32[4,128,128]{2,1,0:T(8,128)S(1)}, u32[]{:S(2)}, u32[]{:S(2)}) collective-permute-start(f32[4,128,128]{2,1,0:T(8,128)S(1)} %multiply_add_fusion.5), channel_id=1, source_target_pairs={{32,0},{40,8},{48,16},{56,24},{64,32},{72,40},{80,48},{88,56},{96,... | collective-permute-start | bytes 786440 | tf_op jit(solution)/shard_map/ppermute | solution.py:12
  205.8 13.4 %collective-permute-start.21 = (f32[4,128,128]{2,1,0:T(8,128)S(1)}, f32[4,128,128]{2,1,0:T(8,128)S(1)}, u32[]{:S(2)}, u32[]{:S(2)}) collective-permute-start(f32[4,128,128]{2,1,0:T(8,128)S(1)} %multiply_add_fusion.4), channel_id=1, source_target_pairs={{64,0},{72,8},{80,16},{88,24},{96,32},{104,40},{112,48},{120,56},{... | collective-permute-start | bytes 786440 | tf_op jit(solution)/shard_map/ppermute | solution.py:12
  219.2 16.5 %collective-permute-start.22 = (f32[4,128,128]{2,1,0:T(8,128)S(1)}, f32[4,128,128]{2,1,0:T(8,128)S(1)}, u32[]{:S(2)}, u32[]{:S(2)}) collective-permute-start(f32[4,128,128]{2,1,0:T(8,128)S(1)} %multiply_add_fusion.3), channel_id=1, source_target_pairs={{128,0},{136,8},{144,16},{152,24},{160,32},{168,40},{176,48},{184,... | collective-permute-start | bytes 786440 | tf_op jit(solution)/shard_map/ppermute | solution.py:12
  223.4 13.0 %copy-start.10 = (f32[4,128,128]{2,1,0:T(8,128)S(1)}, f32[4,128,128]{2,1,0:T(8,128)}, u32[]{:S(2)}) copy-start(f32[4,128,128]{2,1,0:T(8,128)} %copy-done.9) | copy-start | bytes 786436
  237.9 4.0 copy-start.3
  245.3 5.7 collective-permute-start.23
  252.3 2.3 copy-start.1
  263.1 11.8 %copy-start.8 = (f32[4,512,128]{1,2,0:T(8,128)S(1)}, f32[4,512,128]{1,2,0:T(8,128)}, u32[]{:S(2)}) copy-start(f32[4,512,128]{1,2,0:T(8,128)} %copy-done.7) | copy-start | bytes 3145732
  263.1 11.8 %copy-start.11 = (f32[4,512,128]{1,2,0:T(8,128)S(1)}, f32[4,512,128]{1,2,0:T(8,128)}, u32[]{:S(2)}) copy-start(f32[4,512,128]{1,2,0:T(8,128)} %get-tuple-element.81) | copy-start | bytes 3145732
  274.6 386.5 %reduce-scatter.7.cloned.1.call-start = ((), (), s32[]{:S(2)}) async-start(), calls=%async_computation.6 | async-start | bytes 4325376
  288.2 411.1 %reduce-scatter.5.cloned.1.call-start = ((), (), s32[]{:S(2)}) async-start(), calls=%async_computation.3 | async-start | bytes 4718592 | tf_op jit(solution)/shard_map/reduce_scatter | solution.py:110
  294.8 1.4 copy-start.4
Sparse Core Ops, SparseCore 0:
  9.8 36.5 all-gather.4
  48.9 98.3 all-gather.2
  274.8 161.5 all-reduce.1
  440.1 220.9 reduce-scatter.6
  664.1 35.1 reduce-scatter.4

commit v2 on v1

--- a/solution.py
+++ b/solution.py
@@ -15,14 +15,22 @@
 def entering(log_total, state, axis, reverse):
     length = lax.axis_size(axis)
     step = -1 if reverse else 1
-    log_total, state = shifted((log_total, state), axis, step)
+    heads, rows, cols = state.shape
+    total_rows = jnp.broadcast_to(log_total[:, None, None], (heads, 8, cols))
+    packed = shifted(jnp.concatenate([state, total_rows], axis=1), axis, step)
     distance = 1
     while distance < length:
-        far_total, far_state = shifted((log_total, state), axis, step * distance)
-        state = jnp.exp(log_total)[:, None, None] * far_state + state
-        log_total = far_total + log_total
+        far = shifted(packed, axis, step * distance)
+        near_total = packed[:, rows : rows + 1, :]
+        packed = jnp.concatenate(
+            [
+                jnp.exp(near_total) * far[:, :rows, :] + packed[:, :rows, :],
+                far[:, rows:, :] + packed[:, rows:, :],
+            ],
+            axis=1,
+        )
         distance *= 2
-    return state
+    return packed[:, :rows, :]
 
 
 def on_device(
@@ -123,9 +131,15 @@
     weight_terms = lax.dot_general(
         normed, cotangent, contract_first, preferred_element_type=jnp.float32
     )
-    grad_weight = lax.psum_scatter(
-        weight_terms.astype(jnp.bfloat16), "seq", scatter_dimension=1, tiled=True
-    ).astype(jnp.float32)
+    seq_count = lax.axis_size("seq")
+    col_block = weight_terms.shape[1] // seq_count
+    weight_parts = (
+        weight_terms.astype(jnp.bfloat16)
+        .reshape(feat_width, seq_count, col_block)
+        .transpose(1, 0, 2)
+    )
+    weight_parts = lax.all_to_all(weight_parts, "seq", 0, 0, tiled=True)
+    grad_weight = jnp.sum(weight_parts.astype(jnp.float32), axis=0)
     grad_heads = split_heads(grad_normed).astype(jnp.float32)
     gain_terms = jnp.sum(grad_heads * unit_norm, axis=1).reshape(feat_width)
     grad_unit = grad_heads * gain_heads
@@ -185,6 +199,7 @@
             gain_terms.reshape(1, feat_width),
         ]
     )
+    packed, layer_out = lax.optimization_barrier((packed, layer_out))
     summed = lax.psum(packed.astype(jnp.bfloat16), "seq").astype(jnp.float32)
     grad_tables = summed[:table_rows].reshape(2, buckets, feat_width)
     grad_taps = summed[table_rows : table_rows + tap_rows].reshape(3, kernel, feat_width)

time: 717 us -> 540 us (0.75)
  waiting for transfers between devices: 465 us -> 331 us
  starting transfers between devices: 114 us -> 78.9 us
    unnamed x6 -> x4, waiting for transfers between devices: 219 us -> 0.73 us
    ppermute x24 -> x14, waiting for transfers between devices: 66.9 us -> 145 us  [shifted(): return lax.ppermute(x, axis, pairs)]
    ppermute x24 -> x14, starting transfers between devices: 114 us -> 71.6 us  [shifted(): return lax.ppermute(x, axis, pairs)]
    reduce_scatter x1, waiting for transfers between devices: 36.4 us -> 0.01 us  [on_device(): lax.psum_scatter(partial_sum.astype(jnp.bfloat16), 'tp', scatter_dimensio...]
    all_gather x1, waiting for transfers between devices: 5.43 us -> 28.5 us  [on_device(): lax.all_gather(out_weight, 'seq', axis=1, tiled=True)]
    psum x1, waiting for transfers between devices: 137 us -> 157 us  [on_device(): summed = lax.psum(packed.astype(jnp.bfloat16), 'seq').astype(jnp.float32)]
    unnamed x55 -> x62, local copies, waits for them, and re-layouts: 16.6 us -> 8.37 us
  transfers between devices with their start and end apart: 29 -> 19, of which waited for: 19 -> 14; matrix products, arithmetic and copies ran while one was open for 11% -> 17% of each run, Pallas kernels for 0% -> 0%
where the time goes in v2:
time: 540 us; the launch traced here: 533 us
  waiting for transfers between devices  331 us (61%)
  starting transfers between devices  78.9 us (15%)
  matrix products  46.3 us (9%)
  local copies, waits for them, and re-layouts  35.2 us (7%)
  other arithmetic  26.4 us (5%)
  between operations  14.9 us (3%)
    psum x1, waiting for transfers between devices, on_device(): summed = lax.psum(packed.astype(jnp.bfloat16), 'seq').astype(jnp.float32)  157 us
    ppermute x14, waiting for transfers between devices, shifted(): return lax.ppermute(x, axis, pairs)  145 us
    ppermute x14, starting transfers between devices, shifted(): return lax.ppermute(x, axis, pairs)  71.6 us
    all_gather x1, waiting for transfers between devices, on_device(): lax.all_gather(out_weight, 'seq', axis=1, tiled=True)  28.5 us
    concatenate x1, local copies, waits for them, and re-layouts, on_device(): jnp.concatenate([table_terms.reshape(table_rows, feat_width), tap_terms.r...  11.5 us
  transfers between devices with their start and end apart: 19, of which 14 were waited for; matrix products, arithmetic and copies ran while one was open for 17% of the time, Pallas kernels for 0%

profile of v2, /device:TPU:2, one launch (start us, length us, event | category | flops | bytes accessed | tf_op | source)
XLA Modules:
  0.0 533.0 jit_solution(723401852916892114)
XLA Ops:
  8.0 1.3 copy.58
  9.2 1.3 copy.59
  10.5 1.3 copy.60
  11.9 3.5 collective-permute-start
  15.6 1.2 reduce-window.6
  17.5 2.3 fusion.56
  19.8 4.0 collective-permute-done
  24.6 3.7 multiply_add_fusion
  28.5 1.1 fusion.62
  30.4 1.3 fusion.79
  31.8 4.4 collective-permute-start.1
  36.2 5.0 collective-permute-done.1
  41.3 4.4 collective-permute-start.2
  45.7 4.3 collective-permute-done.2
  50.0 6.0 %collective-permute-start.3 = (f32[4,136,128]{2,1,0:T(8,128)S(1)}, f32[4,136,128]{2,1,0:T(8,128)S(1)}, u32[]{:S(2)}, u32[]{:S(2)}) collective-permute-start(f32[4,136,128]{2,1,0:T(8,128)S(1)} %pad_maximum_fusion.7), channel_id=1, source_target_pairs={{0,16},{8,24},{16,32},{24,40},{32,48},{40,56},{48,64},{56,72},{64,... | collective-permute-start | bytes 835592 | tf_op jit(solution)/shard_map/ppermute | solution.py:12
  56.0 4.0 collective-permute-done.3
  60.1 12.8 %collective-permute-start.4 = (f32[4,136,128]{2,1,0:T(8,128)S(1)}, f32[4,136,128]{2,1,0:T(8,128)S(1)}, u32[]{:S(2)}, u32[]{:S(2)}) collective-permute-start(f32[4,136,128]{2,1,0:T(8,128)S(1)} %pad_maximum_fusion.8), channel_id=1, source_target_pairs={{0,32},{8,40},{16,48},{24,56},{32,64},{40,72},{48,80},{56,88},{64,... | collective-permute-start | bytes 835592 | tf_op jit(solution)/shard_map/ppermute | solution.py:12
  72.9 4.7 collective-permute-done.4
  77.7 6.3 %collective-permute-start.5 = (f32[4,136,128]{2,1,0:T(8,128)S(1)}, f32[4,136,128]{2,1,0:T(8,128)S(1)}, u32[]{:S(2)}, u32[]{:S(2)}) collective-permute-start(f32[4,136,128]{2,1,0:T(8,128)S(1)} %pad_maximum_fusion.9), channel_id=1, source_target_pairs={{0,64},{8,72},{16,80},{24,88},{32,96},{40,104},{48,112},{56,120},{... | collective-permute-start | bytes 835592 | tf_op jit(solution)/shard_map/ppermute | solution.py:12
  84.2 4.3 collective-permute-done.5
  88.5 24.3 %collective-permute-start.6 = (f32[4,136,128]{2,1,0:T(8,128)S(1)}, f32[4,136,128]{2,1,0:T(8,128)S(1)}, u32[]{:S(2)}, u32[]{:S(2)}) collective-permute-start(f32[4,136,128]{2,1,0:T(8,128)S(1)} %pad_maximum_fusion.10), channel_id=1, source_target_pairs={{0,128},{8,136},{16,144},{24,152},{32,160},{40,168},{48,176},{56,1... | collective-permute-start | bytes 835592 | tf_op jit(solution)/shard_map/ppermute | solution.py:12
  113.6 4.9 collective-permute-done.6
  119.2 3.6 multiply_reduce_fusion.4
  122.8 1.1 fusion.66
  123.9 28.5 %all-gather.5.cloned.1.call-done = bf16[512,4096]{1,0:T(8,128)(2,1)} async-done(((bf16[512,128]{1,0:T(8,128)(2,1)}), bf16[512,4096]{1,0:T(8,128)(2,1)}) %all-gather.5.cloned.1.call-update) | async-done | bytes 4194320 | tf_op jit(solution)/shard_map/all_gather | solution.py:125
  152.4 5.9 %convolution_convert_fusion.2 = bf16[512,512]{0,1:T(8,128)(2,1)S(1)} fusion(bf16[512,4096]{1,0:T(8,128)(2,1)} %all-gather.3.cloned.1.call-done, bf16[512,4096]{1,0:T(8,128)(2,1)} %all-gather.5.cloned.1.call-done), kind=kOutput, calls=%fused_computation.68 | convolution fusion | flops 2147745792 | bytes 8912896 | tf_op jit(solution)/shard_map/dot_general | solution.py:123
  158.8 1.4 fusion.76
  161.0 1.3 collective-permute-start.7
  162.3 4.4 convolution_convert_fusion.1
  166.7 5.3 collective-permute-done.7
  172.0 1.5 collective-permute-start.8
  173.5 4.5 fusion.14
  178.0 3.2 copy.114
  181.2 7.1 %all-to-all-start = ((bf16[32,512,128]{2,1,0:T(8,128)(2,1)}), bf16[32,512,128]{2,1,0:T(8,128)(2,1)}, u32[]{:S(2)}, u32[]{:S(2)}) async-start(bf16[32,512,128]{2,1,0:T(8,128)(2,1)} %bitcast.202), calls=%async_computation.1 | async-start | bytes 8388608 | tf_op jit(solution)/shard_map/all_to_all | solution.py:141
  189.9 1.1 slice_add_fusion
  191.0 1.3 collective-permute-start.9
  192.3 5.8 %fusion.41 = f32[512,4,128]{0,2,1:T(8,128)S(1)} fusion(f32[4,512,512]{2,1,0:T(8,128)} %copy-done.7, f32[4,512]{1,0:T(4,128)S(1)} %bitcast.243, pred[512,512]{1,0:T(8,128)(4,1)S(1)} %copy-done.19, f32[4,512,128]{1,2,0:T(8,128)S(1)} %get-tuple-element.43, f32[4,512]{1,0:T(4,128)S(1)} %broadcast_multiply_fusion, f32[4,128]{1,0:T(4,128)S(1)} %bitcast.234, ...), kind=kOutput, calls=%fused_computation.56 | convolution fusion | flops 1616379904 | bytes 7104512 | tf_op jit(solution)/shard_map/hts,htj->hsj/dot_general | solution.py:162
  198.1 7.6 %collective-permute-done.9 = f32[4,136,128]{2,1,0:T(8,128)S(1)} collective-permute-done((f32[4,136,128]{2,1,0:T(8,128)S(1)}, f32[4,136,128]{2,1,0:T(8,128)S(1)}, u32[]{:S(2)}, u32[]{:S(2)}) %collective-permute-start.9) | collective-permute-done | bytes 278560 | tf_op jit(solution)/shard_map/ppermute | solution.py:12
  205.8 1.4 collective-permute-start.10
  207.2 2.0 fusion.120
  209.2 78.8 %collective-permute-done.10 = f32[4,136,128]{2,1,0:T(8,128)S(1)} collective-permute-done((f32[4,136,128]{2,1,0:T(8,128)S(1)}, f32[4,136,128]{2,1,0:T(8,128)S(1)}, u32[]{:S(2)}, u32[]{:S(2)}) %collective-permute-start.10) | collective-permute-done | bytes 278560 | tf_op jit(solution)/shard_map/ppermute | solution.py:12
  288.1 1.3 collective-permute-start.11
  289.5 3.5 fusion.35
  292.9 7.8 %collective-permute-done.11 = f32[4,136,128]{2,1,0:T(8,128)S(1)} collective-permute-done((f32[4,136,128]{2,1,0:T(8,128)S(1)}, f32[4,136,128]{2,1,0:T(8,128)S(1)}, u32[]{:S(2)}, u32[]{:S(2)}) %collective-permute-start.11) | collective-permute-done | bytes 278560 | tf_op jit(solution)/shard_map/ppermute | solution.py:12
  300.8 1.5 collective-permute-start.12
  302.3 2.7 fusion.38
  305.1 14.7 %collective-permute-done.12 = f32[4,136,128]{2,1,0:T(8,128)S(1)} collective-permute-done((f32[4,136,128]{2,1,0:T(8,128)S(1)}, f32[4,136,128]{2,1,0:T(8,128)S(1)}, u32[]{:S(2)}, u32[]{:S(2)}) %collective-permute-start.12) | collective-permute-done | bytes 278560 | tf_op jit(solution)/shard_map/ppermute | solution.py:12
  321.3 2.2 add_convert_fusion
  323.8 1.1 slice.308
  324.9 1.4 copy.75
  326.3 1.7 collective-permute-start.13
  328.0 2.0 convolution_bitcast_fusion.1
  331.0 1.5 pad_maximum_fusion
  332.5 1.3 copy.76
  333.8 1.6 pad_maximum_fusion.1
  336.1 8.4 %multiply_reduce_fusion.3 = (bf16[3,512]{1,0:T(4,128)(2,1)S(1)}, bf16[3,512]{1,0:T(4,128)(2,1)S(1)}, bf16[3,512]{1,0:T(4,128)(2,1)S(1)}, bf16[3,512]{1,0:T(4,128)(2,1)S(1)}, bf16[3,512,512]{1,2,0:T(8,128)(2,1)}) fusion(f32[3,515,512]{1,2,0:T(8,128)S(1)} %copy-done.1, f32[1,512,512]{1,2,0:T(8,128)S(1)} %bitcast.205, f32[1,512,512]{1,2,0:T(8,128)S(1)} %bitcast.198, ...), kind=kLoop, calls=%fused_computation.20 | loop fusion | flops 14149632 | bytes 26775552 | tf_op jit(solution)/shard_map/reduce_sum | solution.py:178
  344.6 11.5 %concatenate.50 = bf16[2061,512]{1,0:T(8,128)(2,1)} concatenate(bf16[2048,512]{1,0:T(8,128)(2,1)} %bitcast.206, bf16[12,512]{1,0:T(8,128)(2,1)S(1)} %reshape.166, f32[1,512]{1,0:T(1,128)S(1)} %bitcast.246), dimensions={0} | concatenate | bytes 4221952 | tf_op jit(solution)/shard_map/concatenate | solution.py:195
  356.2 1.0 copy.78
  357.2 1.0 copy.79
  358.2 1.0 copy.80
  359.2 3.5 convert_reduce_fusion
  362.7 156.6 %all-reduce.2.cloned.1.call-done = bf16[2061,512]{1,0:T(8,128)(2,1)} async-done(((bf16[2061,512]{1,0:T(8,128)(2,1)}), bf16[2061,512]{1,0:T(8,128)(2,1)}) %all-reduce.2.cloned.1.call-update) | async-done | bytes 2110480 | tf_op jit(solution)/shard_map/psum | solution.py:203
  520.7 4.2 slice.316
  524.9 1.3 slice.317
  (136 shorter events, 13.2 us)
Async XLA Ops:
  7.2 8.4 %copy-start.22 = (f32[3,4,512]{2,1,0:T(4,128)S(1)}, f32[3,4,512]{2,1,0:T(4,128)}, u32[]{:S(2)}) copy-start(f32[3,4,512]{2,1,0:T(4,128)} %param.13) | copy-start | bytes 73732
  7.2 8.4 %copy-start.23 = (f32[4,512]{1,0:T(4,128)S(1)}, f32[4,512]{1,0:T(4,128)}, u32[]{:S(2)}) copy-start(f32[4,512]{1,0:T(4,128)} %param.16) | copy-start | bytes 24580
  7.2 10.2 %copy-start.24 = (s32[4,512]{1,0:T(4,128)S(1)}, s32[4,512]{1,0:T(4,128)}, u32[]{:S(2)}) copy-start(s32[4,512]{1,0:T(4,128)} %param.14) | copy-start | bytes 24580
  7.2 116.7 %all-gather.3.cloned.1.call-start = ((), (), s32[]{:S(2)}) async-start(), calls=%async_computation.2 | async-start | bytes 4718592 | tf_op jit(solution)/shard_map/all_gather | solution.py:121
  7.9 144.5 %all-gather.5.cloned.1.call-start = ((), (), s32[]{:S(2)}) async-start(), calls=%async_computation.3 | async-start | bytes 4325376 | tf_op jit(solution)/shard_map/all_gather | solution.py:125
  11.9 11.8 %collective-permute-start = (bf16[3,3,512]{1,2,0:T(8,128)(2,1)S(1)}, bf16[3,3,512]{1,2,0:T(8,128)(2,1)S(1)}, u32[]{:S(2)}, u32[]{:S(2)}) collective-permute-start(bf16[3,3,512]{1,2,0:T(8,128)(2,1)S(1)} %pad_maximum_fusion.5), channel_id=1, source_target_pairs={{0,8},{8,16},{16,24},{24,32},{32,40},{40,48},{48,56},{56,64},{64,7... | collective-permute-start | bytes 27656 | tf_op jit(solution)/shard_map/ppermute | solution.py:12
  15.5 340.6 %reduce-scatter.2.cloned.1.call-start = ((), (), s32[]{:S(2)}) async-start(), calls=%async_computation.4 | async-start | bytes 4718592 | tf_op jit(solution)/shard_map/reduce_scatter | solution.py:118
  24.6 3.8 copy-start
  24.6 3.9 copy-start.25
  29.6 0.8 copy-start.16
  29.6 129.2 %copy-start.9 = (bf16[512,512]{0,1:T(8,128)(2,1)}, bf16[512,512]{0,1:T(8,128)(2,1)S(1)}, u32[]{:S(2)}) copy-start(bf16[512,512]{0,1:T(8,128)(2,1)S(1)} %get-tuple-element.44) | copy-start | bytes 1572868
  31.8 9.4 %collective-permute-start.1 = (f32[4,136,128]{2,1,0:T(8,128)S(1)}, f32[4,136,128]{2,1,0:T(8,128)S(1)}, u32[]{:S(2)}, u32[]{:S(2)}) collective-permute-start(f32[4,136,128]{2,1,0:T(8,128)S(1)} %pad_maximum_fusion.4), channel_id=1, source_target_pairs={{0,8},{8,16},{16,24},{24,32},{32,40},{40,48},{48,56},{56,64},{64,7... | collective-permute-start | bytes 835592 | tf_op jit(solution)/shard_map/ppermute | solution.py:12
  41.3 8.7 %collective-permute-start.2 = (f32[4,136,128]{2,1,0:T(8,128)S(1)}, f32[4,136,128]{2,1,0:T(8,128)S(1)}, u32[]{:S(2)}, u32[]{:S(2)}) collective-permute-start(f32[4,136,128]{2,1,0:T(8,128)S(1)} %collective-permute-done.1), channel_id=1, source_target_pairs={{0,8},{8,16},{16,24},{24,32},{32,40},{40,48},{48,56},{56,64},{64,7... | collective-permute-start | bytes 835592 | tf_op jit(solution)/shard_map/ppermute | solution.py:12
  50.0 10.1 %collective-permute-start.3 = (f32[4,136,128]{2,1,0:T(8,128)S(1)}, f32[4,136,128]{2,1,0:T(8,128)S(1)}, u32[]{:S(2)}, u32[]{:S(2)}) collective-permute-start(f32[4,136,128]{2,1,0:T(8,128)S(1)} %pad_maximum_fusion.7), channel_id=1, source_target_pairs={{0,16},{8,24},{16,32},{24,40},{32,48},{40,56},{48,64},{56,72},{64,... | collective-permute-start | bytes 835592 | tf_op jit(solution)/shard_map/ppermute | solution.py:12
  60.1 17.5 %collective-permute-start.4 = (f32[4,136,128]{2,1,0:T(8,128)S(1)}, f32[4,136,128]{2,1,0:T(8,128)S(1)}, u32[]{:S(2)}, u32[]{:S(2)}) collective-permute-start(f32[4,136,128]{2,1,0:T(8,128)S(1)} %pad_maximum_fusion.8), channel_id=1, source_target_pairs={{0,32},{8,40},{16,48},{24,56},{32,64},{40,72},{48,80},{56,88},{64,... | collective-permute-start | bytes 835592 | tf_op jit(solution)/shard_map/ppermute | solution.py:12
  77.7 10.7 %collective-permute-start.5 = (f32[4,136,128]{2,1,0:T(8,128)S(1)}, f32[4,136,128]{2,1,0:T(8,128)S(1)}, u32[]{:S(2)}, u32[]{:S(2)}) collective-permute-start(f32[4,136,128]{2,1,0:T(8,128)S(1)} %pad_maximum_fusion.9), channel_id=1, source_target_pairs={{0,64},{8,72},{16,80},{24,88},{32,96},{40,104},{48,112},{56,120},{... | collective-permute-start | bytes 835592 | tf_op jit(solution)/shard_map/ppermute | solution.py:12
  84.1 35.0 %copy-start.18 = (pred[512,512]{1,0:T(8,128)(4,1)}, pred[512,512]{1,0:T(8,128)(4,1)S(1)}, u32[]{:S(2)}) copy-start(pred[512,512]{1,0:T(8,128)(4,1)S(1)} %iota_compare_fusion.4) | copy-start | bytes 786436
  88.5 30.0 %collective-permute-start.6 = (f32[4,136,128]{2,1,0:T(8,128)S(1)}, f32[4,136,128]{2,1,0:T(8,128)S(1)}, u32[]{:S(2)}, u32[]{:S(2)}) collective-permute-start(f32[4,136,128]{2,1,0:T(8,128)S(1)} %pad_maximum_fusion.10), channel_id=1, source_target_pairs={{0,128},{8,136},{16,144},{24,152},{32,160},{40,168},{48,176},{56,1... | collective-permute-start | bytes 835592 | tf_op jit(solution)/shard_map/ppermute | solution.py:12
  113.5 5.6 %copy-start.7 = (f32[4,512,512]{2,1,0:T(8,128)}, f32[4,512,512]{2,1,0:T(8,128)S(1)}, u32[]{:S(2)}) copy-start(f32[4,512,512]{2,1,0:T(8,128)S(1)} %fusion.94) | copy-start | bytes 12582916
  118.5 4.3 copy-start.13
  119.2 3.7 copy-start.21
  122.8 84.4 %copy-start.2 = (f32[4,512,128]{1,2,0:T(8,128)}, f32[4,512,128]{1,2,0:T(8,128)S(1)}, u32[]{:S(2)}) copy-start(f32[4,512,128]{1,2,0:T(8,128)S(1)} %get-tuple-element.43) | copy-start | bytes 3145732
  152.4 9.8 %copy-start.11 = (bf16[512,4,128]{0,2,1:T(8,128)(2,1)S(1)}, bf16[512,4,128]{0,2,1:T(8,128)(2,1)}, u32[]{:S(2)}) copy-start(bf16[512,4,128]{0,2,1:T(8,128)(2,1)} %fusion.66) | copy-start | bytes 1572868
  158.3 48.9 %copy-start.5 = (bf16[512,512]{0,1:T(8,128)(2,1)}, bf16[512,512]{0,1:T(8,128)(2,1)S(1)}, u32[]{:S(2)}) copy-start(bf16[512,512]{0,1:T(8,128)(2,1)S(1)} %convolution_convert_fusion.2) | copy-start | bytes 1572868
  158.3 4.0 copy-start.8
  161.0 11.0 %collective-permute-start.7 = (f32[4,136,128]{2,1,0:T(8,128)}, f32[4,136,128]{2,1,0:T(8,128)}, u32[]{:S(2)}, u32[]{:S(2)}) collective-permute-start(f32[4,136,128]{2,1,0:T(8,128)} %pad_maximum_fusion.3), channel_id=1, source_target_pairs={{8,0},{16,8},{24,16},{32,24},{40,32},{48,40},{56,48},{64,56},{72,6... | collective-permute-start | bytes 835592 | tf_op jit(solution)/shard_map/ppermute | solution.py:12
  166.7 6.8 %copy-start.12 = (bf16[512,4,128]{0,2,1:T(8,128)(2,1)S(1)}, bf16[512,4,128]{0,2,1:T(8,128)(2,1)}, u32[]{:S(2)}) copy-start(bf16[512,4,128]{0,2,1:T(8,128)(2,1)} %fusion.66) | copy-start | bytes 1572868
  172.0 17.1 %collective-permute-start.8 = (f32[4,136,128]{2,1,0:T(8,128)}, f32[4,136,128]{2,1,0:T(8,128)}, u32[]{:S(2)}, u32[]{:S(2)}) collective-permute-start(f32[4,136,128]{2,1,0:T(8,128)} %collective-permute-done.7), channel_id=1, source_target_pairs={{8,0},{16,8},{24,16},{32,24},{40,32},{48,40},{56,48},{64,56},{72,6... | collective-permute-start | bytes 835592 | tf_op jit(solution)/shard_map/ppermute | solution.py:12
  181.2 11.0 %copy-start.19 = (pred[512,512]{1,0:T(8,128)(4,1)S(1)}, pred[512,512]{1,0:T(8,128)(4,1)}, u32[]{:S(2)}) copy-start(pred[512,512]{1,0:T(8,128)(4,1)} %copy-done.18) | copy-start | bytes 786436
  181.2 178.0 %all-to-all-start = ((bf16[32,512,128]{2,1,0:T(8,128)(2,1)}), bf16[32,512,128]{2,1,0:T(8,128)(2,1)}, u32[]{:S(2)}, u32[]{:S(2)}) async-start(bf16[32,512,128]{2,1,0:T(8,128)(2,1)} %bitcast.202), calls=%async_computation.1 | async-start | bytes 8388608 | tf_op jit(solution)/shard_map/all_to_all | solution.py:141
  188.3 331.0 %all-reduce.2.cloned.1.call-start = ((), (), s32[]{:S(2)}) async-start(), calls=%async_computation.5 | async-start | bytes 4227072 | tf_op jit(solution)/shard_map/psum | solution.py:203
  191.0 14.7 %collective-permute-start.9 = (f32[4,136,128]{2,1,0:T(8,128)S(1)}, f32[4,136,128]{2,1,0:T(8,128)S(1)}, u32[]{:S(2)}, u32[]{:S(2)}) collective-permute-start(f32[4,136,128]{2,1,0:T(8,128)S(1)} %pad_maximum_fusion.11), channel_id=1, source_target_pairs={{16,0},{24,8},{32,16},{40,24},{48,32},{56,40},{64,48},{72,56},{80,... | collective-permute-start | bytes 835592 | tf_op jit(solution)/shard_map/ppermute | solution.py:12
  205.7 83.7 %copy-start.17 = (bf16[512,512]{0,1:T(8,128)(2,1)S(1)}, bf16[512,512]{0,1:T(8,128)(2,1)}, u32[]{:S(2)}) copy-start(bf16[512,512]{0,1:T(8,128)(2,1)} %copy-done.16) | copy-start | bytes 1572868
  205.8 83.7 %copy-start.20 = (pred[512,512]{1,0:T(8,128)(4,1)S(1)}, pred[512,512]{1,0:T(8,128)(4,1)}, u32[]{:S(2)}) copy-start(pred[512,512]{1,0:T(8,128)(4,1)} %copy-done.18) | copy-start | bytes 786436
  205.8 82.3 %collective-permute-start.10 = (f32[4,136,128]{2,1,0:T(8,128)S(1)}, f32[4,136,128]{2,1,0:T(8,128)S(1)}, u32[]{:S(2)}, u32[]{:S(2)}) collective-permute-start(f32[4,136,128]{2,1,0:T(8,128)S(1)} %pad_maximum_fusion.12), channel_id=1, source_target_pairs={{32,0},{40,8},{48,16},{56,24},{64,32},{72,40},{80,48},{88,56},{96,... | collective-permute-start | bytes 835592 | tf_op jit(solution)/shard_map/ppermute | solution.py:12
  288.1 12.6 %collective-permute-start.11 = (f32[4,136,128]{2,1,0:T(8,128)S(1)}, f32[4,136,128]{2,1,0:T(8,128)S(1)}, u32[]{:S(2)}, u32[]{:S(2)}) collective-permute-start(f32[4,136,128]{2,1,0:T(8,128)S(1)} %pad_maximum_fusion.13), channel_id=1, source_target_pairs={{64,0},{72,8},{80,16},{88,24},{96,32},{104,40},{112,48},{120,56},{... | collective-permute-start | bytes 835592 | tf_op jit(solution)/shard_map/ppermute | solution.py:12
  289.4 12.9 %copy-start.10 = (bf16[512,512]{0,1:T(8,128)(2,1)S(1)}, bf16[512,512]{0,1:T(8,128)(2,1)}, u32[]{:S(2)}) copy-start(bf16[512,512]{0,1:T(8,128)(2,1)} %copy-done.9) | copy-start | bytes 1572868
  300.8 19.0 %collective-permute-start.12 = (f32[4,136,128]{2,1,0:T(8,128)S(1)}, f32[4,136,128]{2,1,0:T(8,128)S(1)}, u32[]{:S(2)}, u32[]{:S(2)}) collective-permute-start(f32[4,136,128]{2,1,0:T(8,128)S(1)} %pad_maximum_fusion.14), channel_id=1, source_target_pairs={{128,0},{136,8},{144,16},{152,24},{160,32},{168,40},{176,48},{184,... | collective-permute-start | bytes 835592 | tf_op jit(solution)/shard_map/ppermute | solution.py:12
  319.8 1.2 copy-start.3
  319.8 1.4 copy-start.6
  319.8 1.4 copy-start.14
  326.3 3.7 copy-start.15
  326.3 6.2 %collective-permute-start.13 = (f32[3,3,512]{2,1,0:T(4,128)S(1)}, f32[3,3,512]{2,1,0:T(4,128)S(1)}, u32[]{:S(2)}, u32[]{:S(2)}) collective-permute-start(f32[3,3,512]{2,1,0:T(4,128)S(1)} %copy.75), channel_id=1, source_target_pairs={{8,0},{16,8},{24,16},{32,24},{40,32},{48,40},{56,48},{64,56},{72,6... | collective-permute-start | bytes 55304 | tf_op jit(solution)/shard_map/ppermute | solution.py:12
  333.8 2.3 copy-start.1
  344.6 11.5 %copy-start.4 = (bf16[3,512,512]{1,2,0:T(8,128)(2,1)S(1)}, bf16[3,512,512]{1,2,0:T(8,128)(2,1)}, u32[]{:S(2)}) copy-start(bf16[3,512,512]{1,2,0:T(8,128)(2,1)} %get-tuple-element.46) | copy-start | bytes 4718596
Sparse Core Ops, SparseCore 0:
  9.8 36.5 all-gather.2
  48.9 103.5 all-gather.4
  166.8 34.5 reduce-scatter.1
  356.2 163.0 all-reduce.1

commit v3 on v2

--- a/solution.py
+++ b/solution.py
@@ -131,6 +131,16 @@
     weight_terms = lax.dot_general(
         normed, cotangent, contract_first, preferred_element_type=jnp.float32
     )
+    grad_heads = split_heads(grad_normed).astype(jnp.float32)
+    gain_terms = jnp.sum(grad_heads * unit_norm, axis=1).reshape(feat_width)
+    grad_unit = grad_heads * gain_heads
+    grad_attended = inverse * (
+        grad_unit - unit_norm * jnp.mean(grad_unit * unit_norm, axis=-1, keepdims=True)
+    )
+    back_state = jnp.einsum(
+        "hti,htj->hij", query_heads * head_decay, grad_attended, precision=HIGHEST
+    )
+    later_state = entering(decay_total, back_state, "seq", True)
     seq_count = lax.axis_size("seq")
     col_block = weight_terms.shape[1] // seq_count
     weight_parts = (
@@ -138,18 +148,9 @@
         .reshape(feat_width, seq_count, col_block)
         .transpose(1, 0, 2)
     )
+    weight_parts, later_state = lax.optimization_barrier((weight_parts, later_state))
     weight_parts = lax.all_to_all(weight_parts, "seq", 0, 0, tiled=True)
     grad_weight = jnp.sum(weight_parts.astype(jnp.float32), axis=0)
-    grad_heads = split_heads(grad_normed).astype(jnp.float32)
-    gain_terms = jnp.sum(grad_heads * unit_norm, axis=1).reshape(feat_width)
-    grad_unit = grad_heads * gain_heads
-    grad_attended = inverse * (
-        grad_unit - unit_norm * jnp.mean(grad_unit * unit_norm, axis=-1, keepdims=True)
-    )
-    back_state = jnp.einsum(
-        "hti,htj->hij", query_heads * head_decay, grad_attended, precision=HIGHEST
-    )
-    later_state = entering(decay_total, back_state, "seq", True)
     grad_scores = decay_mask * jnp.einsum(
         "htj,hsj->hts", grad_attended, value_heads, precision=HIGHEST
     )

time: 540 us -> 523 us (0.969)
  waiting for transfers between devices: 331 us -> 303 us
  starting transfers between devices: 78.9 us -> 92 us
    ppermute x14, waiting for transfers between devices: 145 us -> 81.4 us  [shifted(): return lax.ppermute(x, axis, pairs)]
    all_to_all x1, waiting for transfers between devices: 0.01 us -> 21.6 us  [on_device(): weight_parts = lax.all_to_all(weight_parts, 'seq', 0, 0, tiled=True)]
    psum x1, waiting for transfers between devices: 157 us -> 171 us  [on_device(): summed = lax.psum(packed.astype(jnp.bfloat16), 'seq').astype(jnp.float32)]
    all_to_all x1, starting transfers between devices: 7.1 us -> 20.6 us  [on_device(): weight_parts = lax.all_to_all(weight_parts, 'seq', 0, 0, tiled=True)]
  transfers between devices with their start and end apart: 19 -> 19, of which waited for: 14 -> 17; matrix products, arithmetic and copies ran while one was open for 17% -> 17% of each run, Pallas kernels for 0% -> 0%
where the time goes in v3:
time: 523 us; the launch traced here: 516 us
  waiting for transfers between devices  303 us (58%)
  starting transfers between devices  92 us (18%)
  matrix products  47.2 us (9%)
  local copies, waits for them, and re-layouts  34.4 us (7%)
  other arithmetic  23.8 us (5%)
  between operations  15 us (3%)
    psum x1, waiting for transfers between devices, on_device(): summed = lax.psum(packed.astype(jnp.bfloat16), 'seq').astype(jnp.float32)  171 us
    ppermute x14, waiting for transfers between devices, shifted(): return lax.ppermute(x, axis, pairs)  81.4 us
    ppermute x14, starting transfers between devices, shifted(): return lax.ppermute(x, axis, pairs)  71.1 us
    all_gather x1, waiting for transfers between devices, on_device(): lax.all_gather(out_weight, 'seq', axis=1, tiled=True)  28.4 us
    all_to_all x1, waiting for transfers between devices, on_device(): weight_parts = lax.all_to_all(weight_parts, 'seq', 0, 0, tiled=True)  21.6 us
    all_to_all x1, starting transfers between devices, on_device(): weight_parts = lax.all_to_all(weight_parts, 'seq', 0, 0, tiled=True)  20.6 us
    concatenate x1, local copies, waits for them, and re-layouts, on_device(): jnp.concatenate([table_terms.reshape(table_rows, feat_width), tap_terms.r...  11.5 us
  transfers between devices with their start and end apart: 19, of which 17 were waited for; matrix products, arithmetic and copies ran while one was open for 17% of the time, Pallas kernels for 0%

profile of v3, /device:TPU:2, one launch (start us, length us, event | category | flops | bytes accessed | tf_op | source)
XLA Modules:
  0.0 515.8 jit_solution(1227974130972141265)
XLA Ops:
  8.0 1.3 copy.58
  9.2 1.3 copy.59
  10.5 1.3 copy.60
  11.9 3.5 collective-permute-start
  15.5 1.2 reduce-window.6
  17.5 2.3 fusion.56
  19.8 4.0 collective-permute-done
  24.6 3.7 multiply_add_fusion
  28.5 1.1 fusion.62
  30.4 1.3 fusion.79
  31.8 4.4 collective-permute-start.1
  36.2 5.0 collective-permute-done.1
  41.3 4.4 collective-permute-start.2
  45.7 4.3 collective-permute-done.2
  50.0 6.0 %collective-permute-start.3 = (f32[4,136,128]{2,1,0:T(8,128)S(1)}, f32[4,136,128]{2,1,0:T(8,128)S(1)}, u32[]{:S(2)}, u32[]{:S(2)}) collective-permute-start(f32[4,136,128]{2,1,0:T(8,128)S(1)} %pad_maximum_fusion.7), channel_id=1, source_target_pairs={{0,16},{8,24},{16,32},{24,40},{32,48},{40,56},{48,64},{56,72},{64,... | collective-permute-start | bytes 835592 | tf_op jit(solution)/shard_map/ppermute | solution.py:12
  56.0 4.0 collective-permute-done.3
  60.1 12.7 %collective-permute-start.4 = (f32[4,136,128]{2,1,0:T(8,128)S(1)}, f32[4,136,128]{2,1,0:T(8,128)S(1)}, u32[]{:S(2)}, u32[]{:S(2)}) collective-permute-start(f32[4,136,128]{2,1,0:T(8,128)S(1)} %pad_maximum_fusion.8), channel_id=1, source_target_pairs={{0,32},{8,40},{16,48},{24,56},{32,64},{40,72},{48,80},{56,88},{64,... | collective-permute-start | bytes 835592 | tf_op jit(solution)/shard_map/ppermute | solution.py:12
  72.9 4.7 collective-permute-done.4
  77.7 6.3 %collective-permute-start.5 = (f32[4,136,128]{2,1,0:T(8,128)S(1)}, f32[4,136,128]{2,1,0:T(8,128)S(1)}, u32[]{:S(2)}, u32[]{:S(2)}) collective-permute-start(f32[4,136,128]{2,1,0:T(8,128)S(1)} %pad_maximum_fusion.9), channel_id=1, source_target_pairs={{0,64},{8,72},{16,80},{24,88},{32,96},{40,104},{48,112},{56,120},{... | collective-permute-start | bytes 835592 | tf_op jit(solution)/shard_map/ppermute | solution.py:12
  84.1 4.3 collective-permute-done.5
  88.5 24.3 %collective-permute-start.6 = (f32[4,136,128]{2,1,0:T(8,128)S(1)}, f32[4,136,128]{2,1,0:T(8,128)S(1)}, u32[]{:S(2)}, u32[]{:S(2)}) collective-permute-start(f32[4,136,128]{2,1,0:T(8,128)S(1)} %pad_maximum_fusion.10), channel_id=1, source_target_pairs={{0,128},{8,136},{16,144},{24,152},{32,160},{40,168},{48,176},{56,1... | collective-permute-start | bytes 835592 | tf_op jit(solution)/shard_map/ppermute | solution.py:12
  113.6 4.9 collective-permute-done.6
  119.2 4.7 multiply_reduce_fusion.4
  124.0 28.4 %all-gather.5.cloned.1.call-done = bf16[512,4096]{1,0:T(8,128)(2,1)} async-done(((bf16[512,128]{1,0:T(8,128)(2,1)}), bf16[512,4096]{1,0:T(8,128)(2,1)}) %all-gather.5.cloned.1.call-update) | async-done | bytes 4194320 | tf_op jit(solution)/shard_map/all_gather | solution.py:125
  152.4 5.8 %convolution_convert_fusion.2 = bf16[512,512]{0,1:T(8,128)(2,1)S(1)} fusion(bf16[512,4096]{1,0:T(8,128)(2,1)} %all-gather.3.cloned.1.call-done, bf16[512,4096]{1,0:T(8,128)(2,1)} %all-gather.5.cloned.1.call-done), kind=kOutput, calls=%fused_computation.68 | convolution fusion | flops 2147745792 | bytes 8912896 | tf_op jit(solution)/shard_map/dot_general | solution.py:123
  158.7 1.4 fusion.76
  160.2 1.6 collective-permute-start.7
  161.8 8.8 %collective-permute-done.7 = f32[4,136,128]{2,1,0:T(8,128)S(1)} collective-permute-done((f32[4,136,128]{2,1,0:T(8,128)S(1)}, f32[4,136,128]{2,1,0:T(8,128)S(1)}, u32[]{:S(2)}, u32[]{:S(2)}) %collective-permute-start.7) | collective-permute-done | bytes 278560 | tf_op jit(solution)/shard_map/ppermute | solution.py:12
  170.6 1.3 collective-permute-start.8
  171.9 7.1 %collective-permute-done.8 = f32[4,136,128]{2,1,0:T(8,128)S(1)} collective-permute-done((f32[4,136,128]{2,1,0:T(8,128)S(1)}, f32[4,136,128]{2,1,0:T(8,128)S(1)}, u32[]{:S(2)}, u32[]{:S(2)}) %collective-permute-start.8) | collective-permute-done | bytes 278560 | tf_op jit(solution)/shard_map/ppermute | solution.py:12
  179.1 1.3 collective-permute-start.9
  180.6 8.4 %collective-permute-done.9 = f32[4,136,128]{2,1,0:T(8,128)S(1)} collective-permute-done((f32[4,136,128]{2,1,0:T(8,128)S(1)}, f32[4,136,128]{2,1,0:T(8,128)S(1)}, u32[]{:S(2)}, u32[]{:S(2)}) %collective-permute-start.9) | collective-permute-done | bytes 278560 | tf_op jit(solution)/shard_map/ppermute | solution.py:12
  189.8 1.3 collective-permute-start.10
  191.1 4.4 convolution_convert_fusion
  195.5 7.4 %collective-permute-done.10 = f32[4,136,128]{2,1,0:T(8,128)S(1)} collective-permute-done((f32[4,136,128]{2,1,0:T(8,128)}, f32[4,136,128]{2,1,0:T(8,128)S(1)}, u32[]{:S(2)}, u32[]{:S(2)}) %collective-permute-start.10) | collective-permute-done | bytes 278560 | tf_op jit(solution)/shard_map/ppermute | solution.py:12
  203.0 1.3 collective-permute-start.11
  204.3 14.5 %collective-permute-done.11 = f32[4,136,128]{2,1,0:T(8,128)S(1)} collective-permute-done((f32[4,136,128]{2,1,0:T(8,128)S(1)}, f32[4,136,128]{2,1,0:T(8,128)S(1)}, u32[]{:S(2)}, u32[]{:S(2)}) %collective-permute-start.11) | collective-permute-done | bytes 278560 | tf_op jit(solution)/shard_map/ppermute | solution.py:12
  218.9 1.3 collective-permute-start.12
  220.2 4.8 fusion.14
  225.0 3.1 copy.114
  228.1 3.2 collective-permute-done.12
  231.3 20.6 %all-to-all-start = ((bf16[32,512,128]{2,1,0:T(8,128)(2,1)}), bf16[32,512,128]{2,1,0:T(8,128)(2,1)}, u32[]{:S(2)}, u32[]{:S(2)}) async-start(bf16[32,512,128]{2,1,0:T(8,128)(2,1)} %bitcast.204), calls=%async_computation.1 | async-start | bytes 8388608 | tf_op jit(solution)/shard_map/all_to_all | solution.py:152
  252.2 2.1 fusion.118
  254.3 2.8 fusion.38
  257.1 3.5 fusion.35
  260.7 3.9 fusion.41
  265.6 1.6 fusion.47
  267.2 2.3 add_convert_fusion
  269.8 1.1 slice.308
  270.8 1.4 copy.76
  272.2 1.4 collective-permute-start.13
  273.7 2.0 convolution_bitcast_fusion.1
  276.7 1.5 pad_maximum_fusion
  279.0 1.3 copy.77
  280.3 1.6 pad_maximum_fusion.1
  282.6 8.4 %multiply_reduce_fusion.3 = (bf16[3,512]{1,0:T(4,128)(2,1)S(1)}, bf16[3,512]{1,0:T(4,128)(2,1)S(1)}, bf16[3,512]{1,0:T(4,128)(2,1)S(1)}, bf16[3,512]{1,0:T(4,128)(2,1)S(1)}, bf16[3,512,512]{1,2,0:T(8,128)(2,1)}) fusion(f32[3,515,512]{1,2,0:T(8,128)S(1)} %copy-done.1, f32[1,512,512]{1,2,0:T(8,128)S(1)} %bitcast.207, f32[1,512,512]{1,2,0:T(8,128)S(1)} %bitcast.200, ...), kind=kLoop, calls=%fused_computation.20 | loop fusion | flops 14149632 | bytes 26775552 | tf_op jit(solution)/shard_map/reduce_sum | solution.py:179
  291.2 11.5 %concatenate.50 = bf16[2061,512]{1,0:T(8,128)(2,1)} concatenate(bf16[2048,512]{1,0:T(8,128)(2,1)} %bitcast.208, bf16[12,512]{1,0:T(8,128)(2,1)S(1)} %reshape.167, f32[1,512]{1,0:T(1,128)S(1)} %bitcast.246), dimensions={0} | concatenate | bytes 4221952 | tf_op jit(solution)/shard_map/concatenate | solution.py:196
  302.8 1.0 copy.78
  303.8 1.0 copy.79
  305.8 21.6 %all-to-all-done = bf16[32,512,128]{2,1,0:T(8,128)(2,1)} async-done(((bf16[32,512,128]{2,1,0:T(8,128)(2,1)}), bf16[32,512,128]{2,1,0:T(8,128)(2,1)}, u32[]{:S(2)}, u32[]{:S(2)}) %all-to-all-start) | async-done | bytes 4194336 | tf_op jit(solution)/shard_map/all_to_all | solution.py:152
  327.5 3.5 convert_reduce_fusion
  331.0 171.2 %all-reduce.2.cloned.1.call-done = bf16[2061,512]{1,0:T(8,128)(2,1)} async-done(((bf16[2061,512]{1,0:T(8,128)(2,1)}), bf16[2061,512]{1,0:T(8,128)(2,1)}) %all-reduce.2.cloned.1.call-update) | async-done | bytes 2110480 | tf_op jit(solution)/shard_map/psum | solution.py:204
  503.5 4.2 slice.316
  507.7 1.3 slice.317
  (143 shorter events, 13.7 us)
Async XLA Ops:
  7.2 8.4 %copy-start.26 = (f32[4,512]{1,0:T(4,128)S(1)}, f32[4,512]{1,0:T(4,128)}, u32[]{:S(2)}) copy-start(f32[4,512]{1,0:T(4,128)} %param.16) | copy-start | bytes 24580
  7.2 10.2 %copy-start.27 = (s32[4,512]{1,0:T(4,128)S(1)}, s32[4,512]{1,0:T(4,128)}, u32[]{:S(2)}) copy-start(s32[4,512]{1,0:T(4,128)} %param.14) | copy-start | bytes 24580
  7.2 10.2 %copy-start.25 = (f32[3,4,512]{2,1,0:T(4,128)S(1)}, f32[3,4,512]{2,1,0:T(4,128)}, u32[]{:S(2)}) copy-start(f32[3,4,512]{2,1,0:T(4,128)} %param.13) | copy-start | bytes 73732
  7.2 116.8 %all-gather.3.cloned.1.call-start = ((), (), s32[]{:S(2)}) async-start(), calls=%async_computation.2 | async-start | bytes 4718592 | tf_op jit(solution)/shard_map/all_gather | solution.py:121
  7.9 144.4 %all-gather.5.cloned.1.call-start = ((), (), s32[]{:S(2)}) async-start(), calls=%async_computation.3 | async-start | bytes 4325376 | tf_op jit(solution)/shard_map/all_gather | solution.py:125
  11.9 11.8 %collective-permute-start = (bf16[3,3,512]{1,2,0:T(8,128)(2,1)S(1)}, bf16[3,3,512]{1,2,0:T(8,128)(2,1)S(1)}, u32[]{:S(2)}, u32[]{:S(2)}) collective-permute-start(bf16[3,3,512]{1,2,0:T(8,128)(2,1)S(1)} %pad_maximum_fusion.5), channel_id=1, source_target_pairs={{0,8},{8,16},{16,24},{24,32},{32,40},{40,48},{48,56},{56,64},{64,7... | collective-permute-start | bytes 27656 | tf_op jit(solution)/shard_map/ppermute | solution.py:12
  15.5 287.2 %reduce-scatter.2.cloned.1.call-start = ((), (), s32[]{:S(2)}) async-start(), calls=%async_computation.4 | async-start | bytes 4718592 | tf_op jit(solution)/shard_map/reduce_scatter | solution.py:118
  24.6 3.8 copy-start
  24.6 3.9 copy-start.28
  29.6 0.8 copy-start.20
  29.6 129.1 %copy-start.13 = (bf16[512,512]{0,1:T(8,128)(2,1)}, bf16[512,512]{0,1:T(8,128)(2,1)S(1)}, u32[]{:S(2)}) copy-start(bf16[512,512]{0,1:T(8,128)(2,1)S(1)} %get-tuple-element.48) | copy-start | bytes 1572868
  31.8 9.4 %collective-permute-start.1 = (f32[4,136,128]{2,1,0:T(8,128)S(1)}, f32[4,136,128]{2,1,0:T(8,128)S(1)}, u32[]{:S(2)}, u32[]{:S(2)}) collective-permute-start(f32[4,136,128]{2,1,0:T(8,128)S(1)} %pad_maximum_fusion.4), channel_id=1, source_target_pairs={{0,8},{8,16},{16,24},{24,32},{32,40},{40,48},{48,56},{56,64},{64,7... | collective-permute-start | bytes 835592 | tf_op jit(solution)/shard_map/ppermute | solution.py:12
  41.3 8.7 %collective-permute-start.2 = (f32[4,136,128]{2,1,0:T(8,128)S(1)}, f32[4,136,128]{2,1,0:T(8,128)S(1)}, u32[]{:S(2)}, u32[]{:S(2)}) collective-permute-start(f32[4,136,128]{2,1,0:T(8,128)S(1)} %collective-permute-done.1), channel_id=1, source_target_pairs={{0,8},{8,16},{16,24},{24,32},{32,40},{40,48},{48,56},{56,64},{64,7... | collective-permute-start | bytes 835592 | tf_op jit(solution)/shard_map/ppermute | solution.py:12
  50.0 10.1 %collective-permute-start.3 = (f32[4,136,128]{2,1,0:T(8,128)S(1)}, f32[4,136,128]{2,1,0:T(8,128)S(1)}, u32[]{:S(2)}, u32[]{:S(2)}) collective-permute-start(f32[4,136,128]{2,1,0:T(8,128)S(1)} %pad_maximum_fusion.7), channel_id=1, source_target_pairs={{0,16},{8,24},{16,32},{24,40},{32,48},{40,56},{48,64},{56,72},{64,... | collective-permute-start | bytes 835592 | tf_op jit(solution)/shard_map/ppermute | solution.py:12
  60.1 17.5 %collective-permute-start.4 = (f32[4,136,128]{2,1,0:T(8,128)S(1)}, f32[4,136,128]{2,1,0:T(8,128)S(1)}, u32[]{:S(2)}, u32[]{:S(2)}) collective-permute-start(f32[4,136,128]{2,1,0:T(8,128)S(1)} %pad_maximum_fusion.8), channel_id=1, source_target_pairs={{0,32},{8,40},{16,48},{24,56},{32,64},{40,72},{48,80},{56,88},{64,... | collective-permute-start | bytes 835592 | tf_op jit(solution)/shard_map/ppermute | solution.py:12
  77.7 10.7 %collective-permute-start.5 = (f32[4,136,128]{2,1,0:T(8,128)S(1)}, f32[4,136,128]{2,1,0:T(8,128)S(1)}, u32[]{:S(2)}, u32[]{:S(2)}) collective-permute-start(f32[4,136,128]{2,1,0:T(8,128)S(1)} %pad_maximum_fusion.9), channel_id=1, source_target_pairs={{0,64},{8,72},{16,80},{24,88},{32,96},{40,104},{48,112},{56,120},{... | collective-permute-start | bytes 835592 | tf_op jit(solution)/shard_map/ppermute | solution.py:12
  84.1 35.1 %copy-start.22 = (pred[512,512]{1,0:T(8,128)(4,1)}, pred[512,512]{1,0:T(8,128)(4,1)S(1)}, u32[]{:S(2)}) copy-start(pred[512,512]{1,0:T(8,128)(4,1)S(1)} %iota_compare_fusion.4) | copy-start | bytes 786436
  88.5 30.0 %collective-permute-start.6 = (f32[4,136,128]{2,1,0:T(8,128)S(1)}, f32[4,136,128]{2,1,0:T(8,128)S(1)}, u32[]{:S(2)}, u32[]{:S(2)}) collective-permute-start(f32[4,136,128]{2,1,0:T(8,128)S(1)} %pad_maximum_fusion.10), channel_id=1, source_target_pairs={{0,128},{8,136},{16,144},{24,152},{32,160},{40,168},{48,176},{56,1... | collective-permute-start | bytes 835592 | tf_op jit(solution)/shard_map/ppermute | solution.py:12
  113.6 10.4 %copy-start.7 = (f32[4,512,512]{2,1,0:T(8,128)}, f32[4,512,512]{2,1,0:T(8,128)S(1)}, u32[]{:S(2)}) copy-start(f32[4,512,512]{2,1,0:T(8,128)S(1)} %fusion.94) | copy-start | bytes 12582916
  118.5 0.7 copy-start.17
  119.2 4.7 copy-start.9
  123.9 136.7 %copy-start.2 = (f32[4,512,128]{1,2,0:T(8,128)}, f32[4,512,128]{1,2,0:T(8,128)S(1)}, u32[]{:S(2)}) copy-start(f32[4,512,128]{1,2,0:T(8,128)S(1)} %get-tuple-element.47) | copy-start | bytes 3145732
  124.0 34.3 %copy-start.24 = (f32[512]{0:T(512)S(1)}, f32[512]{0:T(512)}, u32[]{:S(2)}) copy-start(f32[512]{0:T(512)} %param.17) | copy-start | bytes 6148
  158.2 102.5 %copy-start.5 = (bf16[512,512]{0,1:T(8,128)(2,1)}, bf16[512,512]{0,1:T(8,128)(2,1)S(1)}, u32[]{:S(2)}) copy-start(bf16[512,512]{0,1:T(8,128)(2,1)S(1)} %convolution_convert_fusion.2) | copy-start | bytes 1572868
  158.2 22.2 %copy-start.10 = (f32[4,512,128]{1,2,0:T(8,128)S(1)}, f32[4,512,128]{1,2,0:T(8,128)}, u32[]{:S(2)}) copy-start(f32[4,512,128]{1,2,0:T(8,128)} %copy-done.9) | copy-start | bytes 3145732
  158.2 22.2 %copy-start.16 = (f32[4,512,128]{1,2,0:T(8,128)S(1)}, f32[4,512,128]{1,2,0:T(8,128)}, u32[]{:S(2)}) copy-start(f32[4,512,128]{1,2,0:T(8,128)} %get-tuple-element.67) | copy-start | bytes 3145732
  160.2 30.9 %copy-start.11 = (bf16[512,4096]{1,0:T(8,128)(2,1)S(1)}, bf16[512,4096]{1,0:T(8,128)(2,1)}, u32[]{:S(2)}) copy-start(bf16[512,4096]{1,0:T(8,128)(2,1)} %all-gather.5.cloned.1.call-done) | copy-start | bytes 12582916
  160.2 10.4 %collective-permute-start.7 = (f32[4,136,128]{2,1,0:T(8,128)S(1)}, f32[4,136,128]{2,1,0:T(8,128)S(1)}, u32[]{:S(2)}, u32[]{:S(2)}) collective-permute-start(f32[4,136,128]{2,1,0:T(8,128)S(1)} %pad_maximum_fusion.3), channel_id=1, source_target_pairs={{8,0},{16,8},{24,16},{32,24},{40,32},{48,40},{56,48},{64,56},{72,6... | collective-permute-start | bytes 835592 | tf_op jit(solution)/shard_map/ppermute | solution.py:12
  170.6 8.4 %collective-permute-start.8 = (f32[4,136,128]{2,1,0:T(8,128)S(1)}, f32[4,136,128]{2,1,0:T(8,128)S(1)}, u32[]{:S(2)}, u32[]{:S(2)}) collective-permute-start(f32[4,136,128]{2,1,0:T(8,128)S(1)} %collective-permute-done.7), channel_id=1, source_target_pairs={{8,0},{16,8},{24,16},{32,24},{40,32},{48,40},{56,48},{64,56},{72,6... | collective-permute-start | bytes 835592 | tf_op jit(solution)/shard_map/ppermute | solution.py:12
  179.1 9.9 %collective-permute-start.9 = (f32[4,136,128]{2,1,0:T(8,128)S(1)}, f32[4,136,128]{2,1,0:T(8,128)S(1)}, u32[]{:S(2)}, u32[]{:S(2)}) collective-permute-start(f32[4,136,128]{2,1,0:T(8,128)S(1)} %pad_maximum_fusion.11), channel_id=1, source_target_pairs={{16,0},{24,8},{32,16},{40,24},{48,32},{56,40},{64,48},{72,56},{80,... | collective-permute-start | bytes 835592 | tf_op jit(solution)/shard_map/ppermute | solution.py:12
  180.6 10.5 %copy-start.15 = (bf16[512,4,128]{0,2,1:T(8,128)(2,1)}, bf16[512,4,128]{0,2,1:T(8,128)(2,1)S(1)}, u32[]{:S(2)}) copy-start(bf16[512,4,128]{0,2,1:T(8,128)(2,1)S(1)} %fusion.73) | copy-start | bytes 1572868
  189.8 13.2 %collective-permute-start.10 = (f32[4,136,128]{2,1,0:T(8,128)}, f32[4,136,128]{2,1,0:T(8,128)S(1)}, u32[]{:S(2)}, u32[]{:S(2)}) collective-permute-start(f32[4,136,128]{2,1,0:T(8,128)} %pad_maximum_fusion.12), channel_id=1, source_target_pairs={{32,0},{40,8},{48,16},{56,24},{64,32},{72,40},{80,48},{88,56},{96,... | collective-permute-start | bytes 835592 | tf_op jit(solution)/shard_map/ppermute | solution.py:12
  203.0 15.8 %collective-permute-start.11 = (f32[4,136,128]{2,1,0:T(8,128)S(1)}, f32[4,136,128]{2,1,0:T(8,128)S(1)}, u32[]{:S(2)}, u32[]{:S(2)}) collective-permute-start(f32[4,136,128]{2,1,0:T(8,128)S(1)} %pad_maximum_fusion.13), channel_id=1, source_target_pairs={{64,0},{72,8},{80,16},{88,24},{96,32},{104,40},{112,48},{120,56},{... | collective-permute-start | bytes 835592 | tf_op jit(solution)/shard_map/ppermute | solution.py:12
  218.9 12.3 %collective-permute-start.12 = (f32[4,136,128]{2,1,0:T(8,128)S(1)}, f32[4,136,128]{2,1,0:T(8,128)S(1)}, u32[]{:S(2)}, u32[]{:S(2)}) collective-permute-start(f32[4,136,128]{2,1,0:T(8,128)S(1)} %pad_maximum_fusion.14), channel_id=1, source_target_pairs={{128,0},{136,8},{144,16},{152,24},{160,32},{168,40},{176,48},{184,... | collective-permute-start | bytes 835592 | tf_op jit(solution)/shard_map/ppermute | solution.py:12
  231.3 33.4 %copy-start.12 = (f32[4,128,128]{2,1,0:T(8,128)}, f32[4,128,128]{2,1,0:T(8,128)S(1)}, u32[]{:S(2)}) copy-start(f32[4,128,128]{2,1,0:T(8,128)S(1)} %fusion.98) | copy-start | bytes 786436
  231.3 96.2 %all-to-all-start = ((bf16[32,512,128]{2,1,0:T(8,128)(2,1)}), bf16[32,512,128]{2,1,0:T(8,128)(2,1)}, u32[]{:S(2)}, u32[]{:S(2)}) async-start(bf16[32,512,128]{2,1,0:T(8,128)(2,1)} %bitcast.204), calls=%async_computation.1 | async-start | bytes 8388608 | tf_op jit(solution)/shard_map/all_to_all | solution.py:152
  251.9 2.3 copy-start.23
  251.9 250.3 %all-reduce.2.cloned.1.call-start = ((), (), s32[]{:S(2)}) async-start(), calls=%async_computation.5 | async-start | bytes 4227072 | tf_op jit(solution)/shard_map/psum | solution.py:204
  252.1 2.1 copy-start.14
  254.2 2.9 copy-start.21
  257.1 3.6 copy-start.8
  264.6 2.5 copy-start.3
  264.6 2.5 copy-start.6
  264.6 2.5 copy-start.18
  272.2 3.4 copy-start.19
  272.2 6.8 %collective-permute-start.13 = (f32[3,3,512]{2,1,0:T(4,128)S(1)}, f32[3,3,512]{2,1,0:T(4,128)S(1)}, u32[]{:S(2)}, u32[]{:S(2)}) collective-permute-start(f32[3,3,512]{2,1,0:T(4,128)S(1)} %copy.76), channel_id=1, source_target_pairs={{8,0},{16,8},{24,16},{32,24},{40,32},{48,40},{56,48},{64,56},{72,6... | collective-permute-start | bytes 55304 | tf_op jit(solution)/shard_map/ppermute | solution.py:12
  280.3 2.3 copy-start.1
  291.2 11.5 %copy-start.4 = (bf16[3,512,512]{1,2,0:T(8,128)(2,1)S(1)}, bf16[3,512,512]{1,2,0:T(8,128)(2,1)}, u32[]{:S(2)}) copy-start(bf16[3,512,512]{1,2,0:T(8,128)(2,1)} %get-tuple-element.50) | copy-start | bytes 4718596
Sparse Core Ops, SparseCore 0:
  9.8 36.5 all-gather.2
  48.9 103.4 all-gather.4
  195.6 45.2 reduce-scatter.1
  302.8 199.3 all-reduce.1

commit v4 on v3

--- a/solution.py
+++ b/solution.py
@@ -149,8 +149,6 @@
         .transpose(1, 0, 2)
     )
     weight_parts, later_state = lax.optimization_barrier((weight_parts, later_state))
-    weight_parts = lax.all_to_all(weight_parts, "seq", 0, 0, tiled=True)
-    grad_weight = jnp.sum(weight_parts.astype(jnp.float32), axis=0)
     grad_scores = decay_mask * jnp.einsum(
         "htj,hsj->hts", grad_attended, value_heads, precision=HIGHEST
     )
@@ -195,13 +193,15 @@
     tap_rows = 3 * kernel
     packed = jnp.concatenate(
         [
-            table_terms.reshape(table_rows, feat_width),
-            tap_terms.reshape(tap_rows, feat_width),
-            gain_terms.reshape(1, feat_width),
+            table_terms.astype(jnp.bfloat16).reshape(table_rows, feat_width),
+            tap_terms.astype(jnp.bfloat16).reshape(tap_rows, feat_width),
+            gain_terms.astype(jnp.bfloat16).reshape(1, feat_width),
         ]
     )
-    packed, layer_out = lax.optimization_barrier((packed, layer_out))
-    summed = lax.psum(packed.astype(jnp.bfloat16), "seq").astype(jnp.float32)
+    packed, layer_out, weight_parts = lax.optimization_barrier((packed, layer_out, weight_parts))
+    summed = lax.psum(packed, "seq").astype(jnp.float32)
+    weight_parts = lax.all_to_all(weight_parts, "seq", 0, 0, tiled=True)
+    grad_weight = jnp.sum(weight_parts.astype(jnp.float32), axis=0)
     grad_tables = summed[:table_rows].reshape(2, buckets, feat_width)
     grad_taps = summed[table_rows : table_rows + tap_rows].reshape(3, kernel, feat_width)
     grad_gain = summed[table_rows + tap_rows]

time: 523 us -> 497 us (0.950)
  waiting for transfers between devices: 303 us -> 283 us
    all_to_all x1, waiting for transfers between devices: 21.6 us -> 0.01 us  [on_device(): weight_parts = lax.all_to_all(weight_parts, 'seq', 0, 0, tiled=True)]
    psum x1, waiting for transfers between devices: 171 us -> 184 us  [on_device(): summed = lax.psum(packed, 'seq').astype(jnp.float32)]
    ppermute x14, waiting for transfers between devices: 81.4 us -> 68.3 us  [shifted(): return lax.ppermute(x, axis, pairs)]
  transfers between devices with their start and end apart: 19 -> 19, of which waited for: 17 -> 16; matrix products, arithmetic and copies ran while one was open for 17% -> 19% of each run, Pallas kernels for 0% -> 0%
where the time goes in v4:
time: 497 us; the launch traced here: 490 us
  waiting for transfers between devices  283 us (57%)
  starting transfers between devices  87.9 us (18%)
  matrix products  44.2 us (9%)
  local copies, waits for them, and re-layouts  34.9 us (7%)
  other arithmetic  25.7 us (5%)
  between operations  14.9 us (3%)
    psum x1, waiting for transfers between devices, on_device(): summed = lax.psum(packed, 'seq').astype(jnp.float32)  184 us
    ppermute x14, starting transfers between devices, shifted(): return lax.ppermute(x, axis, pairs)  71.4 us
    ppermute x14, waiting for transfers between devices, shifted(): return lax.ppermute(x, axis, pairs)  68.3 us
    all_gather x1, waiting for transfers between devices, on_device(): lax.all_gather(out_weight, 'seq', axis=1, tiled=True)  28.5 us
    all_to_all x1, starting transfers between devices, on_device(): weight_parts = lax.all_to_all(weight_parts, 'seq', 0, 0, tiled=True)  16.4 us
    concatenate x1, local copies, waits for them, and re-layouts, on_device(): jnp.concatenate([table_terms.astype(jnp.bfloat16).reshape(table_rows, fea...  11.3 us
  transfers between devices with their start and end apart: 19, of which 16 were waited for; matrix products, arithmetic and copies ran while one was open for 19% of the time, Pallas kernels for 0%

profile of v4, /device:TPU:2, one launch (start us, length us, event | category | flops | bytes accessed | tf_op | source)
XLA Modules:
  0.0 490.2 jit_solution(6953520611271623817)
XLA Ops:
  8.0 1.3 copy.79
  9.2 1.3 copy.80
  10.5 1.3 copy.81
  11.9 3.5 collective-permute-start
  15.6 1.2 reduce-window.6
  17.5 2.3 fusion.58
  19.8 4.0 collective-permute-done
  24.6 3.7 multiply_add_fusion
  28.5 1.1 fusion.64
  30.4 1.3 fusion.81
  31.8 4.4 collective-permute-start.1
  36.2 5.0 %collective-permute-done.1 = f32[4,136,128]{2,1,0:T(8,128)S(1)} collective-permute-done((f32[4,136,128]{2,1,0:T(8,128)S(1)}, f32[4,136,128]{2,1,0:T(8,128)S(1)}, u32[]{:S(2)}, u32[]{:S(2)}) %collective-permute-start.1) | collective-permute-done | bytes 278560 | tf_op jit(solution)/shard_map/ppermute | solution.py:12
  41.3 4.4 collective-permute-start.2
  45.7 4.3 collective-permute-done.2
  50.0 6.0 %collective-permute-start.3 = (f32[4,136,128]{2,1,0:T(8,128)S(1)}, f32[4,136,128]{2,1,0:T(8,128)S(1)}, u32[]{:S(2)}, u32[]{:S(2)}) collective-permute-start(f32[4,136,128]{2,1,0:T(8,128)S(1)} %pad_maximum_fusion.7), channel_id=1, source_target_pairs={{0,16},{8,24},{16,32},{24,40},{32,48},{40,56},{48,64},{56,72},{64,... | collective-permute-start | bytes 835592 | tf_op jit(solution)/shard_map/ppermute | solution.py:12
  56.0 4.0 collective-permute-done.3
  60.1 12.8 %collective-permute-start.4 = (f32[4,136,128]{2,1,0:T(8,128)S(1)}, f32[4,136,128]{2,1,0:T(8,128)S(1)}, u32[]{:S(2)}, u32[]{:S(2)}) collective-permute-start(f32[4,136,128]{2,1,0:T(8,128)S(1)} %pad_maximum_fusion.8), channel_id=1, source_target_pairs={{0,32},{8,40},{16,48},{24,56},{32,64},{40,72},{48,80},{56,88},{64,... | collective-permute-start | bytes 835592 | tf_op jit(solution)/shard_map/ppermute | solution.py:12
  72.9 4.7 collective-permute-done.4
  77.7 6.3 %collective-permute-start.5 = (f32[4,136,128]{2,1,0:T(8,128)S(1)}, f32[4,136,128]{2,1,0:T(8,128)S(1)}, u32[]{:S(2)}, u32[]{:S(2)}) collective-permute-start(f32[4,136,128]{2,1,0:T(8,128)S(1)} %pad_maximum_fusion.9), channel_id=1, source_target_pairs={{0,64},{8,72},{16,80},{24,88},{32,96},{40,104},{48,112},{56,120},{... | collective-permute-start | bytes 835592 | tf_op jit(solution)/shard_map/ppermute | solution.py:12
  84.2 4.3 collective-permute-done.5
  88.5 24.3 %collective-permute-start.6 = (f32[4,136,128]{2,1,0:T(8,128)S(1)}, f32[4,136,128]{2,1,0:T(8,128)S(1)}, u32[]{:S(2)}, u32[]{:S(2)}) collective-permute-start(f32[4,136,128]{2,1,0:T(8,128)S(1)} %pad_maximum_fusion.10), channel_id=1, source_target_pairs={{0,128},{8,136},{16,144},{24,152},{32,160},{40,168},{48,176},{56,1... | collective-permute-start | bytes 835592 | tf_op jit(solution)/shard_map/ppermute | solution.py:12
  113.6 4.9 %collective-permute-done.6 = f32[4,136,128]{2,1,0:T(8,128)S(1)} collective-permute-done((f32[4,136,128]{2,1,0:T(8,128)S(1)}, f32[4,136,128]{2,1,0:T(8,128)S(1)}, u32[]{:S(2)}, u32[]{:S(2)}) %collective-permute-start.6) | collective-permute-done | bytes 278560 | tf_op jit(solution)/shard_map/ppermute | solution.py:12
  119.2 3.6 multiply_reduce_fusion.4
  122.8 1.1 fusion.75
  123.9 28.5 %all-gather.5.cloned.1.call-done = bf16[512,4096]{1,0:T(8,128)(2,1)} async-done(((bf16[512,128]{1,0:T(8,128)(2,1)}), bf16[512,4096]{1,0:T(8,128)(2,1)}) %all-gather.5.cloned.1.call-update) | async-done | bytes 4194320 | tf_op jit(solution)/shard_map/all_gather | solution.py:125
  152.5 6.0 %convolution_convert_fusion.4 = bf16[512,512]{0,1:T(8,128)(2,1)S(1)} fusion(bf16[512,4096]{1,0:T(8,128)(2,1)} %all-gather.3.cloned.1.call-done, bf16[512,4096]{1,0:T(8,128)(2,1)} %all-gather.5.cloned.1.call-done), kind=kOutput, calls=%fused_computation.70 | convolution fusion | flops 2147745792 | bytes 8912896 | tf_op jit(solution)/shard_map/dot_general | solution.py:123
  158.9 1.4 fusion.78
  160.4 1.3 collective-permute-start.7
  161.7 2.4 fusion.14
  164.1 3.1 copy.138
  167.2 4.2 collective-permute-done.7
  171.4 1.5 collective-permute-start.8
  172.8 4.5 convolution_convert_fusion
  177.3 2.6 collective-permute-done.8
  180.6 1.1 slice_add_fusion
  181.7 1.3 collective-permute-start.9
  183.0 5.8 %fusion.41 = f32[512,4,128]{0,2,1:T(8,128)S(1)} fusion(f32[4,512,512]{2,1,0:T(8,128)} %copy-done.7, f32[4,512]{1,0:T(4,128)S(1)} %bitcast.265, pred[512,512]{1,0:T(8,128)(4,1)} %copy-done.18, f32[4,512,128]{1,2,0:T(8,128)S(1)} %get-tuple-element.57, f32[4,512]{1,0:T(4,128)S(1)} %broadcast_multiply_fusion, f32[4,128]{1,0:T(4,128)S(1)} %bitcast.254, ...), kind=kOutput, calls=%fused_computation.56 | convolution fusion | flops 1616379904 | bytes 7104512 | tf_op jit(solution)/shard_map/hts,htj->hsj/dot_general | solution.py:161
  188.8 2.9 collective-permute-done.9
  191.8 1.4 collective-permute-start.10
  193.2 2.0 fusion.120
  195.2 6.3 %collective-permute-done.10 = f32[4,136,128]{2,1,0:T(8,128)S(1)} collective-permute-done((f32[4,136,128]{2,1,0:T(8,128)S(1)}, f32[4,136,128]{2,1,0:T(8,128)S(1)}, u32[]{:S(2)}, u32[]{:S(2)}) %collective-permute-start.10) | collective-permute-done | bytes 278560 | tf_op jit(solution)/shard_map/ppermute | solution.py:12
  201.6 1.3 collective-permute-start.11
  202.9 3.5 fusion.35
  206.4 10.0 %collective-permute-done.11 = f32[4,136,128]{2,1,0:T(8,128)S(1)} collective-permute-done((f32[4,136,128]{2,1,0:T(8,128)S(1)}, f32[4,136,128]{2,1,0:T(8,128)S(1)}, u32[]{:S(2)}, u32[]{:S(2)}) %collective-permute-start.11) | collective-permute-done | bytes 278560 | tf_op jit(solution)/shard_map/ppermute | solution.py:12
  216.5 1.5 collective-permute-start.12
  218.0 2.7 fusion.38
  220.8 10.7 %collective-permute-done.12 = f32[4,136,128]{2,1,0:T(8,128)S(1)} collective-permute-done((f32[4,136,128]{2,1,0:T(8,128)S(1)}, f32[4,136,128]{2,1,0:T(8,128)S(1)}, u32[]{:S(2)}, u32[]{:S(2)}) %collective-permute-start.12) | collective-permute-done | bytes 278560 | tf_op jit(solution)/shard_map/ppermute | solution.py:12
  232.9 2.2 add_convert_fusion
  236.5 1.4 copy.98
  237.9 1.4 collective-permute-start.13
  239.3 2.0 fusion.51
  242.3 1.5 pad_maximum_fusion.2
  244.3 1.2 copy.99
  245.5 1.6 pad_maximum_fusion
  247.9 8.4 %multiply_reduce_fusion.3 = (bf16[3,512]{1,0:T(4,128)(2,1)S(1)}, bf16[3,512]{1,0:T(4,128)(2,1)S(1)}, bf16[3,512]{1,0:T(4,128)(2,1)S(1)}, bf16[3,512]{1,0:T(4,128)(2,1)S(1)}, bf16[3,512,512]{1,2,0:T(8,128)(2,1)}) fusion(f32[3,515,512]{1,2,0:T(8,128)S(1)} %copy-done.1, f32[1,512,512]{1,2,0:T(8,128)S(1)} %bitcast.225, f32[1,512,512]{1,2,0:T(8,128)S(1)} %bitcast.218, ...), kind=kLoop, calls=%fused_computation.19 | loop fusion | flops 14149632 | bytes 26775552 | tf_op jit(solution)/shard_map/reduce_sum | solution.py:177
  256.3 11.3 %concatenate.50 = bf16[2061,512]{1,0:T(8,128)(2,1)} concatenate(bf16[2048,512]{1,0:T(8,128)(2,1)} %bitcast.226, bf16[12,512]{1,0:T(8,128)(2,1)S(1)} %convert_element_type.123, bf16[1,512]{1,0:T(2,128)(2,1)S(1)} %bitcast.268), dimensions={0} | concatenate | bytes 4220928 | tf_op jit(solution)/shard_map/concatenate | solution.py:194
  267.7 16.4 %all-to-all-start = ((bf16[32,512,128]{2,1,0:T(8,128)(2,1)}), bf16[32,512,128]{2,1,0:T(8,128)(2,1)}, u32[]{:S(2)}, u32[]{:S(2)}) async-start(bf16[32,512,128]{2,1,0:T(8,128)(2,1)} %bitcast.222), calls=%async_computation.1 | async-start | bytes 8388608 | tf_op jit(solution)/shard_map/all_to_all | solution.py:203
  285.6 1.0 copy.100
  286.6 1.0 copy.101
  287.6 1.0 copy.102
  288.6 184.5 %all-reduce.2.cloned.1.call-done = bf16[2061,512]{1,0:T(8,128)(2,1)} async-done(((bf16[2061,512]{1,0:T(8,128)(2,1)}), bf16[2061,512]{1,0:T(8,128)(2,1)}) %all-reduce.2.cloned.1.call-update) | async-done | bytes 2110480 | tf_op jit(solution)/shard_map/psum | solution.py:202
  474.4 4.2 slice.316
  478.6 1.3 slice.317
  479.9 3.5 convert_reduce_fusion
  (135 shorter events, 14.5 us)
Async XLA Ops:
  7.2 8.4 %copy-start.21 = (f32[3,4,512]{2,1,0:T(4,128)S(1)}, f32[3,4,512]{2,1,0:T(4,128)}, u32[]{:S(2)}) copy-start(f32[3,4,512]{2,1,0:T(4,128)} %param.13) | copy-start | bytes 73732
  7.2 8.4 %copy-start.22 = (f32[4,512]{1,0:T(4,128)S(1)}, f32[4,512]{1,0:T(4,128)}, u32[]{:S(2)}) copy-start(f32[4,512]{1,0:T(4,128)} %param.16) | copy-start | bytes 24580
  7.2 10.2 %copy-start.23 = (s32[4,512]{1,0:T(4,128)S(1)}, s32[4,512]{1,0:T(4,128)}, u32[]{:S(2)}) copy-start(s32[4,512]{1,0:T(4,128)} %param.14) | copy-start | bytes 24580
  7.2 116.7 %all-gather.3.cloned.1.call-start = ((), (), s32[]{:S(2)}) async-start(), calls=%async_computation.2 | async-start | bytes 4718592 | tf_op jit(solution)/shard_map/all_gather | solution.py:121
  7.9 144.5 %all-gather.5.cloned.1.call-start = ((), (), s32[]{:S(2)}) async-start(), calls=%async_computation.3 | async-start | bytes 4325376 | tf_op jit(solution)/shard_map/all_gather | solution.py:125
  11.9 11.8 %collective-permute-start = (bf16[3,3,512]{1,2,0:T(8,128)(2,1)S(1)}, bf16[3,3,512]{1,2,0:T(8,128)(2,1)S(1)}, u32[]{:S(2)}, u32[]{:S(2)}) collective-permute-start(bf16[3,3,512]{1,2,0:T(8,128)(2,1)S(1)} %pad_maximum_fusion.5), channel_id=1, source_target_pairs={{0,8},{8,16},{16,24},{24,32},{32,40},{40,48},{48,56},{56,64},{64,7... | collective-permute-start | bytes 27656 | tf_op jit(solution)/shard_map/ppermute | solution.py:12
  15.5 252.2 %reduce-scatter.2.cloned.1.call-start = ((), (), s32[]{:S(2)}) async-start(), calls=%async_computation.4 | async-start | bytes 4718592 | tf_op jit(solution)/shard_map/reduce_scatter | solution.py:118
  24.6 3.8 copy-start
  24.6 3.9 copy-start.25
  29.6 0.8 copy-start.15
  29.6 129.3 %copy-start.9 = (bf16[512,512]{0,1:T(8,128)(2,1)}, bf16[512,512]{0,1:T(8,128)(2,1)S(1)}, u32[]{:S(2)}) copy-start(bf16[512,512]{0,1:T(8,128)(2,1)S(1)} %get-tuple-element.58) | copy-start | bytes 1572868
  31.8 9.4 %collective-permute-start.1 = (f32[4,136,128]{2,1,0:T(8,128)S(1)}, f32[4,136,128]{2,1,0:T(8,128)S(1)}, u32[]{:S(2)}, u32[]{:S(2)}) collective-permute-start(f32[4,136,128]{2,1,0:T(8,128)S(1)} %pad_maximum_fusion.4), channel_id=1, source_target_pairs={{0,8},{8,16},{16,24},{24,32},{32,40},{40,48},{48,56},{56,64},{64,7... | collective-permute-start | bytes 835592 | tf_op jit(solution)/shard_map/ppermute | solution.py:12
  41.3 8.7 %collective-permute-start.2 = (f32[4,136,128]{2,1,0:T(8,128)S(1)}, f32[4,136,128]{2,1,0:T(8,128)S(1)}, u32[]{:S(2)}, u32[]{:S(2)}) collective-permute-start(f32[4,136,128]{2,1,0:T(8,128)S(1)} %collective-permute-done.1), channel_id=1, source_target_pairs={{0,8},{8,16},{16,24},{24,32},{32,40},{40,48},{48,56},{56,64},{64,7... | collective-permute-start | bytes 835592 | tf_op jit(solution)/shard_map/ppermute | solution.py:12
  50.0 10.1 %collective-permute-start.3 = (f32[4,136,128]{2,1,0:T(8,128)S(1)}, f32[4,136,128]{2,1,0:T(8,128)S(1)}, u32[]{:S(2)}, u32[]{:S(2)}) collective-permute-start(f32[4,136,128]{2,1,0:T(8,128)S(1)} %pad_maximum_fusion.7), channel_id=1, source_target_pairs={{0,16},{8,24},{16,32},{24,40},{32,48},{40,56},{48,64},{56,72},{64,... | collective-permute-start | bytes 835592 | tf_op jit(solution)/shard_map/ppermute | solution.py:12
  60.1 17.5 %collective-permute-start.4 = (f32[4,136,128]{2,1,0:T(8,128)S(1)}, f32[4,136,128]{2,1,0:T(8,128)S(1)}, u32[]{:S(2)}, u32[]{:S(2)}) collective-permute-start(f32[4,136,128]{2,1,0:T(8,128)S(1)} %pad_maximum_fusion.8), channel_id=1, source_target_pairs={{0,32},{8,40},{16,48},{24,56},{32,64},{40,72},{48,80},{56,88},{64,... | collective-permute-start | bytes 835592 | tf_op jit(solution)/shard_map/ppermute | solution.py:12
  77.7 10.7 %collective-permute-start.5 = (f32[4,136,128]{2,1,0:T(8,128)S(1)}, f32[4,136,128]{2,1,0:T(8,128)S(1)}, u32[]{:S(2)}, u32[]{:S(2)}) collective-permute-start(f32[4,136,128]{2,1,0:T(8,128)S(1)} %pad_maximum_fusion.9), channel_id=1, source_target_pairs={{0,64},{8,72},{16,80},{24,88},{32,96},{40,104},{48,112},{56,120},{... | collective-permute-start | bytes 835592 | tf_op jit(solution)/shard_map/ppermute | solution.py:12
  84.1 35.0 %copy-start.18 = (pred[512,512]{1,0:T(8,128)(4,1)}, pred[512,512]{1,0:T(8,128)(4,1)S(1)}, u32[]{:S(2)}) copy-start(pred[512,512]{1,0:T(8,128)(4,1)S(1)} %iota_compare_fusion.4) | copy-start | bytes 786436
  88.5 30.0 %collective-permute-start.6 = (f32[4,136,128]{2,1,0:T(8,128)S(1)}, f32[4,136,128]{2,1,0:T(8,128)S(1)}, u32[]{:S(2)}, u32[]{:S(2)}) collective-permute-start(f32[4,136,128]{2,1,0:T(8,128)S(1)} %pad_maximum_fusion.10), channel_id=1, source_target_pairs={{0,128},{8,136},{16,144},{24,152},{32,160},{40,168},{48,176},{56,1... | collective-permute-start | bytes 835592 | tf_op jit(solution)/shard_map/ppermute | solution.py:12
  113.5 5.6 %copy-start.7 = (f32[4,512,512]{2,1,0:T(8,128)}, f32[4,512,512]{2,1,0:T(8,128)S(1)}, u32[]{:S(2)}) copy-start(f32[4,512,512]{2,1,0:T(8,128)S(1)} %fusion.96) | copy-start | bytes 12582916
  118.5 4.3 copy-start.12
  119.2 3.7 copy-start.20
  122.8 70.4 %copy-start.2 = (f32[4,512,128]{1,2,0:T(8,128)}, f32[4,512,128]{1,2,0:T(8,128)S(1)}, u32[]{:S(2)}) copy-start(f32[4,512,128]{1,2,0:T(8,128)S(1)} %get-tuple-element.57) | copy-start | bytes 3145732
  152.4 9.2 %copy-start.24 = (bf16[512,4096]{1,0:T(8,128)(2,1)S(1)}, bf16[512,4096]{1,0:T(8,128)(2,1)}, u32[]{:S(2)}) copy-start(bf16[512,4096]{1,0:T(8,128)(2,1)} %all-gather.3.cloned.1.call-done) | copy-start | bytes 12582916
  158.4 34.8 %copy-start.5 = (bf16[512,512]{0,1:T(8,128)(2,1)}, bf16[512,512]{0,1:T(8,128)(2,1)S(1)}, u32[]{:S(2)}) copy-start(bf16[512,512]{0,1:T(8,128)(2,1)S(1)} %convolution_convert_fusion.4) | copy-start | bytes 1572868
  158.4 3.3 copy-start.11
  160.4 11.0 %collective-permute-start.7 = (f32[4,136,128]{2,1,0:T(8,128)S(1)}, f32[4,136,128]{2,1,0:T(8,128)S(1)}, u32[]{:S(2)}, u32[]{:S(2)}) collective-permute-start(f32[4,136,128]{2,1,0:T(8,128)S(1)} %pad_maximum_fusion.3), channel_id=1, source_target_pairs={{8,0},{16,8},{24,16},{32,24},{40,32},{48,40},{56,48},{64,56},{72,6... | collective-permute-start | bytes 835592 | tf_op jit(solution)/shard_map/ppermute | solution.py:12
  164.1 8.8 %copy-start.8 = (bf16[512,4096]{1,0:T(8,128)(2,1)S(1)}, bf16[512,4096]{1,0:T(8,128)(2,1)}, u32[]{:S(2)}) copy-start(bf16[512,4096]{1,0:T(8,128)(2,1)} %all-gather.5.cloned.1.call-done) | copy-start | bytes 12582916
  171.4 8.5 %copy-start.17 = (f32[4,136,128]{2,1,0:T(8,128)}, f32[4,136,128]{2,1,0:T(8,128)S(1)}, u32[]{:S(2)}) copy-start(f32[4,136,128]{2,1,0:T(8,128)S(1)} %collective-permute-done.7) | copy-start | bytes 835588
  171.4 8.5 %collective-permute-start.8 = (f32[4,136,128]{2,1,0:T(8,128)S(1)}, f32[4,136,128]{2,1,0:T(8,128)}, u32[]{:S(2)}, u32[]{:S(2)}) collective-permute-start(f32[4,136,128]{2,1,0:T(8,128)S(1)} %collective-permute-done.7), channel_id=1, source_target_pairs={{8,0},{16,8},{24,16},{32,24},{40,32},{48,40},{56,48},{64,56},{72,6... | collective-permute-start | bytes 835592 | tf_op jit(solution)/shard_map/ppermute | solution.py:12
  181.7 9.9 %collective-permute-start.9 = (f32[4,136,128]{2,1,0:T(8,128)S(1)}, f32[4,136,128]{2,1,0:T(8,128)S(1)}, u32[]{:S(2)}, u32[]{:S(2)}) collective-permute-start(f32[4,136,128]{2,1,0:T(8,128)S(1)} %pad_maximum_fusion.11), channel_id=1, source_target_pairs={{16,0},{24,8},{32,16},{40,24},{48,32},{56,40},{64,48},{72,56},{80,... | collective-permute-start | bytes 835592 | tf_op jit(solution)/shard_map/ppermute | solution.py:12
  191.8 11.2 %copy-start.16 = (bf16[512,512]{0,1:T(8,128)(2,1)S(1)}, bf16[512,512]{0,1:T(8,128)(2,1)}, u32[]{:S(2)}) copy-start(bf16[512,512]{0,1:T(8,128)(2,1)} %copy-done.15) | copy-start | bytes 1572868
  191.8 11.2 %copy-start.19 = (pred[512,512]{1,0:T(8,128)(4,1)S(1)}, pred[512,512]{1,0:T(8,128)(4,1)}, u32[]{:S(2)}) copy-start(pred[512,512]{1,0:T(8,128)(4,1)} %copy-done.18) | copy-start | bytes 786436
  191.8 9.8 %collective-permute-start.10 = (f32[4,136,128]{2,1,0:T(8,128)S(1)}, f32[4,136,128]{2,1,0:T(8,128)S(1)}, u32[]{:S(2)}, u32[]{:S(2)}) collective-permute-start(f32[4,136,128]{2,1,0:T(8,128)S(1)} %pad_maximum_fusion.12), channel_id=1, source_target_pairs={{32,0},{40,8},{48,16},{56,24},{64,32},{72,40},{80,48},{88,56},{96,... | collective-permute-start | bytes 835592 | tf_op jit(solution)/shard_map/ppermute | solution.py:12
  201.6 14.8 %collective-permute-start.11 = (f32[4,136,128]{2,1,0:T(8,128)S(1)}, f32[4,136,128]{2,1,0:T(8,128)S(1)}, u32[]{:S(2)}, u32[]{:S(2)}) collective-permute-start(f32[4,136,128]{2,1,0:T(8,128)S(1)} %pad_maximum_fusion.13), channel_id=1, source_target_pairs={{64,0},{72,8},{80,16},{88,24},{96,32},{104,40},{112,48},{120,56},{... | collective-permute-start | bytes 835592 | tf_op jit(solution)/shard_map/ppermute | solution.py:12
  202.9 15.1 %copy-start.10 = (bf16[512,512]{0,1:T(8,128)(2,1)S(1)}, bf16[512,512]{0,1:T(8,128)(2,1)}, u32[]{:S(2)}) copy-start(bf16[512,512]{0,1:T(8,128)(2,1)} %copy-done.9) | copy-start | bytes 1572868
  216.5 15.0 %collective-permute-start.12 = (f32[4,136,128]{2,1,0:T(8,128)S(1)}, f32[4,136,128]{2,1,0:T(8,128)S(1)}, u32[]{:S(2)}, u32[]{:S(2)}) collective-permute-start(f32[4,136,128]{2,1,0:T(8,128)S(1)} %pad_maximum_fusion.14), channel_id=1, source_target_pairs={{128,0},{136,8},{144,16},{152,24},{160,32},{168,40},{176,48},{184,... | collective-permute-start | bytes 835592 | tf_op jit(solution)/shard_map/ppermute | solution.py:12
  231.5 1.3 copy-start.3
  231.5 1.4 copy-start.6
  231.5 1.4 copy-start.13
  237.9 3.5 copy-start.14
  237.9 6.4 %collective-permute-start.13 = (f32[3,3,512]{2,1,0:T(4,128)S(1)}, f32[3,3,512]{2,1,0:T(4,128)S(1)}, u32[]{:S(2)}, u32[]{:S(2)}) collective-permute-start(f32[3,3,512]{2,1,0:T(4,128)S(1)} %copy.98), channel_id=1, source_target_pairs={{8,0},{16,8},{24,16},{32,24},{40,32},{48,40},{56,48},{64,56},{72,6... | collective-permute-start | bytes 55304 | tf_op jit(solution)/shard_map/ppermute | solution.py:12
  245.5 2.3 copy-start.1
  267.7 212.3 %all-to-all-start = ((bf16[32,512,128]{2,1,0:T(8,128)(2,1)}), bf16[32,512,128]{2,1,0:T(8,128)(2,1)}, u32[]{:S(2)}, u32[]{:S(2)}) async-start(bf16[32,512,128]{2,1,0:T(8,128)(2,1)} %bitcast.222), calls=%async_computation.1 | async-start | bytes 8388608 | tf_op jit(solution)/shard_map/all_to_all | solution.py:203
  284.1 1.4 copy-start.4
  284.1 189.0 %all-reduce.2.cloned.1.call-start = ((), (), s32[]{:S(2)}) async-start(), calls=%async_computation.5 | async-start | bytes 4227072 | tf_op jit(solution)/shard_map/psum | solution.py:202
Sparse Core Ops, SparseCore 0:
  9.8 36.5 all-gather.2
  48.9 103.5 all-gather.4
  177.4 35.0 reduce-scatter.1
  288.1 184.9 all-reduce.1

commit v5 on v4

--- a/solution.py
+++ b/solution.py
@@ -12,25 +12,33 @@
     return lax.ppermute(x, axis, pairs)
 
 
+def exchanged(log_total, state, axis, by):
+    heads, rows, cols = state.shape
+    high = log_total.astype(jnp.bfloat16)
+    low = (log_total - high.astype(jnp.float32)).astype(jnp.bfloat16)
+    message = jnp.concatenate(
+        [
+            state.astype(jnp.bfloat16),
+            jnp.broadcast_to(high[:, None, None], (heads, 8, cols)),
+            jnp.broadcast_to(low[:, None, None], (heads, 8, cols)),
+        ],
+        axis=1,
+    )
+    message = shifted(message, axis, by).astype(jnp.float32)
+    return message[:, rows, 0] + message[:, rows + 8, 0], message[:, :rows, :]
+
+
 def entering(log_total, state, axis, reverse):
     length = lax.axis_size(axis)
     step = -1 if reverse else 1
-    heads, rows, cols = state.shape
-    total_rows = jnp.broadcast_to(log_total[:, None, None], (heads, 8, cols))
-    packed = shifted(jnp.concatenate([state, total_rows], axis=1), axis, step)
+    log_total, state = exchanged(log_total, state, axis, step)
     distance = 1
     while distance < length:
-        far = shifted(packed, axis, step * distance)
-        near_total = packed[:, rows : rows + 1, :]
-        packed = jnp.concatenate(
-            [
-                jnp.exp(near_total) * far[:, :rows, :] + packed[:, :rows, :],
-                far[:, rows:, :] + packed[:, rows:, :],
-            ],
-            axis=1,
-        )
+        far_total, far_state = exchanged(log_total, state, axis, step * distance)
+        state = jnp.exp(log_total)[:, None, None] * far_state + state
+        log_total = far_total + log_total
         distance *= 2
-    return packed[:, :rows, :]
+    return state
 
 
 def on_device(
@@ -199,7 +207,8 @@
         ]
     )
     packed, layer_out, weight_parts = lax.optimization_barrier((packed, layer_out, weight_parts))
-    summed = lax.psum(packed, "seq").astype(jnp.float32)
+    summed = lax.psum(packed, "seq")
+    summed = summed.astype(jnp.float32)
     weight_parts = lax.all_to_all(weight_parts, "seq", 0, 0, tiled=True)
     grad_weight = jnp.sum(weight_parts.astype(jnp.float32), axis=0)
     grad_tables = summed[:table_rows].reshape(2, buckets, feat_width)

time: 497 us -> 472 us (0.950)
  waiting for transfers between devices: 283 us -> 261 us
  starting transfers between devices: 87.9 us -> 80.2 us
    ppermute x14, waiting for transfers between devices: 68.3 us -> 48 us  [shifted(): return lax.ppermute(x, axis, pairs)]
    ppermute x14, starting transfers between devices: 71.4 us -> 66.3 us  [shifted(): return lax.ppermute(x, axis, pairs)]
  transfers between devices with their start and end apart: 19 -> 19, of which waited for: 16 -> 14; matrix products, arithmetic and copies ran while one was open for 19% -> 20% of each run, Pallas kernels for 0% -> 0%
where the time goes in v5:
time: 472 us; the launch traced here: 465 us
  waiting for transfers between devices  261 us (55%)
  starting transfers between devices  80.2 us (17%)
  matrix products  44.5 us (9%)
  local copies, waits for them, and re-layouts  36 us (8%)
  other arithmetic  28.3 us (6%)
  between operations  15.3 us (3%)
    psum x1, waiting for transfers between devices, on_device(): summed = lax.psum(packed, 'seq')  183 us
    ppermute x14, starting transfers between devices, shifted(): return lax.ppermute(x, axis, pairs)  66.3 us
    ppermute x14, waiting for transfers between devices, shifted(): return lax.ppermute(x, axis, pairs)  48 us
    all_gather x1, waiting for transfers between devices, on_device(): lax.all_gather(out_weight, 'seq', axis=1, tiled=True)  27.9 us
    all_to_all x1, starting transfers between devices, on_device(): weight_parts = lax.all_to_all(weight_parts, 'seq', 0, 0, tiled=True)  13.7 us
    concatenate x1, local copies, waits for them, and re-layouts, on_device(): jnp.concatenate([table_terms.astype(jnp.bfloat16).reshape(table_rows, fea...  11.3 us
  transfers between devices with their start and end apart: 19, of which 14 were waited for; matrix products, arithmetic and copies ran while one was open for 20% of the time, Pallas kernels for 0%

profile of v5, /device:TPU:2, one launch (start us, length us, event | category | flops | bytes accessed | tf_op | source)
XLA Modules:
  0.0 464.6 jit_solution(10957595580384527918)
XLA Ops:
  8.0 1.3 copy.79
  9.2 1.3 copy.80
  10.5 1.3 copy.81
  11.9 3.5 collective-permute-start
  15.7 1.2 reduce-window.6
  17.6 2.3 fusion.58
  19.9 3.9 collective-permute-done
  24.7 3.7 multiply_add_fusion
  28.6 1.1 fusion.64
  30.0 1.3 convolution_convert_fusion.6
  31.5 4.4 collective-permute-start.1
  35.9 2.6 collective-permute-done.1
  39.0 4.4 collective-permute-start.2
  43.4 2.6 collective-permute-done.2
  46.6 6.0 %collective-permute-start.3 = (bf16[4,144,128]{2,1,0:T(8,128)(2,1)S(1)}, bf16[4,144,128]{2,1,0:T(8,128)(2,1)S(1)}, u32[]{:S(2)}, u32[]{:S(2)}) collective-permute-start(bf16[4,144,128]{2,1,0:T(8,128)(2,1)S(1)} %pad_maximum_fusion.10), channel_id=1, source_target_pairs={{0,16},{8,24},{16,32},{24,40},{32,48},{40,56},{48,64},{56,72},{64,... | collective-permute-start | bytes 442376 | tf_op jit(solution)/shard_map/ppermute | solution.py:12
  52.6 2.6 collective-permute-done.3
  55.8 11.8 %collective-permute-start.4 = (bf16[4,144,128]{2,1,0:T(8,128)(2,1)S(1)}, bf16[4,144,128]{2,1,0:T(8,128)(2,1)S(1)}, u32[]{:S(2)}, u32[]{:S(2)}) collective-permute-start(bf16[4,144,128]{2,1,0:T(8,128)(2,1)S(1)} %pad_maximum_fusion.11), channel_id=1, source_target_pairs={{0,32},{8,40},{16,48},{24,56},{32,64},{40,72},{48,80},{56,88},{64,... | collective-permute-start | bytes 442376 | tf_op jit(solution)/shard_map/ppermute | solution.py:12
  67.6 3.0 collective-permute-done.4
  71.2 5.7 %collective-permute-start.5 = (bf16[4,144,128]{2,1,0:T(8,128)(2,1)S(1)}, bf16[4,144,128]{2,1,0:T(8,128)(2,1)S(1)}, u32[]{:S(2)}, u32[]{:S(2)}) collective-permute-start(bf16[4,144,128]{2,1,0:T(8,128)(2,1)S(1)} %pad_maximum_fusion.12), channel_id=1, source_target_pairs={{0,64},{8,72},{16,80},{24,88},{32,96},{40,104},{48,112},{56,120},{... | collective-permute-start | bytes 442376 | tf_op jit(solution)/shard_map/ppermute | solution.py:12
  77.0 2.6 collective-permute-done.5
  80.1 20.4 %collective-permute-start.6 = (bf16[4,144,128]{2,1,0:T(8,128)(2,1)S(1)}, bf16[4,144,128]{2,1,0:T(8,128)(2,1)S(1)}, u32[]{:S(2)}, u32[]{:S(2)}) collective-permute-start(bf16[4,144,128]{2,1,0:T(8,128)(2,1)S(1)} %pad_maximum_fusion.13), channel_id=1, source_target_pairs={{0,128},{8,136},{16,144},{24,152},{32,160},{40,168},{48,176},{56,1... | collective-permute-start | bytes 442376 | tf_op jit(solution)/shard_map/ppermute | solution.py:12
  101.4 3.5 collective-permute-done.6
  105.6 3.6 multiply_reduce_fusion.4
  109.3 1.1 fusion.75
  110.4 27.9 %all-gather.5.cloned.1.call-done = bf16[512,4096]{1,0:T(8,128)(2,1)} async-done(((bf16[512,128]{1,0:T(8,128)(2,1)}), bf16[512,4096]{1,0:T(8,128)(2,1)}) %all-gather.5.cloned.1.call-update) | async-done | bytes 4194320 | tf_op jit(solution)/shard_map/all_gather | solution.py:133
  138.3 5.9 %convolution_convert_fusion.4 = bf16[512,512]{0,1:T(8,128)(2,1)S(1)} fusion(bf16[512,4096]{1,0:T(8,128)(2,1)} %all-gather.3.cloned.1.call-done, bf16[512,4096]{1,0:T(8,128)(2,1)} %all-gather.5.cloned.1.call-done), kind=kOutput, calls=%fused_computation.70 | convolution fusion | flops 2147745792 | bytes 8912896 | tf_op jit(solution)/shard_map/dot_general | solution.py:131
  144.2 1.1 fusion.71
  145.3 1.4 convolution_convert_fusion.5
  147.4 1.3 collective-permute-start.7
  148.7 4.4 convolution_convert_fusion
  153.1 1.8 collective-permute-done.7
  155.4 1.5 collective-permute-start.8
  156.9 4.5 fusion.14
  161.5 3.1 copy.138
  165.2 1.3 collective-permute-start.9
  166.5 3.9 fusion.41
  170.4 3.3 collective-permute-done.9
  174.3 1.4 collective-permute-start.10
  175.7 2.0 fusion.131
  177.7 8.9 %collective-permute-done.10 = bf16[4,144,128]{2,1,0:T(8,128)(2,1)S(1)} collective-permute-done((bf16[4,144,128]{2,1,0:T(8,128)(2,1)S(1)}, bf16[4,144,128]{2,1,0:T(8,128)(2,1)S(1)}, u32[]{:S(2)}, u32[]{:S(2)}) %collective-permute-start.10) | collective-permute-done | bytes 147488 | tf_op jit(solution)/shard_map/ppermute | solution.py:12
  187.2 1.7 collective-permute-start.11
  188.9 3.5 fusion.35
  192.4 5.9 %collective-permute-done.11 = bf16[4,144,128]{2,1,0:T(8,128)(2,1)S(1)} collective-permute-done((bf16[4,144,128]{2,1,0:T(8,128)(2,1)S(1)}, bf16[4,144,128]{2,1,0:T(8,128)(2,1)S(1)}, u32[]{:S(2)}, u32[]{:S(2)}) %collective-permute-start.11) | collective-permute-done | bytes 147488 | tf_op jit(solution)/shard_map/ppermute | solution.py:12
  198.8 1.3 collective-permute-start.12
  200.1 2.7 fusion.38
  202.9 7.2 %collective-permute-done.12 = bf16[4,144,128]{2,1,0:T(8,128)(2,1)S(1)} collective-permute-done((bf16[4,144,128]{2,1,0:T(8,128)(2,1)S(1)}, bf16[4,144,128]{2,1,0:T(8,128)(2,1)S(1)}, u32[]{:S(2)}, u32[]{:S(2)}) %collective-permute-start.12) | collective-permute-done | bytes 147488 | tf_op jit(solution)/shard_map/ppermute | solution.py:12
  211.5 2.2 add_convert_fusion
  214.1 1.0 slice.316
  215.1 1.4 copy.98
  216.5 1.6 collective-permute-start.13
  218.1 2.0 fusion.51
  221.1 1.5 pad_maximum_fusion.2
  222.6 1.2 copy.99
  223.8 1.6 pad_maximum_fusion
  226.2 8.4 %multiply_reduce_fusion.3 = (bf16[3,512]{1,0:T(4,128)(2,1)S(1)}, bf16[3,512]{1,0:T(4,128)(2,1)S(1)}, bf16[3,512]{1,0:T(4,128)(2,1)S(1)}, bf16[3,512]{1,0:T(4,128)(2,1)S(1)}, bf16[3,512,512]{1,2,0:T(8,128)(2,1)}) fusion(f32[3,515,512]{1,2,0:T(8,128)S(1)} %copy-done.1, f32[1,512,512]{1,2,0:T(8,128)S(1)} %bitcast.216, f32[1,512,512]{1,2,0:T(8,128)S(1)} %bitcast.212, ...), kind=kLoop, calls=%fused_computation.19 | loop fusion | flops 14149632 | bytes 26775552 | tf_op jit(solution)/shard_map/reduce_sum | solution.py:185
  234.7 11.3 %concatenate.58 = bf16[2061,512]{1,0:T(8,128)(2,1)} concatenate(bf16[2048,512]{1,0:T(8,128)(2,1)} %bitcast.220, bf16[12,512]{1,0:T(8,128)(2,1)S(1)} %convert_element_type.403, bf16[1,512]{1,0:T(2,128)(2,1)S(1)} %bitcast.260), dimensions={0} | concatenate | bytes 4220928 | tf_op jit(solution)/shard_map/concatenate | solution.py:202
  246.0 13.7 %all-to-all-start = ((bf16[32,512,128]{2,1,0:T(8,128)(2,1)}), bf16[32,512,128]{2,1,0:T(8,128)(2,1)}, u32[]{:S(2)}, u32[]{:S(2)}) async-start(bf16[32,512,128]{2,1,0:T(8,128)(2,1)} %bitcast.213), calls=%async_computation.1 | async-start | bytes 8388608 | tf_op jit(solution)/shard_map/all_to_all | solution.py:212
  261.2 1.0 copy.100
  262.2 1.0 copy.101
  263.2 1.0 copy.102
  264.2 183.4 %all-reduce.2.cloned.1.call-done = bf16[2061,512]{1,0:T(8,128)(2,1)} async-done(((bf16[2061,512]{1,0:T(8,128)(2,1)}), bf16[2061,512]{1,0:T(8,128)(2,1)}) %all-reduce.2.cloned.1.call-update) | async-done | bytes 2110480 | tf_op jit(solution)/shard_map/psum | solution.py:210
  448.9 4.2 slice.324
  453.1 1.3 slice.325
  454.4 3.5 convert_reduce_fusion
  (234 shorter events, 16.9 us)
Async XLA Ops:
  7.2 8.4 %copy-start.39 = (f32[3,4,512]{2,1,0:T(4,128)S(1)}, f32[3,4,512]{2,1,0:T(4,128)}, u32[]{:S(2)}) copy-start(f32[3,4,512]{2,1,0:T(4,128)} %param.13) | copy-start | bytes 73732
  7.2 8.4 %copy-start.42 = (s32[4,512]{1,0:T(4,128)S(1)}, s32[4,512]{1,0:T(4,128)}, u32[]{:S(2)}) copy-start(s32[4,512]{1,0:T(4,128)} %param.14) | copy-start | bytes 24580
  7.2 8.4 %copy-start.43 = (f32[4,512]{1,0:T(4,128)S(1)}, f32[4,512]{1,0:T(4,128)}, u32[]{:S(2)}) copy-start(f32[4,512]{1,0:T(4,128)} %param.16) | copy-start | bytes 24580
  7.2 103.2 %all-gather.3.cloned.1.call-start = ((), (), s32[]{:S(2)}) async-start(), calls=%async_computation.2 | async-start | bytes 4718592 | tf_op jit(solution)/shard_map/all_gather | solution.py:129
  7.9 130.4 %all-gather.5.cloned.1.call-start = ((), (), s32[]{:S(2)}) async-start(), calls=%async_computation.3 | async-start | bytes 4325376 | tf_op jit(solution)/shard_map/all_gather | solution.py:133
  11.9 11.8 %collective-permute-start = (bf16[3,3,512]{1,2,0:T(8,128)(2,1)S(1)}, bf16[3,3,512]{1,2,0:T(8,128)(2,1)S(1)}, u32[]{:S(2)}, u32[]{:S(2)}) collective-permute-start(bf16[3,3,512]{1,2,0:T(8,128)(2,1)S(1)} %pad_maximum_fusion.3), channel_id=1, source_target_pairs={{0,8},{8,16},{16,24},{24,32},{32,40},{40,48},{48,56},{56,64},{64,7... | collective-permute-start | bytes 27656 | tf_op jit(solution)/shard_map/ppermute | solution.py:12
  15.5 230.5 %reduce-scatter.2.cloned.1.call-start = ((), (), s32[]{:S(2)}) async-start(), calls=%async_computation.4 | async-start | bytes 4718592 | tf_op jit(solution)/shard_map/reduce_scatter | solution.py:126
  15.6 9.0 %copy-start.51 = (s32[1,512]{1,0:T(1,128)}, s32[1,512]{1,0:T(1,128)S(1)}, u32[]{:S(2)}) copy-start(s32[1,512]{1,0:T(1,128)S(1)} %get-tuple-element.123) | copy-start | bytes 6148
  15.6 9.0 %copy-start.53 = (s32[1,512]{1,0:T(1,128)}, s32[1,512]{1,0:T(1,128)S(1)}, u32[]{:S(2)}) copy-start(s32[1,512]{1,0:T(1,128)S(1)} %get-tuple-element.124) | copy-start | bytes 6148
  15.6 12.9 %copy-start.47 = (s32[1,512]{1,0:T(1,128)}, s32[1,512]{1,0:T(1,128)S(1)}, u32[]{:S(2)}) copy-start(s32[1,512]{1,0:T(1,128)S(1)} %get-tuple-element.122) | copy-start | bytes 6148
  15.6 12.9 %copy-start.49 = (s32[1,512]{1,0:T(1,128)}, s32[1,512]{1,0:T(1,128)S(1)}, u32[]{:S(2)}) copy-start(s32[1,512]{1,0:T(1,128)S(1)} %get-tuple-element.125) | copy-start | bytes 6148
  17.3 88.3 %copy-start.40 = (f32[1,4,4,128]{3,1,2,0:T(4,128)}, f32[1,4,4,128]{3,1,2,0:T(4,128)S(1)}, u32[]{:S(2)}) copy-start(f32[1,4,4,128]{3,1,2,0:T(4,128)S(1)} %copy.139) | copy-start | bytes 24580
  17.5 7.2 %copy-start.23 = (f32[3,512]{1,0:T(4,128)}, f32[3,512]{1,0:T(4,128)S(1)}, u32[]{:S(2)}) copy-start(f32[3,512]{1,0:T(4,128)S(1)} %get-tuple-element.129) | copy-start | bytes 18436
  17.5 7.2 %copy-start.25 = (f32[3,512]{1,0:T(4,128)}, f32[3,512]{1,0:T(4,128)S(1)}, u32[]{:S(2)}) copy-start(f32[3,512]{1,0:T(4,128)S(1)} %get-tuple-element.130) | copy-start | bytes 18436
  17.5 7.2 %copy-start.27 = (f32[3,512]{1,0:T(4,128)}, f32[3,512]{1,0:T(4,128)S(1)}, u32[]{:S(2)}) copy-start(f32[3,512]{1,0:T(4,128)S(1)} %get-tuple-element.131) | copy-start | bytes 18436
  17.5 7.2 %copy-start.29 = (f32[3,512]{1,0:T(4,128)}, f32[3,512]{1,0:T(4,128)S(1)}, u32[]{:S(2)}) copy-start(f32[3,512]{1,0:T(4,128)S(1)} %get-tuple-element.132) | copy-start | bytes 18436
  17.6 12.4 %copy-start.35 = (f32[4,512]{1,0:T(4,128)}, f32[4,512]{1,0:T(4,128)S(1)}, u32[]{:S(2)}) copy-start(f32[4,512]{1,0:T(4,128)S(1)} %get-tuple-element.121) | copy-start | bytes 24580
  17.6 91.7 %copy-start.33 = (f32[512,4]{0,1:T(4,128)}, f32[512,4]{0,1:T(4,128)S(1)}, u32[]{:S(2)}) copy-start(f32[512,4]{0,1:T(4,128)S(1)} %get-tuple-element.119) | copy-start | bytes 24580
  24.6 3.8 copy-start
  24.7 3.9 copy-start.55
  29.7 26.0 %copy-start.14 = (bf16[512,512]{0,1:T(8,128)(2,1)}, bf16[512,512]{0,1:T(8,128)(2,1)S(1)}, u32[]{:S(2)}) copy-start(bf16[512,512]{0,1:T(8,128)(2,1)S(1)} %get-tuple-element.108) | copy-start | bytes 1572868
  29.7 115.6 %copy-start.10 = (bf16[512,512]{0,1:T(8,128)(2,1)}, bf16[512,512]{0,1:T(8,128)(2,1)S(1)}, u32[]{:S(2)}) copy-start(bf16[512,512]{0,1:T(8,128)(2,1)S(1)} %get-tuple-element.107) | copy-start | bytes 1572868
  31.5 7.1 %collective-permute-start.1 = (bf16[4,144,128]{2,1,0:T(8,128)(2,1)S(1)}, bf16[4,144,128]{2,1,0:T(8,128)(2,1)S(1)}, u32[]{:S(2)}, u32[]{:S(2)}) collective-permute-start(bf16[4,144,128]{2,1,0:T(8,128)(2,1)S(1)} %pad_maximum_fusion.6), channel_id=1, source_target_pairs={{0,8},{8,16},{16,24},{24,32},{32,40},{40,48},{48,56},{56,64},{64,7... | collective-permute-start | bytes 442376 | tf_op jit(solution)/shard_map/ppermute | solution.py:12
  39.0 7.0 %collective-permute-start.2 = (bf16[4,144,128]{2,1,0:T(8,128)(2,1)S(1)}, bf16[4,144,128]{2,1,0:T(8,128)(2,1)S(1)}, u32[]{:S(2)}, u32[]{:S(2)}) collective-permute-start(bf16[4,144,128]{2,1,0:T(8,128)(2,1)S(1)} %pad_maximum_fusion.9), channel_id=1, source_target_pairs={{0,8},{8,16},{16,24},{24,32},{32,40},{40,48},{48,56},{56,64},{64,7... | collective-permute-start | bytes 442376 | tf_op jit(solution)/shard_map/ppermute | solution.py:12
  46.6 8.7 %collective-permute-start.3 = (bf16[4,144,128]{2,1,0:T(8,128)(2,1)S(1)}, bf16[4,144,128]{2,1,0:T(8,128)(2,1)S(1)}, u32[]{:S(2)}, u32[]{:S(2)}) collective-permute-start(bf16[4,144,128]{2,1,0:T(8,128)(2,1)S(1)} %pad_maximum_fusion.10), channel_id=1, source_target_pairs={{0,16},{8,24},{16,32},{24,40},{32,48},{40,56},{48,64},{56,72},{64,... | collective-permute-start | bytes 442376 | tf_op jit(solution)/shard_map/ppermute | solution.py:12
  55.8 14.8 %collective-permute-start.4 = (bf16[4,144,128]{2,1,0:T(8,128)(2,1)S(1)}, bf16[4,144,128]{2,1,0:T(8,128)(2,1)S(1)}, u32[]{:S(2)}, u32[]{:S(2)}) collective-permute-start(bf16[4,144,128]{2,1,0:T(8,128)(2,1)S(1)} %pad_maximum_fusion.11), channel_id=1, source_target_pairs={{0,32},{8,40},{16,48},{24,56},{32,64},{40,72},{48,80},{56,88},{64,... | collective-permute-start | bytes 442376 | tf_op jit(solution)/shard_map/ppermute | solution.py:12
  71.2 8.5 %collective-permute-start.5 = (bf16[4,144,128]{2,1,0:T(8,128)(2,1)S(1)}, bf16[4,144,128]{2,1,0:T(8,128)(2,1)S(1)}, u32[]{:S(2)}, u32[]{:S(2)}) collective-permute-start(bf16[4,144,128]{2,1,0:T(8,128)(2,1)S(1)} %pad_maximum_fusion.12), channel_id=1, source_target_pairs={{0,64},{8,72},{16,80},{24,88},{32,96},{40,104},{48,112},{56,120},{... | collective-permute-start | bytes 442376 | tf_op jit(solution)/shard_map/ppermute | solution.py:12
  77.0 28.6 %copy-start.19 = (pred[512,512]{1,0:T(8,128)(4,1)}, pred[512,512]{1,0:T(8,128)(4,1)S(1)}, u32[]{:S(2)}) copy-start(pred[512,512]{1,0:T(8,128)(4,1)S(1)} %iota_compare_fusion.4) | copy-start | bytes 786436
  80.1 24.8 %collective-permute-start.6 = (bf16[4,144,128]{2,1,0:T(8,128)(2,1)S(1)}, bf16[4,144,128]{2,1,0:T(8,128)(2,1)S(1)}, u32[]{:S(2)}, u32[]{:S(2)}) collective-permute-start(bf16[4,144,128]{2,1,0:T(8,128)(2,1)S(1)} %pad_maximum_fusion.13), channel_id=1, source_target_pairs={{0,128},{8,136},{16,144},{24,152},{32,160},{40,168},{48,176},{56,1... | collective-permute-start | bytes 442376 | tf_op jit(solution)/shard_map/ppermute | solution.py:12
  101.2 8.0 %copy-start.7 = (f32[4,512,512]{2,1,0:T(8,128)}, f32[4,512,512]{2,1,0:T(8,128)S(1)}, u32[]{:S(2)}) copy-start(f32[4,512,512]{2,1,0:T(8,128)S(1)} %fusion.94) | copy-start | bytes 12582916
  101.3 4.2 copy-start.44
  105.6 3.7 copy-start.37
  109.2 66.5 %copy-start.2 = (f32[4,512,128]{1,2,0:T(8,128)}, f32[4,512,128]{1,2,0:T(8,128)S(1)}, u32[]{:S(2)}) copy-start(f32[4,512,128]{1,2,0:T(8,128)S(1)} %get-tuple-element.91) | copy-start | bytes 3145732
  109.3 36.0 %copy-start.21 = (f32[4,512]{1,0:T(4,128)}, f32[4,512]{1,0:T(4,128)S(1)}, u32[]{:S(2)}) copy-start(f32[4,512]{1,0:T(4,128)S(1)} %get-tuple-element.118) | copy-start | bytes 24580
  138.3 10.4 %copy-start.12 = (bf16[512,4,128]{0,2,1:T(8,128)(2,1)S(1)}, bf16[512,4,128]{0,2,1:T(8,128)(2,1)}, u32[]{:S(2)}) copy-start(bf16[512,4,128]{0,2,1:T(8,128)(2,1)} %fusion.75) | copy-start | bytes 1572868
  144.2 31.6 %copy-start.5 = (bf16[512,512]{0,1:T(8,128)(2,1)}, bf16[512,512]{0,1:T(8,128)(2,1)S(1)}, u32[]{:S(2)}) copy-start(bf16[512,512]{0,1:T(8,128)(2,1)S(1)} %convolution_convert_fusion.4) | copy-start | bytes 1572868
  144.2 4.5 copy-start.9
  147.4 7.5 %collective-permute-start.7 = (bf16[4,144,128]{2,1,0:T(8,128)(2,1)}, bf16[4,144,128]{2,1,0:T(8,128)(2,1)S(1)}, u32[]{:S(2)}, u32[]{:S(2)}) collective-permute-start(bf16[4,144,128]{2,1,0:T(8,128)(2,1)} %pad_maximum_fusion.5), channel_id=1, source_target_pairs={{8,0},{16,8},{24,16},{32,24},{40,32},{48,40},{56,48},{64,56},{72,6... | collective-permute-start | bytes 442376 | tf_op jit(solution)/shard_map/ppermute | solution.py:12
  153.1 3.8 copy-start.13
  155.4 9.2 %collective-permute-start.8 = (bf16[4,144,128]{2,1,0:T(8,128)(2,1)S(1)}, bf16[4,144,128]{2,1,0:T(8,128)(2,1)S(1)}, u32[]{:S(2)}, u32[]{:S(2)}) collective-permute-start(bf16[4,144,128]{2,1,0:T(8,128)(2,1)S(1)} %pad_maximum_fusion.14), channel_id=1, source_target_pairs={{8,0},{16,8},{24,16},{32,24},{40,32},{48,40},{56,48},{64,56},{72,6... | collective-permute-start | bytes 442376 | tf_op jit(solution)/shard_map/ppermute | solution.py:12
  161.4 5.0 %copy-start.8 = (f32[4,512,512]{2,1,0:T(8,128)S(1)}, f32[4,512,512]{2,1,0:T(8,128)}, u32[]{:S(2)}) copy-start(f32[4,512,512]{2,1,0:T(8,128)} %copy-done.7) | copy-start | bytes 12582916
  161.5 5.0 %copy-start.20 = (pred[512,512]{1,0:T(8,128)(4,1)S(1)}, pred[512,512]{1,0:T(8,128)(4,1)}, u32[]{:S(2)}) copy-start(pred[512,512]{1,0:T(8,128)(4,1)} %copy-done.19) | copy-start | bytes 786436
  161.5 5.0 %copy-start.22 = (f32[4,512]{1,0:T(4,128)S(1)}, f32[4,512]{1,0:T(4,128)}, u32[]{:S(2)}) copy-start(f32[4,512]{1,0:T(4,128)} %copy-done.21) | copy-start | bytes 24580
  161.5 5.0 %copy-start.32 = (f32[4,512]{1,0:T(4,128)S(1)}, f32[4,512]{1,0:T(4,128)}, u32[]{:S(2)}) copy-start(f32[4,512]{1,0:T(4,128)} %copy-done.31) | copy-start | bytes 24580
  161.5 5.0 %copy-start.38 = (f32[512]{0:T(512)S(1)}, f32[512]{0:T(512)}, u32[]{:S(2)}) copy-start(f32[512]{0:T(512)} %param.17) | copy-start | bytes 6148
  161.5 5.0 %copy-start.41 = (f32[1,4,4,128]{3,1,2,0:T(4,128)S(1)}, f32[1,4,4,128]{3,1,2,0:T(4,128)}, u32[]{:S(2)}) copy-start(f32[1,4,4,128]{3,1,2,0:T(4,128)} %copy-done.40) | copy-start | bytes 24580
  165.2 8.6 %collective-permute-start.9 = (bf16[4,144,128]{2,1,0:T(8,128)(2,1)S(1)}, bf16[4,144,128]{2,1,0:T(8,128)(2,1)S(1)}, u32[]{:S(2)}, u32[]{:S(2)}) collective-permute-start(bf16[4,144,128]{2,1,0:T(8,128)(2,1)S(1)} %pad_maximum_fusion.15), channel_id=1, source_target_pairs={{16,0},{24,8},{32,16},{40,24},{48,32},{56,40},{64,48},{72,56},{80,... | collective-permute-start | bytes 442376 | tf_op jit(solution)/shard_map/ppermute | solution.py:12
  174.3 14.6 %copy-start.15 = (bf16[512,512]{0,1:T(8,128)(2,1)S(1)}, bf16[512,512]{0,1:T(8,128)(2,1)}, u32[]{:S(2)}) copy-start(bf16[512,512]{0,1:T(8,128)(2,1)} %copy-done.14) | copy-start | bytes 1572868
  174.3 12.3 %collective-permute-start.10 = (bf16[4,144,128]{2,1,0:T(8,128)(2,1)S(1)}, bf16[4,144,128]{2,1,0:T(8,128)(2,1)S(1)}, u32[]{:S(2)}, u32[]{:S(2)}) collective-permute-start(bf16[4,144,128]{2,1,0:T(8,128)(2,1)S(1)} %pad_maximum_fusion.16), channel_id=1, source_target_pairs={{32,0},{40,8},{48,16},{56,24},{64,32},{72,40},{80,48},{88,56},{96,... | collective-permute-start | bytes 442376 | tf_op jit(solution)/shard_map/ppermute | solution.py:12
  187.2 11.1 %collective-permute-start.11 = (bf16[4,144,128]{2,1,0:T(8,128)(2,1)S(1)}, bf16[4,144,128]{2,1,0:T(8,128)(2,1)S(1)}, u32[]{:S(2)}, u32[]{:S(2)}) collective-permute-start(bf16[4,144,128]{2,1,0:T(8,128)(2,1)S(1)} %pad_maximum_fusion.17), channel_id=1, source_target_pairs={{64,0},{72,8},{80,16},{88,24},{96,32},{104,40},{112,48},{120,56},{... | collective-permute-start | bytes 442376 | tf_op jit(solution)/shard_map/ppermute | solution.py:12
  188.9 11.2 %copy-start.11 = (bf16[512,512]{0,1:T(8,128)(2,1)S(1)}, bf16[512,512]{0,1:T(8,128)(2,1)}, u32[]{:S(2)}) copy-start(bf16[512,512]{0,1:T(8,128)(2,1)} %copy-done.10) | copy-start | bytes 1572868
  198.8 4.1 copy-start.46
  198.8 11.4 %copy-start.36 = (f32[4,512]{1,0:T(4,128)S(1)}, f32[4,512]{1,0:T(4,128)}, u32[]{:S(2)}) copy-start(f32[4,512]{1,0:T(4,128)} %copy-done.35) | copy-start | bytes 24580
  198.8 11.3 %collective-permute-start.12 = (bf16[4,144,128]{2,1,0:T(8,128)(2,1)S(1)}, bf16[4,144,128]{2,1,0:T(8,128)(2,1)S(1)}, u32[]{:S(2)}, u32[]{:S(2)}) collective-permute-start(bf16[4,144,128]{2,1,0:T(8,128)(2,1)S(1)} %pad_maximum_fusion.18), channel_id=1, source_target_pairs={{128,0},{136,8},{144,16},{152,24},{160,32},{168,40},{176,48},{184,... | collective-permute-start | bytes 442376 | tf_op jit(solution)/shard_map/ppermute | solution.py:12
  213.8 4.3 copy-start.52
  213.8 4.3 copy-start.54
  214.1 6.0 %copy-start.48 = (s32[1,512]{1,0:T(1,128)S(1)}, s32[1,512]{1,0:T(1,128)}, u32[]{:S(2)}) copy-start(s32[1,512]{1,0:T(1,128)} %copy-done.47) | copy-start | bytes 6148
  214.1 6.0 %copy-start.50 = (s32[1,512]{1,0:T(1,128)S(1)}, s32[1,512]{1,0:T(1,128)}, u32[]{:S(2)}) copy-start(s32[1,512]{1,0:T(1,128)} %copy-done.49) | copy-start | bytes 6148
  216.5 3.7 copy-start.16
  216.5 6.2 %collective-permute-start.13 = (f32[3,3,512]{2,1,0:T(4,128)S(1)}, f32[3,3,512]{2,1,0:T(4,128)S(1)}, u32[]{:S(2)}, u32[]{:S(2)}) collective-permute-start(f32[3,3,512]{2,1,0:T(4,128)S(1)} %copy.98), channel_id=1, source_target_pairs={{8,0},{16,8},{24,16},{32,24},{40,32},{48,40},{56,48},{64,56},{72,6... | collective-permute-start | bytes 55304 | tf_op jit(solution)/shard_map/ppermute | solution.py:12
  223.8 2.4 copy-start.26
  223.8 2.4 copy-start.28
  246.0 208.4 %all-to-all-start = ((bf16[32,512,128]{2,1,0:T(8,128)(2,1)}), bf16[32,512,128]{2,1,0:T(8,128)(2,1)}, u32[]{:S(2)}, u32[]{:S(2)}) async-start(bf16[32,512,128]{2,1,0:T(8,128)(2,1)} %bitcast.213), calls=%async_computation.1 | async-start | bytes 8388608 | tf_op jit(solution)/shard_map/all_to_all | solution.py:212
  259.7 187.9 %all-reduce.2.cloned.1.call-start = ((), (), s32[]{:S(2)}) async-start(), calls=%async_computation.5 | async-start | bytes 4227072 | tf_op jit(solution)/shard_map/psum | solution.py:210
  (11 other events, 18.3 us)
Sparse Core Ops, SparseCore 0:
  9.8 36.5 all-gather.2
  48.9 89.3 all-gather.4
  153.2 37.6 reduce-scatter.1
  263.7 183.8 all-reduce.1

commit v6 on v5

--- a/solution.py
+++ b/solution.py
@@ -31,8 +31,11 @@
 def entering(log_total, state, axis, reverse):
     length = lax.axis_size(axis)
     step = -1 if reverse else 1
-    log_total, state = exchanged(log_total, state, axis, step)
-    distance = 1
+    near_total, near_state = exchanged(log_total, state, axis, step)
+    far_total, far_state = exchanged(log_total, state, axis, 2 * step)
+    state = jnp.exp(near_total)[:, None, None] * far_state + near_state
+    log_total = far_total + near_total
+    distance = 2
     while distance < length:
         far_total, far_state = exchanged(log_total, state, axis, step * distance)
         state = jnp.exp(log_total)[:, None, None] * far_state + state

time: 472 us -> 473 us (level)
  starting transfers between devices: 80.2 us -> 74.8 us
    all_gather x1, waiting for transfers between devices: 27.9 us -> 36.7 us  [on_device(): lax.all_gather(out_weight, 'seq', axis=1, tiled=True)]
    ppermute x14, starting transfers between devices: 66.3 us -> 59.2 us  [shifted(): return lax.ppermute(x, axis, pairs)]
    ppermute x14, waiting for transfers between devices: 48 us -> 41.3 us  [shifted(): return lax.ppermute(x, axis, pairs)]
where the time goes in v6:
time: 473 us; the launch traced here: 465 us
  waiting for transfers between devices  264 us (56%)
  starting transfers between devices  74.8 us (16%)
  matrix products  45.5 us (10%)
  local copies, waits for them, and re-layouts  36.2 us (8%)
  other arithmetic  29.8 us (6%)
  between operations  15.3 us (3%)
    psum x1, waiting for transfers between devices, on_device(): summed = lax.psum(packed, 'seq')  185 us
    ppermute x14, starting transfers between devices, shifted(): return lax.ppermute(x, axis, pairs)  59.2 us
    ppermute x14, waiting for transfers between devices, shifted(): return lax.ppermute(x, axis, pairs)  41.3 us
    all_gather x1, waiting for transfers between devices, on_device(): lax.all_gather(out_weight, 'seq', axis=1, tiled=True)  36.7 us
    all_to_all x1, starting transfers between devices, on_device(): weight_parts = lax.all_to_all(weight_parts, 'seq', 0, 0, tiled=True)  15.4 us
    concatenate x1, local copies, waits for them, and re-layouts, on_device(): jnp.concatenate([table_terms.astype(jnp.bfloat16).reshape(table_rows, fea...  11.3 us
  transfers between devices with their start and end apart: 19, of which 14 were waited for; matrix products, arithmetic and copies ran while one was open for 20% of the time, Pallas kernels for 0%

profile of v6, /device:TPU:2, one launch (start us, length us, event | category | flops | bytes accessed | tf_op | source)
XLA Modules:
  0.0 465.3 jit_solution(5674850067397232279)
XLA Ops:
  8.0 1.3 copy.79
  9.2 1.3 copy.80
  10.5 1.3 copy.81
  11.9 3.5 collective-permute-start
  15.5 1.2 reduce-window.6
  17.6 2.3 fusion.58
  19.9 3.9 collective-permute-done
  24.7 3.7 multiply_add_fusion
  28.6 1.1 fusion.64
  30.0 1.3 convolution_convert_fusion.6
  31.5 4.4 collective-permute-start.1
  35.9 4.8 %collective-permute-start.2 = (bf16[4,144,128]{2,1,0:T(8,128)(2,1)S(1)}, bf16[4,144,128]{2,1,0:T(8,128)(2,1)S(1)}, u32[]{:S(2)}, u32[]{:S(2)}) collective-permute-start(bf16[4,144,128]{2,1,0:T(8,128)(2,1)S(1)} %pad_maximum_fusion.6), channel_id=1, source_target_pairs={{0,16},{8,24},{16,32},{24,40},{32,48},{40,56},{48,64},{56,72},{64,... | collective-permute-start | bytes 442376 | tf_op jit(solution)/shard_map/ppermute | solution.py:12
  40.8 2.6 collective-permute-done.2
  43.9 5.9 %collective-permute-start.3 = (bf16[4,144,128]{2,1,0:T(8,128)(2,1)S(1)}, bf16[4,144,128]{2,1,0:T(8,128)(2,1)S(1)}, u32[]{:S(2)}, u32[]{:S(2)}) collective-permute-start(bf16[4,144,128]{2,1,0:T(8,128)(2,1)S(1)} %pad_maximum_fusion.9), channel_id=1, source_target_pairs={{0,16},{8,24},{16,32},{24,40},{32,48},{40,56},{48,64},{56,72},{64,... | collective-permute-start | bytes 442376 | tf_op jit(solution)/shard_map/ppermute | solution.py:12
  49.8 2.6 collective-permute-done.3
  53.0 8.2 %collective-permute-start.4 = (bf16[4,144,128]{2,1,0:T(8,128)(2,1)S(1)}, bf16[4,144,128]{2,1,0:T(8,128)(2,1)S(1)}, u32[]{:S(2)}, u32[]{:S(2)}) collective-permute-start(bf16[4,144,128]{2,1,0:T(8,128)(2,1)S(1)} %pad_maximum_fusion.10), channel_id=1, source_target_pairs={{0,32},{8,40},{16,48},{24,56},{32,64},{40,72},{48,80},{56,88},{64,... | collective-permute-start | bytes 442376 | tf_op jit(solution)/shard_map/ppermute | solution.py:12
  61.2 3.3 collective-permute-done.4
  65.2 5.7 %collective-permute-start.5 = (bf16[4,144,128]{2,1,0:T(8,128)(2,1)S(1)}, bf16[4,144,128]{2,1,0:T(8,128)(2,1)S(1)}, u32[]{:S(2)}, u32[]{:S(2)}) collective-permute-start(bf16[4,144,128]{2,1,0:T(8,128)(2,1)S(1)} %pad_maximum_fusion.11), channel_id=1, source_target_pairs={{0,64},{8,72},{16,80},{24,88},{32,96},{40,104},{48,112},{56,120},{... | collective-permute-start | bytes 442376 | tf_op jit(solution)/shard_map/ppermute | solution.py:12
  71.0 2.7 collective-permute-done.5
  74.1 16.7 %collective-permute-start.6 = (bf16[4,144,128]{2,1,0:T(8,128)(2,1)S(1)}, bf16[4,144,128]{2,1,0:T(8,128)(2,1)S(1)}, u32[]{:S(2)}, u32[]{:S(2)}) collective-permute-start(bf16[4,144,128]{2,1,0:T(8,128)(2,1)S(1)} %pad_maximum_fusion.12), channel_id=1, source_target_pairs={{0,128},{8,136},{16,144},{24,152},{32,160},{40,168},{48,176},{56,1... | collective-permute-start | bytes 442376 | tf_op jit(solution)/shard_map/ppermute | solution.py:12
  91.7 1.2 collective-permute-done.6
  93.7 3.6 multiply_reduce_fusion.4
  98.0 1.0 fusion.75
  99.0 36.7 %all-gather.5.cloned.1.call-done = bf16[512,4096]{1,0:T(8,128)(2,1)} async-done(((bf16[512,128]{1,0:T(8,128)(2,1)}), bf16[512,4096]{1,0:T(8,128)(2,1)}) %all-gather.5.cloned.1.call-update) | async-done | bytes 4194320 | tf_op jit(solution)/shard_map/all_gather | solution.py:136
  135.7 6.0 %convolution_convert_fusion.4 = bf16[512,512]{0,1:T(8,128)(2,1)S(1)} fusion(bf16[512,4096]{1,0:T(8,128)(2,1)} %all-gather.3.cloned.1.call-done, bf16[512,4096]{1,0:T(8,128)(2,1)} %all-gather.5.cloned.1.call-done), kind=kOutput, calls=%fused_computation.70 | convolution fusion | flops 2147745792 | bytes 8912896 | tf_op jit(solution)/shard_map/dot_general | solution.py:134
  141.7 1.8 fusion.71
  144.1 4.4 convolution_convert_fusion
  148.5 2.2 convolution_convert_fusion.5
  151.4 1.3 collective-permute-start.7
  152.7 1.5 collective-permute-start.8
  154.2 4.7 %fusion.14 = bf16[64,32,8,128]{3,2,1,0:T(8,128)(2,1)S(1)} fusion(bf16[512,512]{0,1:T(8,128)(2,1)} %bitcast.237, bf16[512,4096]{1,0:T(8,128)(2,1)} %all-gather.3.cloned.1.call-done), kind=kOutput, calls=%fused_computation.25 | convolution fusion | flops 2149580800 | bytes 8912896 | tf_op jit(solution)/shard_map/dot_general | solution.py:142
  159.0 3.1 copy.138
  163.3 1.3 collective-permute-start.9
  164.7 3.9 fusion.41
  168.5 4.8 %collective-permute-done.9 = bf16[4,144,128]{2,1,0:T(8,128)(2,1)S(1)} collective-permute-done((bf16[4,144,128]{2,1,0:T(8,128)(2,1)S(1)}, bf16[4,144,128]{2,1,0:T(8,128)(2,1)S(1)}, u32[]{:S(2)}, u32[]{:S(2)}) %collective-permute-start.9) | collective-permute-done | bytes 147488 | tf_op jit(solution)/shard_map/ppermute | solution.py:12
  173.9 1.4 collective-permute-start.10
  175.3 2.0 fusion.129
  177.3 7.0 %collective-permute-done.10 = bf16[4,144,128]{2,1,0:T(8,128)(2,1)S(1)} collective-permute-done((bf16[4,144,128]{2,1,0:T(8,128)(2,1)S(1)}, bf16[4,144,128]{2,1,0:T(8,128)(2,1)S(1)}, u32[]{:S(2)}, u32[]{:S(2)}) %collective-permute-start.10) | collective-permute-done | bytes 147488 | tf_op jit(solution)/shard_map/ppermute | solution.py:12
  184.9 1.5 collective-permute-start.11
  186.5 3.5 fusion.35
  189.9 3.6 collective-permute-done.11
  194.1 1.3 collective-permute-start.12
  195.4 2.7 fusion.38
  198.7 6.3 %collective-permute-done.12 = bf16[4,144,128]{2,1,0:T(8,128)(2,1)S(1)} collective-permute-done((bf16[4,144,128]{2,1,0:T(8,128)(2,1)S(1)}, bf16[4,144,128]{2,1,0:T(8,128)(2,1)S(1)}, u32[]{:S(2)}, u32[]{:S(2)}) %collective-permute-start.12) | collective-permute-done | bytes 147488 | tf_op jit(solution)/shard_map/ppermute | solution.py:12
  206.4 2.2 add_convert_fusion
  209.0 1.0 slice.316
  210.0 1.4 copy.98
  211.4 1.7 collective-permute-start.13
  213.1 2.0 fusion.51
  215.1 1.0 fusion.52
  216.1 1.5 pad_maximum_fusion.2
  217.6 2.6 collective-permute-done.13
  220.2 1.2 copy.99
  221.4 1.6 pad_maximum_fusion
  223.8 8.4 %multiply_reduce_fusion.3 = (bf16[3,512]{1,0:T(4,128)(2,1)S(1)}, bf16[3,512]{1,0:T(4,128)(2,1)S(1)}, bf16[3,512]{1,0:T(4,128)(2,1)S(1)}, bf16[3,512]{1,0:T(4,128)(2,1)S(1)}, bf16[3,512,512]{1,2,0:T(8,128)(2,1)}) fusion(f32[3,515,512]{1,2,0:T(8,128)S(1)} %copy-done.1, f32[1,512,512]{1,2,0:T(8,128)S(1)} %bitcast.216, f32[1,512,512]{1,2,0:T(8,128)S(1)} %bitcast.212, ...), kind=kLoop, calls=%fused_computation.19 | loop fusion | flops 14149632 | bytes 26775552 | tf_op jit(solution)/shard_map/reduce_sum | solution.py:188
  232.3 11.3 %concatenate.52 = bf16[2061,512]{1,0:T(8,128)(2,1)} concatenate(bf16[2048,512]{1,0:T(8,128)(2,1)} %bitcast.220, bf16[12,512]{1,0:T(8,128)(2,1)S(1)} %convert_element_type.371, bf16[1,512]{1,0:T(2,128)(2,1)S(1)} %bitcast.260), dimensions={0} | concatenate | bytes 4220928 | tf_op jit(solution)/shard_map/concatenate | solution.py:205
  243.6 15.4 %all-to-all-start = ((bf16[32,512,128]{2,1,0:T(8,128)(2,1)}), bf16[32,512,128]{2,1,0:T(8,128)(2,1)}, u32[]{:S(2)}, u32[]{:S(2)}) async-start(bf16[32,512,128]{2,1,0:T(8,128)(2,1)} %bitcast.213), calls=%async_computation.1 | async-start | bytes 8388608 | tf_op jit(solution)/shard_map/all_to_all | solution.py:215
  260.6 1.0 copy.100
  261.6 1.0 copy.101
  262.6 1.0 copy.102
  263.6 184.6 %all-reduce.2.cloned.1.call-done = bf16[2061,512]{1,0:T(8,128)(2,1)} async-done(((bf16[2061,512]{1,0:T(8,128)(2,1)}), bf16[2061,512]{1,0:T(8,128)(2,1)}) %all-reduce.2.cloned.1.call-update) | async-done | bytes 2110480 | tf_op jit(solution)/shard_map/psum | solution.py:213
  449.5 4.2 slice.324
  453.7 1.3 slice.325
  455.0 3.5 convert_reduce_fusion
  (220 shorter events, 17.6 us)
Async XLA Ops:
  7.2 8.4 %copy-start.40 = (f32[4,512]{1,0:T(4,128)S(1)}, f32[4,512]{1,0:T(4,128)}, u32[]{:S(2)}) copy-start(f32[4,512]{1,0:T(4,128)} %param.16) | copy-start | bytes 24580
  7.2 10.2 %copy-start.41 = (s32[4,512]{1,0:T(4,128)S(1)}, s32[4,512]{1,0:T(4,128)}, u32[]{:S(2)}) copy-start(s32[4,512]{1,0:T(4,128)} %param.14) | copy-start | bytes 24580
  7.2 10.2 %copy-start.36 = (f32[3,4,512]{2,1,0:T(4,128)S(1)}, f32[3,4,512]{2,1,0:T(4,128)}, u32[]{:S(2)}) copy-start(f32[3,4,512]{2,1,0:T(4,128)} %param.13) | copy-start | bytes 73732
  7.2 91.8 %all-gather.3.cloned.1.call-start = ((), (), s32[]{:S(2)}) async-start(), calls=%async_computation.2 | async-start | bytes 4718592 | tf_op jit(solution)/shard_map/all_gather | solution.py:132
  7.9 127.8 %all-gather.5.cloned.1.call-start = ((), (), s32[]{:S(2)}) async-start(), calls=%async_computation.3 | async-start | bytes 4325376 | tf_op jit(solution)/shard_map/all_gather | solution.py:136
  11.9 11.8 %collective-permute-start = (bf16[3,3,512]{1,2,0:T(8,128)(2,1)S(1)}, bf16[3,3,512]{1,2,0:T(8,128)(2,1)S(1)}, u32[]{:S(2)}, u32[]{:S(2)}) collective-permute-start(bf16[3,3,512]{1,2,0:T(8,128)(2,1)S(1)} %pad_maximum_fusion.3), channel_id=1, source_target_pairs={{0,8},{8,16},{16,24},{24,32},{32,40},{40,48},{48,56},{56,64},{64,7... | collective-permute-start | bytes 27656 | tf_op jit(solution)/shard_map/ppermute | solution.py:12
  15.5 228.1 %reduce-scatter.2.cloned.1.call-start = ((), (), s32[]{:S(2)}) async-start(), calls=%async_computation.4 | async-start | bytes 4718592 | tf_op jit(solution)/shard_map/reduce_scatter | solution.py:129
  17.2 76.5 %copy-start.37 = (f32[1,4,4,128]{3,1,2,0:T(4,128)}, f32[1,4,4,128]{3,1,2,0:T(4,128)S(1)}, u32[]{:S(2)}) copy-start(f32[1,4,4,128]{3,1,2,0:T(4,128)S(1)} %copy.139) | copy-start | bytes 24580
  17.4 7.2 %copy-start.50 = (s32[1,512]{1,0:T(1,128)}, s32[1,512]{1,0:T(1,128)S(1)}, u32[]{:S(2)}) copy-start(s32[1,512]{1,0:T(1,128)S(1)} %get-tuple-element.117) | copy-start | bytes 6148
  17.4 7.2 %copy-start.52 = (s32[1,512]{1,0:T(1,128)}, s32[1,512]{1,0:T(1,128)S(1)}, u32[]{:S(2)}) copy-start(s32[1,512]{1,0:T(1,128)S(1)} %get-tuple-element.118) | copy-start | bytes 6148
  17.4 11.1 %copy-start.46 = (s32[1,512]{1,0:T(1,128)}, s32[1,512]{1,0:T(1,128)S(1)}, u32[]{:S(2)}) copy-start(s32[1,512]{1,0:T(1,128)S(1)} %get-tuple-element.116) | copy-start | bytes 6148
  17.4 11.1 %copy-start.48 = (s32[1,512]{1,0:T(1,128)}, s32[1,512]{1,0:T(1,128)S(1)}, u32[]{:S(2)}) copy-start(s32[1,512]{1,0:T(1,128)S(1)} %get-tuple-element.119) | copy-start | bytes 6148
  17.5 7.2 %copy-start.19 = (f32[3,512]{1,0:T(4,128)}, f32[3,512]{1,0:T(4,128)S(1)}, u32[]{:S(2)}) copy-start(f32[3,512]{1,0:T(4,128)S(1)} %get-tuple-element.123) | copy-start | bytes 18436
  17.5 7.2 %copy-start.21 = (f32[3,512]{1,0:T(4,128)}, f32[3,512]{1,0:T(4,128)S(1)}, u32[]{:S(2)}) copy-start(f32[3,512]{1,0:T(4,128)S(1)} %get-tuple-element.124) | copy-start | bytes 18436
  17.5 7.2 %copy-start.23 = (f32[3,512]{1,0:T(4,128)}, f32[3,512]{1,0:T(4,128)S(1)}, u32[]{:S(2)}) copy-start(f32[3,512]{1,0:T(4,128)S(1)} %get-tuple-element.125) | copy-start | bytes 18436
  17.5 7.2 %copy-start.25 = (f32[3,512]{1,0:T(4,128)}, f32[3,512]{1,0:T(4,128)S(1)}, u32[]{:S(2)}) copy-start(f32[3,512]{1,0:T(4,128)S(1)} %get-tuple-element.126) | copy-start | bytes 18436
  17.6 12.4 %copy-start.30 = (f32[4,512]{1,0:T(4,128)}, f32[4,512]{1,0:T(4,128)S(1)}, u32[]{:S(2)}) copy-start(f32[4,512]{1,0:T(4,128)S(1)} %get-tuple-element.115) | copy-start | bytes 24580
  17.6 76.1 %copy-start.42 = (f32[4,512]{1,0:T(4,128)}, f32[4,512]{1,0:T(4,128)S(1)}, u32[]{:S(2)}) copy-start(f32[4,512]{1,0:T(4,128)S(1)} %get-tuple-element.114) | copy-start | bytes 24580
  17.6 80.4 %copy-start.28 = (f32[512,4]{0,1:T(4,128)}, f32[512,4]{0,1:T(4,128)S(1)}, u32[]{:S(2)}) copy-start(f32[512,4]{0,1:T(4,128)S(1)} %get-tuple-element.113) | copy-start | bytes 24580
  24.6 3.8 copy-start
  24.7 3.9 copy-start.54
  29.7 34.9 %copy-start.13 = (bf16[512,512]{0,1:T(8,128)(2,1)}, bf16[512,512]{0,1:T(8,128)(2,1)S(1)}, u32[]{:S(2)}) copy-start(bf16[512,512]{0,1:T(8,128)(2,1)S(1)} %get-tuple-element.100) | copy-start | bytes 1572868
  29.7 118.8 %copy-start.10 = (bf16[512,512]{0,1:T(8,128)(2,1)}, bf16[512,512]{0,1:T(8,128)(2,1)S(1)}, u32[]{:S(2)}) copy-start(bf16[512,512]{0,1:T(8,128)(2,1)S(1)} %get-tuple-element.99) | copy-start | bytes 1572868
  31.4 42.3 %copy-start.32 = (bf16[4,8,128]{2,1,0:T(8,128)(2,1)}, bf16[4,8,128]{2,1,0:T(8,128)(2,1)S(1)}, u32[]{:S(2)}) copy-start(bf16[4,8,128]{2,1,0:T(8,128)(2,1)S(1)} %broadcast_in_dim.79) | copy-start | bytes 24580
  31.5 42.3 %copy-start.33 = (bf16[4,8,128]{2,1,0:T(8,128)(2,1)}, bf16[4,8,128]{2,1,0:T(8,128)(2,1)S(1)}, u32[]{:S(2)}) copy-start(bf16[4,8,128]{2,1,0:T(8,128)(2,1)S(1)} %broadcast_in_dim.80) | copy-start | bytes 24580
  31.5 9.2 %collective-permute-start.1 = (bf16[4,144,128]{2,1,0:T(8,128)(2,1)S(1)}, bf16[4,144,128]{2,1,0:T(8,128)(2,1)S(1)}, u32[]{:S(2)}, u32[]{:S(2)}) collective-permute-start(bf16[4,144,128]{2,1,0:T(8,128)(2,1)S(1)} %pad_maximum_fusion.6), channel_id=1, source_target_pairs={{0,8},{8,16},{16,24},{24,32},{32,40},{40,48},{48,56},{56,64},{64,7... | collective-permute-start | bytes 442376 | tf_op jit(solution)/shard_map/ppermute | solution.py:12
  35.9 7.5 %collective-permute-start.2 = (bf16[4,144,128]{2,1,0:T(8,128)(2,1)S(1)}, bf16[4,144,128]{2,1,0:T(8,128)(2,1)S(1)}, u32[]{:S(2)}, u32[]{:S(2)}) collective-permute-start(bf16[4,144,128]{2,1,0:T(8,128)(2,1)S(1)} %pad_maximum_fusion.6), channel_id=1, source_target_pairs={{0,16},{8,24},{16,32},{24,40},{32,48},{40,56},{48,64},{56,72},{64,... | collective-permute-start | bytes 442376 | tf_op jit(solution)/shard_map/ppermute | solution.py:12
  43.9 8.5 %collective-permute-start.3 = (bf16[4,144,128]{2,1,0:T(8,128)(2,1)S(1)}, bf16[4,144,128]{2,1,0:T(8,128)(2,1)S(1)}, u32[]{:S(2)}, u32[]{:S(2)}) collective-permute-start(bf16[4,144,128]{2,1,0:T(8,128)(2,1)S(1)} %pad_maximum_fusion.9), channel_id=1, source_target_pairs={{0,16},{8,24},{16,32},{24,40},{32,48},{40,56},{48,64},{56,72},{64,... | collective-permute-start | bytes 442376 | tf_op jit(solution)/shard_map/ppermute | solution.py:12
  53.0 11.6 %collective-permute-start.4 = (bf16[4,144,128]{2,1,0:T(8,128)(2,1)S(1)}, bf16[4,144,128]{2,1,0:T(8,128)(2,1)S(1)}, u32[]{:S(2)}, u32[]{:S(2)}) collective-permute-start(bf16[4,144,128]{2,1,0:T(8,128)(2,1)S(1)} %pad_maximum_fusion.10), channel_id=1, source_target_pairs={{0,32},{8,40},{16,48},{24,56},{32,64},{40,72},{48,80},{56,88},{64,... | collective-permute-start | bytes 442376 | tf_op jit(solution)/shard_map/ppermute | solution.py:12
  65.2 8.5 %collective-permute-start.5 = (bf16[4,144,128]{2,1,0:T(8,128)(2,1)S(1)}, bf16[4,144,128]{2,1,0:T(8,128)(2,1)S(1)}, u32[]{:S(2)}, u32[]{:S(2)}) collective-permute-start(bf16[4,144,128]{2,1,0:T(8,128)(2,1)S(1)} %pad_maximum_fusion.11), channel_id=1, source_target_pairs={{0,64},{8,72},{16,80},{24,88},{32,96},{40,104},{48,112},{56,120},{... | collective-permute-start | bytes 442376 | tf_op jit(solution)/shard_map/ppermute | solution.py:12
  71.0 22.7 %copy-start.16 = (pred[512,512]{1,0:T(8,128)(4,1)}, pred[512,512]{1,0:T(8,128)(4,1)S(1)}, u32[]{:S(2)}) copy-start(pred[512,512]{1,0:T(8,128)(4,1)S(1)} %iota_compare_fusion.4) | copy-start | bytes 786436
  74.1 18.8 %collective-permute-start.6 = (bf16[4,144,128]{2,1,0:T(8,128)(2,1)S(1)}, bf16[4,144,128]{2,1,0:T(8,128)(2,1)S(1)}, u32[]{:S(2)}, u32[]{:S(2)}) collective-permute-start(bf16[4,144,128]{2,1,0:T(8,128)(2,1)S(1)} %pad_maximum_fusion.12), channel_id=1, source_target_pairs={{0,128},{8,136},{16,144},{24,152},{32,160},{40,168},{48,176},{56,1... | collective-permute-start | bytes 442376 | tf_op jit(solution)/shard_map/ppermute | solution.py:12
  91.6 5.8 %copy-start.7 = (f32[4,512,512]{2,1,0:T(8,128)}, f32[4,512,512]{2,1,0:T(8,128)S(1)}, u32[]{:S(2)}) copy-start(f32[4,512,512]{2,1,0:T(8,128)S(1)} %fusion.94) | copy-start | bytes 12582916
  91.7 5.6 %copy-start.43 = (f32[4]{0:T(128)}, f32[4]{0:T(128)S(1)}, u32[]{:S(2)}) copy-start(f32[4]{0:T(128)S(1)} %exponential_reduce_fusion.6) | copy-start | bytes 52
  93.7 4.3 copy-start.34
  97.3 78.0 %copy-start.2 = (f32[4,512,128]{1,2,0:T(8,128)}, f32[4,512,128]{1,2,0:T(8,128)S(1)}, u32[]{:S(2)}) copy-start(f32[4,512,128]{1,2,0:T(8,128)S(1)} %get-tuple-element.85) | copy-start | bytes 3145732
  135.7 8.4 %copy-start.9 = (bf16[512,4096]{1,0:T(8,128)(2,1)S(1)}, bf16[512,4096]{1,0:T(8,128)(2,1)}, u32[]{:S(2)}) copy-start(bf16[512,4096]{1,0:T(8,128)(2,1)} %all-gather.5.cloned.1.call-done) | copy-start | bytes 12582916
  135.7 8.4 %copy-start.12 = (bf16[512,4,128]{0,2,1:T(8,128)(2,1)S(1)}, bf16[512,4,128]{0,2,1:T(8,128)(2,1)}, u32[]{:S(2)}) copy-start(bf16[512,4,128]{0,2,1:T(8,128)(2,1)} %fusion.75) | copy-start | bytes 1572868
  141.7 33.7 %copy-start.5 = (bf16[512,512]{0,1:T(8,128)(2,1)}, bf16[512,512]{0,1:T(8,128)(2,1)S(1)}, u32[]{:S(2)}) copy-start(bf16[512,512]{0,1:T(8,128)(2,1)S(1)} %convolution_convert_fusion.4) | copy-start | bytes 1572868
  151.4 10.7 %collective-permute-start.7 = (bf16[4,144,128]{2,1,0:T(8,128)(2,1)S(1)}, bf16[4,144,128]{2,1,0:T(8,128)(2,1)S(1)}, u32[]{:S(2)}, u32[]{:S(2)}) collective-permute-start(bf16[4,144,128]{2,1,0:T(8,128)(2,1)S(1)} %pad_maximum_fusion.5), channel_id=1, source_target_pairs={{8,0},{16,8},{24,16},{32,24},{40,32},{48,40},{56,48},{64,56},{72,6... | collective-permute-start | bytes 442376 | tf_op jit(solution)/shard_map/ppermute | solution.py:12
  152.7 10.0 %collective-permute-start.8 = (bf16[4,144,128]{2,1,0:T(8,128)(2,1)S(1)}, bf16[4,144,128]{2,1,0:T(8,128)(2,1)S(1)}, u32[]{:S(2)}, u32[]{:S(2)}) collective-permute-start(bf16[4,144,128]{2,1,0:T(8,128)(2,1)S(1)} %pad_maximum_fusion.5), channel_id=1, source_target_pairs={{16,0},{24,8},{32,16},{40,24},{48,32},{56,40},{64,48},{72,56},{80,... | collective-permute-start | bytes 442376 | tf_op jit(solution)/shard_map/ppermute | solution.py:12
  158.9 5.7 %copy-start.8 = (f32[4,512,512]{2,1,0:T(8,128)S(1)}, f32[4,512,512]{2,1,0:T(8,128)}, u32[]{:S(2)}) copy-start(f32[4,512,512]{2,1,0:T(8,128)} %copy-done.7) | copy-start | bytes 12582916
  158.9 5.7 %copy-start.17 = (pred[512,512]{1,0:T(8,128)(4,1)S(1)}, pred[512,512]{1,0:T(8,128)(4,1)}, u32[]{:S(2)}) copy-start(pred[512,512]{1,0:T(8,128)(4,1)} %copy-done.16) | copy-start | bytes 786436
  158.9 5.7 %copy-start.18 = (f32[4,512]{1,0:T(4,128)S(1)}, f32[4,512]{1,0:T(4,128)}, u32[]{:S(2)}) copy-start(f32[4,512]{1,0:T(4,128)} %get-tuple-element.112) | copy-start | bytes 24580
  158.9 5.7 %copy-start.27 = (f32[4,512]{1,0:T(4,128)S(1)}, f32[4,512]{1,0:T(4,128)}, u32[]{:S(2)}) copy-start(f32[4,512]{1,0:T(4,128)} %broadcast_multiply_fusion) | copy-start | bytes 24580
  159.0 5.7 %copy-start.35 = (f32[512]{0:T(512)S(1)}, f32[512]{0:T(512)}, u32[]{:S(2)}) copy-start(f32[512]{0:T(512)} %param.17) | copy-start | bytes 6148
  159.0 5.7 %copy-start.38 = (f32[1,4,4,128]{3,1,2,0:T(4,128)S(1)}, f32[1,4,4,128]{3,1,2,0:T(4,128)}, u32[]{:S(2)}) copy-start(f32[1,4,4,128]{3,1,2,0:T(4,128)} %copy-done.37) | copy-start | bytes 24580
  163.3 10.0 %collective-permute-start.9 = (bf16[4,144,128]{2,1,0:T(8,128)(2,1)S(1)}, bf16[4,144,128]{2,1,0:T(8,128)(2,1)S(1)}, u32[]{:S(2)}, u32[]{:S(2)}) collective-permute-start(bf16[4,144,128]{2,1,0:T(8,128)(2,1)S(1)} %pad_maximum_fusion.13), channel_id=1, source_target_pairs={{16,0},{24,8},{32,16},{40,24},{48,32},{56,40},{64,48},{72,56},{80,... | collective-permute-start | bytes 442376 | tf_op jit(solution)/shard_map/ppermute | solution.py:12
  173.9 12.6 %copy-start.14 = (bf16[512,512]{0,1:T(8,128)(2,1)S(1)}, bf16[512,512]{0,1:T(8,128)(2,1)}, u32[]{:S(2)}) copy-start(bf16[512,512]{0,1:T(8,128)(2,1)} %copy-done.13) | copy-start | bytes 1572868
  173.9 10.5 %collective-permute-start.10 = (bf16[4,144,128]{2,1,0:T(8,128)(2,1)S(1)}, bf16[4,144,128]{2,1,0:T(8,128)(2,1)S(1)}, u32[]{:S(2)}, u32[]{:S(2)}) collective-permute-start(bf16[4,144,128]{2,1,0:T(8,128)(2,1)S(1)} %pad_maximum_fusion.14), channel_id=1, source_target_pairs={{32,0},{40,8},{48,16},{56,24},{64,32},{72,40},{80,48},{88,56},{96,... | collective-permute-start | bytes 442376 | tf_op jit(solution)/shard_map/ppermute | solution.py:12
  184.9 8.6 %collective-permute-start.11 = (bf16[4,144,128]{2,1,0:T(8,128)(2,1)S(1)}, bf16[4,144,128]{2,1,0:T(8,128)(2,1)S(1)}, u32[]{:S(2)}, u32[]{:S(2)}) collective-permute-start(bf16[4,144,128]{2,1,0:T(8,128)(2,1)S(1)} %pad_maximum_fusion.15), channel_id=1, source_target_pairs={{64,0},{72,8},{80,16},{88,24},{96,32},{104,40},{112,48},{120,56},{... | collective-permute-start | bytes 442376 | tf_op jit(solution)/shard_map/ppermute | solution.py:12
  186.5 8.9 %copy-start.11 = (bf16[512,512]{0,1:T(8,128)(2,1)S(1)}, bf16[512,512]{0,1:T(8,128)(2,1)}, u32[]{:S(2)}) copy-start(bf16[512,512]{0,1:T(8,128)(2,1)} %copy-done.10) | copy-start | bytes 1572868
  194.0 4.1 copy-start.45
  194.1 11.1 %copy-start.31 = (f32[4,512]{1,0:T(4,128)S(1)}, f32[4,512]{1,0:T(4,128)}, u32[]{:S(2)}) copy-start(f32[4,512]{1,0:T(4,128)} %copy-done.30) | copy-start | bytes 24580
  194.1 10.9 %collective-permute-start.12 = (bf16[4,144,128]{2,1,0:T(8,128)(2,1)S(1)}, bf16[4,144,128]{2,1,0:T(8,128)(2,1)S(1)}, u32[]{:S(2)}, u32[]{:S(2)}) collective-permute-start(bf16[4,144,128]{2,1,0:T(8,128)(2,1)S(1)} %pad_maximum_fusion.16), channel_id=1, source_target_pairs={{128,0},{136,8},{144,16},{152,24},{160,32},{168,40},{176,48},{184,... | collective-permute-start | bytes 442376 | tf_op jit(solution)/shard_map/ppermute | solution.py:12
  208.7 4.4 copy-start.51
  208.7 4.4 copy-start.53
  209.0 6.1 %copy-start.47 = (s32[1,512]{1,0:T(1,128)S(1)}, s32[1,512]{1,0:T(1,128)}, u32[]{:S(2)}) copy-start(s32[1,512]{1,0:T(1,128)} %copy-done.46) | copy-start | bytes 6148
  209.0 6.1 %copy-start.49 = (s32[1,512]{1,0:T(1,128)S(1)}, s32[1,512]{1,0:T(1,128)}, u32[]{:S(2)}) copy-start(s32[1,512]{1,0:T(1,128)} %copy-done.48) | copy-start | bytes 6148
  211.4 3.7 copy-start.15
  211.4 8.8 %collective-permute-start.13 = (f32[3,3,512]{2,1,0:T(4,128)S(1)}, f32[3,3,512]{2,1,0:T(4,128)S(1)}, u32[]{:S(2)}, u32[]{:S(2)}) collective-permute-start(f32[3,3,512]{2,1,0:T(4,128)S(1)} %copy.98), channel_id=1, source_target_pairs={{8,0},{16,8},{24,16},{32,24},{40,32},{48,40},{56,48},{64,56},{72,6... | collective-permute-start | bytes 55304 | tf_op jit(solution)/shard_map/ppermute | solution.py:12
  223.8 8.5 %copy-start.39 = (bf16[1,1,4,128]{3,1,2,0:T(2,128)(2,1)S(1)}, bf16[1,1,4,128]{3,1,2,0:T(2,128)(2,1)}, u32[]{:S(2)}) copy-start(bf16[1,1,4,128]{3,1,2,0:T(2,128)(2,1)} %copy.140) | copy-start | bytes 3076
  243.6 211.4 %all-to-all-start = ((bf16[32,512,128]{2,1,0:T(8,128)(2,1)}), bf16[32,512,128]{2,1,0:T(8,128)(2,1)}, u32[]{:S(2)}, u32[]{:S(2)}) async-start(bf16[32,512,128]{2,1,0:T(8,128)(2,1)} %bitcast.213), calls=%async_computation.1 | async-start | bytes 8388608 | tf_op jit(solution)/shard_map/all_to_all | solution.py:215
  259.1 189.1 %all-reduce.2.cloned.1.call-start = ((), (), s32[]{:S(2)}) async-start(), calls=%async_computation.5 | async-start | bytes 4227072 | tf_op jit(solution)/shard_map/psum | solution.py:213
  (10 other events, 18.7 us)
Sparse Core Ops, SparseCore 0:
  9.8 36.5 all-gather.2
  48.9 86.7 all-gather.4
  148.6 37.6 reduce-scatter.1
  263.1 185.0 all-reduce.1
